TPU v7x, 32 devices: a whole 2x2x4 slice. The times are simulated.
32 devices in a mesh: dp: 8 (over z, x), mp: 4 (over y, core).
Axes of the slice: x: 2, y: 2, z: 4, core: 2. Of those that a mesh axis runs over, the one named last changes fastest.
Arguments:
- tokens: bfloat16 [24, 512, 768], P('dp'), may hold values from -6 to 6
- lengths: int32 [24], P('dp'), may hold values from 216 to 512, as said below
- gain_attn: bfloat16 [768], replicated, may hold values from 0.5 to 1.5
- bias_attn: bfloat16 [768], replicated, may hold values from -4 to 4
- query_w: bfloat16 [768, 768], P(None, 'mp'), may hold values from -0.21875 to 0.21875
- query_b: bfloat16 [768], P('mp'), may hold values from -4 to 4
- key_w: bfloat16 [768, 768], P(None, 'mp'), may hold values from -0.21875 to 0.21875
- value_w: bfloat16 [768, 768], P(None, 'mp'), may hold values from -0.21875 to 0.21875
- value_b: bfloat16 [768], P('mp'), may hold values from -0.75 to 0.75
- out_w: bfloat16 [768, 768], P('mp'), may hold values from -1.75 to 1.75
- out_b: bfloat16 [768], replicated, may hold values from -4 to 4
- gain_mlp: bfloat16 [768], replicated, may hold values from 0.5 to 1.5
- bias_mlp: bfloat16 [768], replicated, may hold values from -4 to 4
- up_w: bfloat16 [768, 3072], P(None, 'mp'), may hold values from -0.21875 to 0.21875
- up_b: bfloat16 [3072], P('mp'), may hold values from -4 to 4
- down_w: bfloat16 [3072, 768], P('mp'), may hold values from -0.15625 to 0.15625
- down_b: bfloat16 [768], replicated, may hold values from -4 to 4
- deconv_w: bfloat16 [768, 1024], P(None, 'mp'), may hold values from -0.21875 to 0.21875
- scale_norm: bfloat16 [128], replicated, may hold values from 0.5 to 1.5
- shift_norm: bfloat16 [128], replicated, may hold values from -6 to 6
- cotangent: bfloat16 [24, 512, 1024], P('dp', None, 'mp'), may hold values from -6 to 6
Outputs:
- volume: float32 [24, 512, 1024], P('dp', None, 'mp')
- grad_tokens: float32 [12288, 768], P(('dp', 'mp'))
- grad_gain_attn: float32 [768], replicated
- grad_bias_attn: float32 [768], replicated
- grad_query_w: float32 [768, 768], P(None, 'mp')
- grad_query_b: float32 [768], P('mp')
- grad_key_w: float32 [768, 768], P(None, 'mp')
- grad_value_w: float32 [768, 768], P(None, 'mp')
- grad_value_b: float32 [768], P('mp')
- grad_out_w: float32 [768, 768], P('mp')
- grad_out_b: float32 [768], replicated
- grad_gain_mlp: float32 [768], replicated
- grad_bias_mlp: float32 [768], replicated
- grad_up_w: float32 [768, 3072], P(None, 'mp')
- grad_up_b: float32 [3072], P('mp')
- grad_down_w: float32 [3072, 768], P('mp')
- grad_down_b: float32 [768], replicated
- grad_deconv_w: float32 [768, 1024], P(None, 'mp')
- grad_scale_norm: float32 [128], replicated
- grad_shift_norm: float32 [128], replicated
Inputs may be any that keep to these rules, and one draw needn't show every extreme that they name: `lengths`: each item holds 216, 256 or 512 patches, drawn independently for each item except that the first item of the whole batch holds 512.
All inputs are finite; a program needn't handle non-finite values.
Results may differ from a plain program's by a relative error of at most 0.025.
Values may be sent and summed in bfloat16 or wider, within the bound.
No kernel may reach another device: no remote copies, remote signals or barrier semaphores. Data moves between devices by JAX's collectives and lax.ppermute only.
A program may use at most 128 MiB of HBM per device.

v0:
```python
import functools

import jax
import jax.numpy as jnp
from jax import lax
from jax.experimental import pallas as pl
from jax.experimental.pallas import tpu as pltpu
from jax.sharding import PartitionSpec as P

HEAD_DIM = 64
CH = 128
EPSILON = 1e-05
SCALE = HEAD_DIM ** (-0.5)
F32 = jnp.float32
BF16 = jnp.bfloat16
TILE = 256
PIECE = 128
PAD = 16
VECTORS = 6
OUT_B, GAIN_MLP, BIAS_MLP, DOWN_B, GAIN_ATTN, BIAS_ATTN, UP_B, MIXED = range(8)
COST = 1
MIB = 1024 * 1024


def dot(left, right):
    return jnp.dot(left, right, preferred_element_type=F32)


def dot_rows(left, right):
    return lax.dot_general(left, right, (((0,), (0,)), ((), ())), preferred_element_type=F32)


def dot_cols(left, right):
    return lax.dot_general(left, right, (((1,), (1,)), ((), ())), preferred_element_type=F32)


def swap(value, axis, bit):
    size = lax.axis_size(axis)
    return lax.ppermute(value, axis, [(i, i ^ bit) for i in range(size)])


def norm_stats(values):
    center = values - jnp.mean(values, axis=-1, keepdims=True)
    inverse = lax.rsqrt(jnp.mean(center * center, axis=-1, keepdims=True) + EPSILON)
    return center * inverse, inverse


def norm_backward(upstream, normal, inverse, gain_vec):
    scaled = upstream * gain_vec
    mean_part = jnp.mean(scaled, axis=-1, keepdims=True)
    mean_cross = jnp.mean(scaled * normal, axis=-1, keepdims=True)
    return inverse * (scaled - mean_part - normal * mean_cross)


def vmem():
    return pl.BlockSpec(memory_space=pltpu.VMEM)


def anywhere():
    return pl.BlockSpec(memory_space=pl.ANY)


def row(index):
    return slice(index, index + 1)


def smem():
    return pl.BlockSpec(memory_space=pltpu.SMEM)


def shape(dims, dtype):
    return jax.ShapeDtypeStruct(dims, dtype)


def join(*values):
    return lax.optimization_barrier(values)


def in_hbm(*values):
    return [pltpu.with_memory_space_constraint(value, pltpu.HBM) for value in values]


def params(name, flops, moved, mebibytes=24):
    return dict(
        compiler_params=pltpu.CompilerParams(vmem_limit_bytes=mebibytes * MIB),
        cost_estimate=pl.CostEstimate(flops=flops // COST, transcendentals=0, bytes_accessed=moved // COST),
        name=name,
    )


def over_pieces(count, step):
    def body(index, carry):
        step(index, pl.ds(pl.multiple_of(index * PIECE, PIECE), PIECE))
        return carry

    lax.fori_loop(0, count // PIECE, body, 0)


def head_cols(head):
    return slice(head * HEAD_DIM, (head + 1) * HEAD_DIM)


def tiles(width):
    return [slice(start, start + TILE) for start in range(0, width, TILE)]


def chip_half():
    return lax.axis_index("mp") // 2


def x_side():
    return lax.axis_index("dp") % 2


def attend_kernel(
    items, heads, span_rows, info_ref, tok_ref, vec_ref, qw_ref, kw_ref, vw_ref,
    normed_ref, q_ref, k_ref, v_ref, lse_ref, near_ref, other_ref, o_ref
):
    seq = tok_ref.shape[0]
    item = pl.program_id(0)
    length = info_ref[item]
    for start in range(0, seq, PIECE):
        rows = slice(start, start + PIECE)
        normal, unused = norm_stats(tok_ref[rows, :].astype(F32))
        normed_ref[rows, :] = (normal * vec_ref[row(GAIN_ATTN), :] + vec_ref[row(BIAS_ATTN), :]).astype(BF16)
    normed = normed_ref[...]
    hw = q_ref.shape[1]
    q_ref[...] = (dot_cols(normed, qw_ref[...]) + vec_ref[row(MIXED), :hw]).astype(BF16) * jnp.asarray(SCALE, BF16)
    k_ref[...] = dot_cols(normed, kw_ref[...]).astype(BF16)
    v_ref[...] = (dot_cols(normed, vw_ref[...]) + vec_ref[row(MIXED), hw : 2 * hw]).astype(BF16)

    def run(span):
        valid = lax.broadcasted_iota(jnp.int32, (span, span), 0) < length
        for head in range(heads):
            cols = head_cols(head)
            scores = jnp.where(valid, dot_cols(k_ref[:span, cols], q_ref[:span, cols]), -1e9)
            top = jnp.max(scores, axis=0, keepdims=True)
            raised = jnp.exp(scores - top)
            total = jnp.sum(raised, axis=0, keepdims=True)
            mixed = dot_rows(v_ref[:span, cols], raised.astype(BF16)) / total
            o_ref[pl.ds(pl.multiple_of(item * seq, seq), span), cols] = mixed.T.astype(BF16)
            lse_ref[0, head : head + 1, :span] = top + jnp.log(total)
        if span < seq:
            o_ref[pl.ds(pl.multiple_of(item * seq + span, span), seq - span), :] = jnp.zeros(
                (seq - span, heads * HEAD_DIM), BF16
            )

    half = seq // 2

    @pl.when(length <= half)
    def _():
        run(half)

    @pl.when(length > half)
    def _():
        run(seq)

    @pl.when(item == items - 1)
    def _():
        start = chip_half() * span_rows
        near_ref[...] = o_ref[pl.ds(pl.multiple_of(start, PIECE), span_rows), :]
        other_ref[...] = o_ref[pl.ds(pl.multiple_of(span_rows - start, PIECE), span_rows), :]


def attend(info, rows2d, vecs, query_w, key_w, value_w, items, seq):
    rows, width = rows2d.shape
    hw = query_w.shape[0]
    heads = hw // HEAD_DIM
    row_block = lambda cols: pl.BlockSpec((seq, cols), lambda i, n: (i, 0))
    whole = lambda dims: pl.BlockSpec(dims, lambda i, n: (0,) * len(dims))
    return pl.pallas_call(
        functools.partial(attend_kernel, items, heads, rows // 2),
        out_shape=[pltpu.HBM((rows, width), BF16)]
        + [pltpu.HBM((rows, hw), BF16)] * 3
        + [pltpu.HBM((items, 8, seq), F32)]
        + [shape((rows // 2, hw), BF16)] * 2,
        grid_spec=pltpu.PrefetchScalarGridSpec(
            num_scalar_prefetch=1,
            grid=(items,),
            in_specs=[row_block(width), whole(vecs.shape)] + [whole((hw, width))] * 3,
            out_specs=[row_block(width)]
            + [row_block(hw)] * 3
            + [pl.BlockSpec((1, 8, seq), lambda i, n: (i, 0, 0))]
            + [whole((rows // 2, hw))] * 2,
            scratch_shapes=[pltpu.VMEM((rows, hw), BF16)],
        ),
        **params("attend", 6 * rows * width * hw + 4 * rows * seq * hw, 4 * rows * width),
    )(info, *in_hbm(rows2d, vecs, query_w, key_w, value_w))


def attend_back_kernel(
    items, heads, share, len_ref, normed_ref, q_ref, k_ref, v_ref, lse_ref, near_ref, other_ref,
    dq_ref, dk_ref, dv_ref, grad_ref, sums_ref, do_ref, grad_acc
):
    seq = normed_ref.shape[0]
    hw = heads * HEAD_DIM
    item = pl.program_id(0)
    length = len_ref[item]

    @pl.when(item == 0)
    def _():
        begin = chip_half() * 2 * share
        do_ref[pl.ds(pl.multiple_of(begin, PIECE), 2 * share), :] = near_ref[...]
        do_ref[pl.ds(pl.multiple_of(2 * share - begin, PIECE), 2 * share), :] = other_ref[...]
        sums_ref[...] = jnp.zeros_like(sums_ref)
        grad_acc[...] = jnp.zeros_like(grad_acc)

    def run(span):
        valid = lax.broadcasted_iota(jnp.int32, (span, span), 0) < length
        for head in range(heads):
            cols = head_cols(head)
            query, keys, vals = q_ref[:span, cols], k_ref[:span, cols], v_ref[:span, cols]
            upstream = do_ref[pl.ds(pl.multiple_of(item * seq, seq), span), cols]
            scores = jnp.where(valid, dot_cols(keys, query), -1e9)
            prob = jnp.exp(scores - lse_ref[0, head : head + 1, :span])
            dv_ref[:span, cols] = dot(prob.astype(BF16), upstream).astype(BF16)
            prob_grad = dot_cols(vals, upstream)
            product = prob * prob_grad
            row_term = jnp.sum(product, axis=0, keepdims=True)
            score_grad = (product - prob * row_term).astype(BF16)
            dk_ref[:span, cols] = dot(score_grad, query).astype(BF16)
            dq_ref[:span, cols] = (dot_rows(keys, score_grad) * SCALE).T.astype(BF16)
        for index, ref in enumerate((dq_ref, dk_ref, dv_ref)):
            grad_acc[index * hw : (index + 1) * hw, :] += dot_rows(ref[:span, :], normed_ref[:span, :])
            if index != 1:
                sums_ref[row(index), :hw] += jnp.sum(ref[:span, :].astype(F32), axis=0, keepdims=True)
            if span < seq:
                ref[span:, :] = jnp.zeros((seq - span, hw), BF16)

    half = seq // 2

    @pl.when(length <= half)
    def _():
        run(half)

    @pl.when(length > half)
    def _():
        run(seq)

    @pl.when(item == items - 1)
    def _():
        grad_ref[...] = grad_acc[...].astype(BF16)


def attend_back(lengths, normed, q, k, v, lse, near, other, items, seq, share):
    rows, width = normed.shape
    hw = q.shape[1]
    heads = hw // HEAD_DIM
    row_block = lambda cols: pl.BlockSpec((seq, cols), lambda i, n: (i, 0))
    whole = lambda dims: pl.BlockSpec(dims, lambda i, n: (0,) * len(dims))
    return pl.pallas_call(
        functools.partial(attend_back_kernel, items, heads, share),
        out_shape=[pltpu.HBM((rows, hw), BF16)] * 3 + [shape((3 * hw, width), BF16), shape((8, width), F32)],
        grid_spec=pltpu.PrefetchScalarGridSpec(
            num_scalar_prefetch=1,
            grid=(items,),
            in_specs=[row_block(width)]
            + [row_block(hw)] * 3
            + [pl.BlockSpec((1, 8, seq), lambda i, n: (i, 0, 0))]
            + [whole((2 * share, hw))] * 2,
            out_specs=[row_block(hw)] * 3 + [whole((3 * hw, width)), whole((8, width))],
            scratch_shapes=[pltpu.VMEM((rows, hw), BF16), pltpu.VMEM((3 * hw, width), F32)],
        ),
        **params("attend_back", 6 * rows * width * hw + 10 * rows * seq * hw, 8 * rows * width),
    )(lengths, *in_hbm(normed, q, k, v, lse, near, other))


def normed_back_kernel(
    items, share, len_ref, tok_ref, dq_ref, dk_ref, dv_ref, qw_ref, kw_ref, vw_ref, vec_in, low_in,
    send_ref, keep_ref, pass_ref, sums_ref, part_ref
):
    seq = tok_ref.shape[0]
    item = pl.program_id(0)
    length = len_ref[item]
    me = lax.axis_index("mp")

    @pl.when(item == 0)
    def _():
        sums_ref[...] = jnp.zeros_like(sums_ref)

    def run(span):
        start = pl.multiple_of(item * seq, seq)

        def back_rows(index, rows):
            piece = dot(dq_ref[rows, :], qw_ref[...]) + dot(dk_ref[rows, :], kw_ref[...]) + dot(dv_ref[rows, :], vw_ref[...])
            part_ref[pl.ds(pl.multiple_of(start + index * PIECE, PIECE), PIECE), :] = piece
            normal, unused = norm_stats(tok_ref[rows, :].astype(F32))
            sums_ref[row(0), :] += jnp.sum(piece * normal, axis=0, keepdims=True)
            sums_ref[row(1), :] += jnp.sum(piece, axis=0, keepdims=True)

        over_pieces(span, back_rows)
        if span < seq:
            part_ref[pl.ds(pl.multiple_of(start + span, span), seq - span), :] = jnp.zeros(
                (seq - span, part_ref.shape[1]), F32
            )

    half = seq // 2

    @pl.when(length <= half)
    def _():
        run(half)

    @pl.when(length > half)
    def _():
        run(seq)

    @pl.when(item == items - 1)
    def _():
        def block(k):
            return part_ref[pl.ds(pl.multiple_of((me ^ k) * share, PIECE), share), :]

        keep_ref[...] = block(0)
        pass_ref[...] = block(2)
        send_ref[:share, :] = block(1).astype(BF16)
        send_ref[share : 2 * share, :] = block(3).astype(BF16)
        sums_ref[2:5, :] = 0.5 * vec_in[0:3, :]
        sums_ref[5:6, :] = 0.5 * low_in[0:1, :]
        vectors = sums_ref[0:VECTORS, :]
        send_ref[2 * share :, :] = jnp.concatenate(
            [vectors, jnp.zeros((PAD - VECTORS, vectors.shape[1]), F32)], axis=0
        ).astype(BF16)


def normed_back(lengths, rows2d, dq, dk, dv, query_w, key_w, value_w, vec_in, low_in, items, seq, share):
    rows, width = rows2d.shape
    hw = query_w.shape[0]
    row_block = lambda cols: pl.BlockSpec((seq, cols), lambda i, n: (i, 0))
    whole = lambda dims: pl.BlockSpec(dims, lambda i, n: (0,) * len(dims))
    return pl.pallas_call(
        functools.partial(normed_back_kernel, items, share),
        out_shape=[
            shape((2 * share + PAD, width), BF16),
            pltpu.HBM((share, width), F32),
            pltpu.HBM((share, width), F32),
            shape((8, width), F32),
        ],
        grid_spec=pltpu.PrefetchScalarGridSpec(
            num_scalar_prefetch=1,
            grid=(items,),
            in_specs=[row_block(width)]
            + [row_block(hw)] * 3
            + [whole((hw, width))] * 3
            + [whole(vec_in.shape), whole(low_in.shape)],
            out_specs=[
                whole((2 * share + PAD, width)),
                whole((share, width)),
                whole((share, width)),
                whole((8, width)),
            ],
            scratch_shapes=[pltpu.VMEM((rows, width), F32)],
        ),
        **params("normed_back", 6 * rows * width * hw, 8 * rows * width),
    )(lengths, *in_hbm(rows2d, dq, dk, dv, query_w, key_w, value_w, vec_in, low_in))


def load_all(pairs, sems):
    copies = [pltpu.make_async_copy(source, target, sems.at[i]) for i, (source, target) in enumerate(pairs)]
    for copy in copies:
        copy.start()
    return copies


def halves(count):
    return [slice(start, start + count // 2) for start in range(0, count, count // 2)]


def project_kernel(near_ref, far_ref, own_ref, pack_ref, out_ref):
    hw = own_ref.shape[0]
    for cols in tiles(out_ref.shape[1]):
        out_ref[:, cols] = (dot(near_ref[...], own_ref[:, cols]) + dot(far_ref[...], pack_ref[:hw, cols])).astype(BF16)


def project(near, far, own, pack):
    span, hw = near.shape
    width = own.shape[1]
    return pl.pallas_call(
        project_kernel,
        out_shape=shape((span, width), BF16),
        in_specs=[vmem()] * 4,
        out_specs=vmem(),
        **params("project", 4 * span * width * hw, 4 * span * width),
    )(near, far, *in_hbm(own), pack)


def quad_pairs(own_ref, parts, buf, begin=0):
    rows = own_ref.shape[0] // 4
    mine = lax.axis_index("dp") % 4
    pairs = [(own_ref, buf.at[0])]
    for index, part in enumerate(parts):
        count = rows // 2 if len(parts) == 5 and index > 2 else rows
        start = (mine ^ min(index, 3)) * rows + (count if index == 4 else 0)
        pairs.append((part.at[pl.ds(begin, count), :], buf.at[1, pl.ds(pl.multiple_of(start, 32), count), :]))
    return pairs


def conv_pairs(conv_ref, parts, wc):
    return quad_pairs(conv_ref, parts, wc, parts[0].shape[0] - conv_ref.shape[0] // 4)


def cot_pairs(cot_ref, far_cot, cots):
    span = cots.shape[1]
    start = pl.multiple_of(chip_half() * span, PIECE)
    return [(cot_ref.at[pl.ds(start, span), :], cots.at[0]), (far_cot, cots.at[1])]


def expand_kernel(tok_ref, vec_ref, part_ref, other_ref, out_far, up_ref, *rest):
    up_parts = rest[:5]
    mid_ref, normed_ref, act_ref, slope_ref, wu, tok_buf, sems = rest[5:]
    span, width = mid_ref.shape
    start = pl.multiple_of(chip_half() * span, PIECE)
    copies = load_all([(tok_ref.at[pl.ds(start, span), :], tok_buf)] + quad_pairs(up_ref, up_parts, wu), sems)
    copies[0].wait()

    def add_rows(index, rows):
        mid = tok_buf[rows, :].astype(F32) + vec_ref[row(OUT_B), :] + part_ref[rows, :].astype(F32) + other_ref[rows, :].astype(F32)
        mid_ref[rows, :] = mid
        normal, unused = norm_stats(mid)
        normed_ref[rows, :] = (normal * vec_ref[row(GAIN_MLP), :] + vec_ref[row(BIAS_MLP), :]).astype(BF16)

    over_pieces(span, add_rows)
    for copy in copies[1:]:
        copy.wait()
    hw = out_far.shape[0] - PAD

    def body(step, carry):
        block = step % 2
        rows = pl.ds(pl.multiple_of(step // 2 * (span // 2), PIECE), span // 2)
        for cols in tiles(width):
            own_bias, other_bias = vec_ref[row(UP_B), cols], out_far[hw:, cols].astype(F32)[0:1]
            preact = dot(normed_ref[rows, :], wu[block, :, cols]) + jnp.where(block == 0, own_bias, other_bias)
            normal_cdf = 0.5 * lax.erf(preact * (0.5**0.5)) + 0.5
            density = jnp.exp(preact * preact * -0.5) * 0.3989422804014327
            act_ref[block, rows, cols] = (preact * normal_cdf).astype(BF16)
            slope_ref[block, rows, cols] = (normal_cdf + preact * density).astype(BF16)
        return carry

    lax.fori_loop(0, 4, body, 0)


def expand(rows2d, vecs, part, other, out_far, up_w, up_parts):
    span, width = part.shape
    return pl.pallas_call(
        expand_kernel,
        out_shape=[
            shape((span, width), F32),
            shape((span, width), BF16),
            shape((2, span, width), BF16),
            shape((2, span, width), BF16),
        ],
        in_specs=[anywhere()] + [vmem()] * 4 + [anywhere()] * 6,
        out_specs=[vmem()] * 4,
        scratch_shapes=[
            pltpu.VMEM((2, width, width), BF16),
            pltpu.VMEM((span, width), BF16),
            pltpu.SemaphoreType.DMA((7,)),
        ],
        **params("expand", 4 * span * width * width, 14 * width * width),
    )(*in_hbm(rows2d, vecs), part, other, *in_hbm(out_far, up_w, *up_parts))


def contract_kernel(act_ref, down_ref, *rest):
    down_parts = rest[:4]
    out_ref, wd, sems = rest[4:]
    for copy in load_all(quad_pairs(down_ref, down_parts, wd), sems):
        copy.wait()
    for cols in tiles(out_ref.shape[1]):
        out_ref[:, cols] = (dot(act_ref[0], wd[0, :, cols]) + dot(act_ref[1], wd[1, :, cols])).astype(BF16)


def contract(act, down_w, down_parts):
    unused, span, width = act.shape
    return pl.pallas_call(
        contract_kernel,
        out_shape=shape((span, width), BF16),
        in_specs=[vmem()] + [anywhere()] * 5,
        out_specs=vmem(),
        scratch_shapes=[pltpu.VMEM((2, width, width), BF16), pltpu.SemaphoreType.DMA((5,))],
        **params("contract", 4 * span * width * width, 8 * width * width),
    )(act, *in_hbm(down_w, *down_parts))


def piece_place(info_ref, items, seq, span, index):
    piece = chip_half() * (span // PIECE) + index
    per_item = seq // PIECE
    item = piece // per_item
    length = info_ref[item]
    slot = lax.broadcasted_iota(jnp.int32, (PIECE, 1), 0) + (piece % per_item) * PIECE
    return item, length, (slot < length).astype(F32)


def convolve_kernel(items, seq, info_ref, vec_ref, mid_ref, part_ref, other_ref, conv_ref, *rest):
    parts, (cot_ref, far_cot) = rest[:4], rest[4:6]
    low_ref, z_ref, sums_ref, wc, cots, sems = rest[6:]
    span, width = mid_ref.shape
    block = wc.shape[1]
    copies = load_all(conv_pairs(conv_ref, parts, wc) + cot_pairs(cot_ref, far_cot, cots), sems)
    low_ref[...] = (
        mid_ref[...] + vec_ref[row(DOWN_B), :] + part_ref[...].astype(F32) + other_ref[...].astype(F32)
    ).astype(BF16)
    for copy in copies:
        copy.wait()
    sums_ref[...] = jnp.zeros_like(sums_ref)
    for k in range(2):
        z_ref[k] = dot_cols(low_ref[...], wc[k])

        def add_sums(index, rows):
            item, unused, mask = piece_place(info_ref, items, seq, span, index)
            z = z_ref[k, rows, :]
            masked = z * mask
            upstream = cots[k, rows, :].astype(F32) * mask
            lines = [
                jnp.sum(part, axis=0, keepdims=True) for part in (masked, masked * z, upstream, upstream * z)
            ]
            total = jnp.concatenate(lines, axis=0)
            for base in range(0, block, CH):
                sums_ref[item] += total[:, base : base + CH]

        over_pieces(span, add_sums)


def convolve(info, vecs, mid, part, other, conv_w, parts, cot_rows, far_cot, items, seq):
    span, width = mid.shape
    block = cot_rows.shape[1]
    return pl.pallas_call(
        functools.partial(convolve_kernel, items, seq),
        out_shape=[shape((span, width), BF16), shape((2, span, block), F32), shape((items, 4, CH), F32)],
        in_specs=[smem()] + [vmem()] * 4 + [anywhere()] * 7,
        out_specs=[vmem()] * 3,
        scratch_shapes=[
            pltpu.VMEM((2, block, width), BF16),
            pltpu.VMEM((2, span, block), BF16),
            pltpu.SemaphoreType.DMA((7,)),
        ],
        **params("convolve", 4 * span * width * block, 14 * width * width),
    )(info, *in_hbm(vecs), mid, part, other, *in_hbm(conv_w, *parts, cot_rows, far_cot))


def norm_back_kernel(items, seq, norm_at, info_ref, norm_ref, tot_ref, got_ref, z_ref, conv_ref, *rest):
    parts, (cot_ref, far_cot) = rest[:4], rest[4:6]
    near_ref, far_ref, dz_ref, out_ref, sums_ref, wc, cots, sems = rest[6:]
    span, width = out_ref.shape
    block = z_ref.shape[2]
    copies = load_all(conv_pairs(conv_ref, parts, wc) + cot_pairs(cot_ref, far_cot, cots), sems)
    scale = norm_ref[row(MIXED), norm_at : norm_at + CH]
    shift = norm_ref[row(MIXED), norm_at + CH : norm_at + 2 * CH]

    def item_terms(item, length):
        count = (8 * length).astype(F32)
        total = tot_ref[item] + got_ref[item]
        center = total[0:1] / count
        spread = lax.rsqrt(total[1:2] / count - center * center + EPSILON)
        plain = total[2:3]
        cross = spread * (total[3:4] - center * plain)
        return count, center, spread, plain, cross

    sums_ref[...] = jnp.zeros_like(sums_ref)
    for item in range(items):
        unused, unused, unused, plain, cross = item_terms(item, info_ref[item])
        sums_ref[0:1, :CH] += cross
        sums_ref[0:1, CH : 2 * CH] += plain
    for copy in copies:
        copy.wait()

    def back_rows(index, rows):
        item, length, mask = piece_place(info_ref, items, seq, span, index)
        count, center, spread, plain, cross = item_terms(item, length)
        terms = [center, spread, plain / count, cross / count, scale, shift, spread * scale]
        wide = [jnp.concatenate([t] * (block // CH), axis=1) for t in terms]
        center, spread, plain, cross, scale_w, shift_w, factor = wide
        for k, vol_ref in enumerate((near_ref, far_ref)):
            normal = (z_ref[k, rows, :] - center) * spread
            vol_ref[rows, :] = (mask * (scale_w * normal + shift_w)).astype(BF16)
            upstream = cots[k, rows, :].astype(F32)
            dz_ref[k, rows, :] = (mask * factor * (upstream - plain - normal * cross)).astype(BF16)

    over_pieces(span, back_rows)
    for cols in tiles(width):
        out_ref[:, cols] = (dot(dz_ref[0], wc[0, :, cols]) + dot(dz_ref[1], wc[1, :, cols])).astype(BF16)


def norm_back(info, vecs, total, got, z, conv_w, parts, cot_rows, far_cot, items, seq, norm_at):
    unused, span, block = z.shape
    width = conv_w.shape[1]
    return pl.pallas_call(
        functools.partial(norm_back_kernel, items, seq, norm_at),
        out_shape=[
            shape((span, block), BF16),
            shape((span, block), BF16),
            shape((2, span, block), BF16),
            shape((span, width), BF16),
            shape((8, width), F32),
        ],
        in_specs=[smem()] + [vmem()] * 4 + [anywhere()] * 7,
        out_specs=[vmem()] * 5,
        scratch_shapes=[
            pltpu.VMEM((2, block, width), BF16),
            pltpu.VMEM((2, span, block), BF16),
            pltpu.SemaphoreType.DMA((7,)),
        ],
        **params("norm_back", 4 * span * width * block, 6 * width * width),
    )(info, *in_hbm(vecs), total, got, z, *in_hbm(conv_w, *parts, cot_rows, far_cot))


def mlp_back_kernel(part_ref, other_ref, slope_ref, up_ref, down_ref, *rest):
    up_parts, down_parts = rest[:5], rest[5:9]
    du_ref, out_ref, sums_ref, up_sums, low_ref, wu, wd, sems = rest[9:]
    span, width = out_ref.shape
    copies = load_all(quad_pairs(down_ref, down_parts, wd) + quad_pairs(up_ref, up_parts, wu), sems)
    sums_ref[...] = jnp.zeros_like(sums_ref)
    up_sums[...] = jnp.zeros_like(up_sums)
    for rows in halves(span):
        grad = part_ref[rows, :].astype(F32) + other_ref[rows, :].astype(F32)
        low_ref[rows, :] = grad.astype(BF16)
        sums_ref[0:1, :] += jnp.sum(grad, axis=0, keepdims=True)
    for copy in copies[:5]:
        copy.wait()

    def body(step, carry):
        block = step % 2
        rows = pl.ds(pl.multiple_of(step // 2 * (span // 2), PIECE), span // 2)
        for cols in tiles(width):
            grad = dot_cols(low_ref[rows, :], wd[block, cols, :]) * slope_ref[block, rows, cols].astype(F32)
            low = grad.astype(BF16)
            du_ref[block, rows, cols] = low
            up_sums[block, 0:1, cols] += jnp.sum(low.astype(F32), axis=0, keepdims=True)
        return carry

    lax.fori_loop(0, 4, body, 0)
    for copy in copies[5:]:
        copy.wait()
    for cols in tiles(width):
        out_ref[:, cols] = (dot_cols(du_ref[0], wu[0, cols, :]) + dot_cols(du_ref[1], wu[1, cols, :])).astype(BF16)


def mlp_back(part, other, slope, up_w, down_w, up_parts, down_parts):
    span, width = part.shape
    return pl.pallas_call(
        mlp_back_kernel,
        out_shape=[
            shape((2, span, width), BF16),
            shape((span, width), BF16),
            shape((8, width), F32),
            shape((2, 8, width), F32),
        ],
        in_specs=[vmem()] * 3 + [anywhere()] * 11,
        out_specs=[vmem()] * 4,
        scratch_shapes=[
            pltpu.VMEM((span, width), BF16),
            pltpu.VMEM((2, width, width), BF16),
            pltpu.VMEM((2, width, width), BF16),
            pltpu.SemaphoreType.DMA((11,)),
        ],
        **params("mlp_back", 8 * span * width * width, 20 * width * width),
    )(part, other, slope, *in_hbm(up_w, down_w, *up_parts, *down_parts))


def mid_back_kernel(share, vec_ref, mid_ref, part_ref, other_ref, grad_ref, got_ref, out_w, pack_ref, *rest):
    near_ref, far_ref, em_ref, mine_ref, sums_ref, dmid_ref = rest
    span, width = mid_ref.shape
    sums_ref[...] = jnp.zeros_like(sums_ref)

    def back_rows(index, rows):
        normal, inverse = norm_stats(mid_ref[rows, :])
        grad = grad_ref[rows, :].astype(F32) + got_ref[rows, :].astype(F32)
        dmid = part_ref[rows, :].astype(F32) + other_ref[rows, :].astype(F32)
        dmid += norm_backward(grad, normal, inverse, vec_ref[row(GAIN_MLP), :])
        dmid_ref[rows, :] = dmid
        em_ref[rows, :] = dmid.astype(BF16)
        sums_ref[0:1, :] += jnp.sum(grad * normal, axis=0, keepdims=True)
        sums_ref[1:2, :] += jnp.sum(grad, axis=0, keepdims=True)
        sums_ref[2:3, :] += jnp.sum(dmid, axis=0, keepdims=True)

    over_pieces(span, back_rows)
    far_ref[...] = dot_cols(em_ref[...], pack_ref[: out_w.shape[0], :]).astype(BF16)
    near_ref[...] = dot_cols(em_ref[...], out_w[...]).astype(BF16)
    mine_ref[...] = dmid_ref[pl.ds(pl.multiple_of(lax.axis_index("mp") % 2 * share, PIECE), share), :]


def mid_back(vecs, mid, part, other, grad, got, out_w, pack):
    span, width = mid.shape
    hw = out_w.shape[0]
    return pl.pallas_call(
        functools.partial(mid_back_kernel, span // 2),
        out_shape=[
            shape((span, hw), BF16),
            shape((span, hw), BF16),
            shape((span, width), BF16),
            shape((span // 2, width), F32),
            shape((8, width), F32),
        ],
        in_specs=[vmem()] * 8,
        out_specs=[vmem()] * 5,
        scratch_shapes=[pltpu.VMEM((span, width), F32)],
        **params("mid_back", 4 * span * width * hw, 12 * width * width),
    )(*in_hbm(vecs), mid, part, other, grad, got, *in_hbm(out_w, pack))


LINKS = {"y": ("mp", 2), "x": ("dp", 1), "z": ("dp", 2)}


class Lane:
    def __init__(self, blocks, rows, parts, link):
        self.blocks, self.rows, self.parts, self.link = blocks, rows, parts, link


class Kept:
    def __init__(self, blocks, rows, array, link, place):
        self.blocks, self.rows, self.array, self.link, self.place = blocks, rows, array, link, place


def high_of(link):
    axis, bit = LINKS[link]
    return (lax.axis_index(axis) // bit) % 2


def aligned(value, rows):
    return value if isinstance(value, int) else pl.multiple_of(value, rows & -rows)


def product_rows(left, right, block, out_ref, at):
    size = left.shape[-1]
    for base in range(0, size, TILE):
        cols = slice(base, min(base + TILE, size))
        lhs = left[block, :, cols] if len(left.shape) == 3 else left[:, cols]
        rhs = right[block] if len(right.shape) == 3 else right[...]
        out_ref[at + base : at + cols.stop, :] = dot_rows(lhs, rhs).astype(BF16)


def products_kernel(lefts, *refs):
    right, out_ref = refs[-2:]
    size = out_ref.shape[0] // 2
    for block in range(2):
        product_rows(refs[block] if lefts == 2 else refs[0], right, block, out_ref, block * size)


def products(name, lefts, right):
    span, width = right.shape[-2:]
    size = lefts[0].shape[-1]
    return pl.pallas_call(
        functools.partial(products_kernel, len(lefts)),
        out_shape=shape((2 * size, width), BF16),
        in_specs=[vmem()] * (len(lefts) + 1),
        out_specs=vmem(),
        **params(name, 4 * span * size * width, 8 * size * width),
    )(*lefts, right)


def emit_kernel(count, inputs, lanes, links, *refs):
    lefts, rights = refs[:count], refs[count : 2 * count]
    sources = list(refs[2 * count : 2 * count + inputs])
    outs = refs[2 * count + inputs :]
    if count:
        product, outs = outs[-1], outs[:-1]
        sources = [product] + sources
        total = product.shape[0] // 2
        begin = 0
        for left, right in zip(lefts, rights):
            for block in range(2):
                product_rows(left, right, block, product, block * total + begin)
            begin += left.shape[-1]
    sends = dict(zip(links, outs))
    kept = iter(outs[len(links) :])
    last = outs[-1]
    places = dict.fromkeys(list(links) + [None], 0)

    for lane in lanes:

        def total_of(block, start, size):
            values = [
                sources[index][pl.ds(aligned(base + block * stride + start, size), size), :]
                for index, base, stride in lane.parts
            ]
            if len(values) == 1:
                return values[0]
            return (values[0].astype(F32) + values[1].astype(F32)).astype(BF16)

        place = places[lane.link]
        if lane.link is None:
            last[place : place + lane.rows, :] = total_of(0, 0, lane.rows)
            places[None] += lane.rows
            continue
        send, keep = sends[lane.link], next(kept)
        if lane.link == "y":
            send[place : place + lane.rows, :] = total_of(1, 0, lane.rows)
            keep[...] = total_of(0, 0, lane.rows)
            places["y"] += lane.rows
            continue
        half = lane.rows // 2
        high = high_of(lane.link)
        for block in range(lane.blocks):
            rows = slice(block * half, (block + 1) * half)
            keep[rows, :] = total_of(block, high * half, half)
            send[place + rows.start : place + rows.stop, :] = total_of(block, (1 - high) * half, half)
        places[lane.link] += lane.blocks * half


def emit(name, lefts, rights, inputs, lanes, width, far=False):
    places = dict.fromkeys(list(LINKS) + [None], 0)
    kept = []
    for lane in lanes:
        sent = lane.blocks * lane.rows // 2 if lane.link else lane.rows
        if lane.link:
            blocks, rows = (1, lane.rows) if lane.link == "y" else (lane.blocks, lane.rows // 2)
            kept.append(Kept(blocks, rows, None, lane.link, places[lane.link]))
        places[lane.link] += sent
    links = [link for link in LINKS if places[link]]
    out_rows = [places[link] for link in links] + [k.blocks * k.rows for k in kept]
    if places[None]:
        out_rows.append(places[None])
    size = sum(left.shape[-1] for left in lefts)
    span = rights[0].shape[-2] if rights else 0
    results = pl.pallas_call(
        functools.partial(emit_kernel, len(lefts), len(inputs), lanes, links),
        out_shape=[
            pltpu.HBM((rows, width), BF16) if far and len(links) <= i < len(links) + len(kept) else shape((rows, width), BF16)
            for i, rows in enumerate(out_rows)
        ],
        in_specs=[vmem()] * (2 * len(lefts) + len(inputs)),
        out_specs=[vmem()] * len(out_rows),
        scratch_shapes=[pltpu.VMEM((2 * size, width), BF16)] if lefts else [],
        **params(name, 4 * span * size * width, 8 * size * width),
    )(*lefts, *rights, *inputs)
    for keep, array in zip(kept, results[len(links) :]):
        keep.array = array
        keep.far = far
    return dict(zip(links, results)), kept, results[-1] if places[None] else None


def send_all(sends):
    return {link: swap(value, *LINKS[link]) for link, value in sends.items()}


def turn(name, kept, got, links, width, fresh=(), far=False):
    inputs = [k.array for k in kept] + list(got.values()) + [lane[0] for lane in fresh]
    inputs = [in_hbm(v)[0] if k.far else v for k, v in zip(kept, inputs)] + inputs[len(kept) :]
    came = {link: len(kept) + i for i, link in enumerate(got)}
    lanes = []
    for i, (k, link) in enumerate(zip(kept, links)):
        lanes.append(Lane(k.blocks, k.rows, [(i, 0, k.rows), (came[k.link], k.place, k.rows)], link))
    for i, (lane, link) in enumerate(zip(fresh, links[len(kept) :])):
        lanes.append(Lane(lane[3], lane[4], [(len(kept) + len(got) + i, lane[1], lane[2])], link))
    return emit(name, [], [], inputs, lanes, width, far)


def spread_kernel(lanes, cuts, flip, *refs):
    first, gots, outs, total = refs[0], refs[1:5], refs[5:-1], refs[-1]
    bits = {"x": high_of("x"), "z": high_of("z")}
    places = [0, 0]
    sizes = [sum(lane[1] for lane in lanes if lane[3] == group) for group in range(2)]
    for base, rows, order, group in lanes:
        at = places[group]
        places[group] += rows
        near, far = ("z", "x") if group == 0 else ("x", "z")
        got_near, got_far = gots[2 * group], gots[2 * group + 1]
        offset = at + (sizes[0] if group else 0)
        pieces = [
            (first[offset : offset + rows, :], ()),
            (got_near[at : at + rows, :], (near,)),
            (got_far[at : at + rows, :], (far,)),
            (got_far[sizes[group] + at : sizes[group] + at + rows, :], (near, far)),
        ]
        for value, flipped in pieces:
            index = [1 - bits[link] if link in flipped else bits[link] for link in order]
            start = base + (index[0] * 2 + index[1]) * rows
            total[pl.ds(aligned(start, rows), rows), :] = value.astype(F32)
    begin = 0
    for i, (out, size) in enumerate(zip(outs, cuts)):
        value = total[begin : begin + size, :]
        out[...] = value.T if i in flip else value
        begin += size


def spread(name, lanes, cuts, flip, first, gots):
    width = first.shape[1]
    return pl.pallas_call(
        functools.partial(spread_kernel, lanes, cuts, flip),
        out_shape=[shape((width, size) if i in flip else (size, width), F32) for i, size in enumerate(cuts)],
        in_specs=[vmem()] * 5,
        out_specs=[vmem()] * len(cuts),
        scratch_shapes=[pltpu.VMEM((sum(cuts), width), F32)],
        **params(name, 0, 8 * sum(cuts) * width),
    )(first, *gots)


def pass_kernel(passed_ref, got_ref, sums_ref, up_ref, send_ref, whole_ref):
    share = passed_ref.shape[0]
    send_ref[:share, :] = (passed_ref[...] + got_ref[share : 2 * share, :].astype(F32)).astype(BF16)
    whole = sums_ref[0:VECTORS, :].astype(BF16).astype(F32) + got_ref[2 * share :, :].astype(F32)[0:VECTORS]
    whole = whole.astype(BF16).astype(F32)
    zero = jnp.zeros((1, whole.shape[1]), F32)
    send_ref[share:, :] = jnp.concatenate([whole, up_ref[1, 0:1, :], zero], axis=0).astype(BF16)
    whole_ref[...] = jnp.concatenate([whole, up_ref[0, 0:1, :], zero], axis=0)


def pass_on(passed, got, sums, up_sums):
    share, width = passed.shape
    return pl.pallas_call(
        pass_kernel,
        out_shape=[shape((share + 8, width), BF16), shape((8, width), F32)],
        in_specs=[vmem()] * 4,
        out_specs=[vmem()] * 2,
        **params("pass_on", 0, 8 * share * width),
    )(*in_hbm(passed), got, sums, up_sums)


def finish_kernel(tok_ref, vec_ref, own_ref, got_ref, last_ref, mine_ref, out_ref, tok_buf, sem):
    share = out_ref.shape[0]
    start = pl.multiple_of(lax.axis_index("mp") * share, PIECE)
    copy = pltpu.make_async_copy(tok_ref.at[pl.ds(start, share), :], tok_buf, sem)
    copy.start()
    copy.wait()

    def back_rows(index, rows):
        normal, inverse = norm_stats(tok_buf[rows, :].astype(F32))
        grad = own_ref[rows, :] + got_ref[rows, :].astype(F32) + last_ref[rows, :].astype(F32)
        out_ref[rows, :] = mine_ref[rows, :] + norm_backward(grad, normal, inverse, vec_ref[row(GAIN_ATTN), :])

    over_pieces(share, back_rows)


def finish(rows2d, vecs, own, got, last, mine):
    share, width = own.shape
    return pl.pallas_call(
        finish_kernel,
        out_shape=shape((share, width), F32),
        in_specs=[anywhere()] + [vmem()] * 5,
        out_specs=vmem(),
        scratch_shapes=[pltpu.VMEM((share, width), BF16), pltpu.SemaphoreType.DMA],
        **params("finish", 0, 14 * share * width),
    )(*in_hbm(rows2d, vecs, own), got, last, *in_hbm(mine))


def add_low(left, right):
    return (left.astype(F32) + right.astype(F32)).astype(BF16)


def bit_of(axis, bit):
    return (lax.axis_index(axis) // bit) % 2


def take_half(value, high):
    half = value.shape[0] // 2
    return lax.dynamic_slice_in_dim(value, high * half, half, 0)


def put_half(mine, other, high):
    return jnp.concatenate([jnp.where(high > 0, other, mine), jnp.where(high > 0, mine, other)], axis=0)


def late_bits():
    bits = []
    bit = 4
    while bit < lax.axis_size("dp"):
        bits.append(bit)
        bit *= 2
    return bits


def finish_reduce(current, bit):
    high = bit_of("dp", bit)
    return add_low(take_half(current, high), swap(take_half(current, 1 - high), "dp", bit))


def finish_gather(current, bit):
    return put_half(current, swap(current, "dp", bit), bit_of("dp", bit))


def shards(
    tokens, lengths, gain_attn, bias_attn, query_w, query_b, key_w, value_w, value_b, out_w, out_b, gain_mlp, bias_mlp,
    up_w, up_b, down_w, down_b, deconv_w, scale_norm, shift_norm, cotangent
):
    items, seq, width = tokens.shape
    rows = items * seq
    me = lax.axis_index("mp")
    share = rows // lax.axis_size("mp")
    span = rows // 2
    hw = query_w.shape[1]
    rows2d = tokens.reshape(rows, width)
    side = bit_of("dp", 1)
    chip = bit_of("mp", 2)
    mixed = jnp.concatenate([query_b, value_b, scale_norm, shift_norm])
    mixed = jnp.pad(mixed, (0, width - mixed.shape[0]))
    vecs = jnp.concatenate([out_b, gain_mlp, bias_mlp, down_b, gain_attn, bias_attn, up_b, mixed])
    vecs = vecs.astype(F32).reshape(8, width)
    weights = [query_w.T, key_w.T, value_w.T]
    conv_w = deconv_w.T

    quarter = width // 4
    mine = lax.axis_index("dp") % 4

    def quarter_of(weight, index):
        count = weight.shape[0] // 4
        return lax.dynamic_slice_in_dim(weight, index * count, count, 0)

    def low_quarter(index):
        return jnp.concatenate([quarter_of(down_w, index), quarter_of(conv_w, index)], axis=0)

    bias_rows = jnp.broadcast_to(up_b[None, :], (PAD, width))
    out_far = swap(jnp.concatenate([out_w, bias_rows], axis=0), "mp", 2)
    up_part = swap(quarter_of(up_w, mine), "mp", 2)
    low_part = swap(low_quarter(mine), "mp", 2)

    normed, q, k, v, lse, near, other = attend(lengths, rows2d, vecs, *weights, items, seq)
    out_far, near, other, up_part, low_part = join(out_far, near, other, up_part, low_part)
    far = swap(other, "mp", 2)
    up_parts = [up_part, swap(up_part, "dp", 1), swap(up_part, "dp", 2)]
    cot_rows = cotangent.reshape(rows, -1)
    cot_sent = lax.dynamic_slice_in_dim(cot_rows, (1 - chip) * span, span, 0)
    low_sent = low_quarter(mine ^ 3)
    far, low_part, low_sent, cot_sent, *up_parts = join(far, low_part, low_sent, cot_sent, *up_parts)
    low_last = swap(low_sent, "mp", 2)
    last_half = quarter // 2
    up_parts.append(swap(up_parts[2][:last_half], "dp", 1))
    up_parts.append(swap(up_parts[1][last_half:], "dp", 2))

    part = project(near, far, out_w, out_far)
    part_got = swap(part, "mp", 1)
    part_got, low_part, cot_sent, *up_parts = join(part_got, low_part, cot_sent, *up_parts)
    down_parts = [low_part, swap(low_part, "dp", 1), swap(low_part, "dp", 2)]
    far_cot = swap(cot_sent, "mp", 2)
    mid, normed_two, act, slope = expand(rows2d, vecs, part, part_got, out_far, up_w, up_parts)
    act, low_last, *down_parts = join(act, low_last, *down_parts)
    down_parts.append(low_last)
    part = contract(act, down_w, down_parts)
    part, far_cot = join(part, far_cot)
    low, z, sums = convolve(
        lengths, vecs, mid, part, swap(part, "mp", 1), conv_w, down_parts, cot_rows, far_cot, items, seq
    )
    sums = sums + swap(sums, "mp", 1)
    vol_near, vol_far, dz, grad, norm_sums = norm_back(
        lengths, vecs, sums, swap(sums, "mp", 2), z, conv_w, down_parts, cot_rows, far_cot, items, seq, 2 * hw
    )
    grad_got = swap(grad, "mp", 1)
    conv_raw = products("conv_grad", [dz], low)
    grad_got, conv_raw = join(grad_got, conv_raw)
    block = conv_w.shape[0]
    half = block // 2
    third = width // 3
    lanes = [Lane(2, third, [(0, i * third, width)], link) for i, link in enumerate("yxz")]
    sends, kept, unused = emit("down_grad", [act], [add_low(grad, grad_got)], [], lanes, width)
    grad_got, sends["y"], sends["x"], sends["z"] = join(grad_got, sends["y"], sends["x"], sends["z"])
    came = send_all(sends)
    du, back, low_sums, up_sums = mlp_back(grad, grad_got, slope, up_w, down_w, up_parts, down_parts)
    back, came["y"], came["x"], came["z"] = join(back, came["y"], came["x"], came["z"])
    back_got = swap(back, "mp", 1)
    up_raw = products("up_grad", [normed_two], du)
    fresh = [(conv_raw, 0, block, 2, half), (conv_raw, half, block, 2, half)]
    sends, kept, unused = turn("turn_one", kept, came, "xzyxz", width, fresh)
    back_got, up_raw, sends["y"], sends["x"], sends["z"] = join(back_got, up_raw, sends["y"], sends["x"], sends["z"])
    came = send_all(sends)
    do_near, do_far, em, dmid, vec_sums = mid_back(vecs, mid, grad, grad_got, back, back_got, out_w, out_far)
    do_far, em, came["y"] = join(do_far, em, came["y"])
    do_got = swap(do_far, "mp", 2)
    out_raw = products("out_grad", [near, far], em)
    do_got, out_raw, came["y"], came["x"], came["z"] = join(do_got, out_raw, came["y"], came["x"], came["z"])
    cut = width * 5 // 12
    fresh = [(up_raw, 0, width, 2, cut), (up_raw, cut, width, 2, cut), (up_raw, 2 * cut, width, 2, width - 2 * cut)]
    fresh.append((out_raw, 0, hw, 2, hw))
    sends, kept, unused = turn("turn_two", kept, came, "zyxzxyxzz", width, fresh, True)
    do_got, sends["y"], sends["x"], sends["z"] = join(do_got, sends["y"], sends["x"], sends["z"])
    came = send_all(sends)

    *dqkv, qkv_grad, bias_sums = attend_back(lengths, normed, q, k, v, lse, do_near, do_got, items, seq, share)
    qkv_grad, vol_far, came["y"], came["x"], came["z"], *dqkv = join(
        qkv_grad, vol_far, came["y"], came["x"], came["z"], *dqkv
    )
    cut = qkv_grad.shape[0] * 4 // 9
    fresh = [(qkv_grad, 0, 0, 1, cut), (qkv_grad, cut, 0, 1, qkv_grad.shape[0] - cut)]
    sizes = [k.blocks * k.rows for k in kept[:3]]
    links = [None] * 3 + ["y", "y", "x", "z", "y", "y", "x", "z"]
    sends, kept, first = turn("turn_three", kept, came, links, width, fresh, True)
    for bit in late_bits():
        first = finish_reduce(first, bit)
    came = send_all(sends)
    sent, own, passed, own_sums = normed_back(
        lengths, rows2d, *dqkv, *weights, vec_sums, low_sums, items, seq, share
    )
    first, sent, came["y"], came["x"], came["z"] = join(first, sent, came["y"], came["x"], came["z"])
    for bit in reversed(late_bits()):
        first = finish_gather(first, bit)
    got = swap(sent, "mp", 1)
    conv_sizes = [k.blocks * k.rows for k in kept[:2]]
    came = {link: in_hbm(value)[0] for link, value in came.items()}
    sends, kept, early = turn("turn_four", kept, came, [None, None] + list("zyxxzx"), width)
    came = send_all(sends)
    first, got, vol_far, came["y"], came["x"], came["z"] = join(first, got, vol_far, came["y"], came["x"], came["z"])
    kept = [kept[i] for i in (0, 1, 4, 2, 3, 5)]
    unused, unused, last = turn("turn_five", kept, came, [None] * 6, width)
    last_sizes = [k.blocks * k.rows for k in kept] + conv_sizes
    last = jnp.concatenate([last, early], axis=0)
    for bit in late_bits():
        last = finish_reduce(last, bit)
    edge = sizes[0]
    sent_near = [first[:edge], first[edge:]]
    near_got = [swap(sent_near[0], "dp", 2), swap(sent_near[1], "dp", 1)]
    second, whole = pass_on(passed, got, own_sums, up_sums)
    second = swap(second, "mp", 2)
    far_got = [
        swap(jnp.concatenate([sent_near[0], near_got[0]], axis=0), "dp", 1),
        swap(jnp.concatenate([sent_near[1], near_got[1]], axis=0), "dp", 2),
    ]
    last, second, vol_far, *far_got = join(last, second, vol_far, *far_got)
    vol_got = swap(vol_far, "mp", 2)
    tokens_grad = finish(rows2d, vecs, own, got, second, dmid)
    for bit in reversed(late_bits()):
        last = finish_gather(last, bit)
    whole = (whole + second[share : share + 8].astype(F32))[: VECTORS + 1]
    lines = jnp.concatenate([whole, bias_sums[0:1], bias_sums[2:3], norm_sums[0:1]], axis=0)
    lines = lines + swap(lines, "dp", 1)
    (down_total,) = spread(
        "spread_one",
        [(0, sizes[0], "xz", 0), (third, sizes[1], "xz", 1), (2 * third, sizes[2], "zx", 1)],
        [width],
        [],
        first,
        [near_got[0], far_got[0], near_got[1], far_got[1]],
    )
    last, lines, down_total, tokens_grad = join(last, lines, down_total, tokens_grad)
    edge = sum(last_sizes[:3])
    sent_last = [last[:edge], last[edge:]]
    last_got = [swap(sent_last[0], "dp", 2), swap(sent_last[1], "dp", 1)]
    lines = lines + swap(lines, "dp", 2)
    for bit in late_bits():
        lines = lines + swap(lines, "dp", bit)
    last_far = [
        swap(jnp.concatenate([sent_last[0], last_got[0]], axis=0), "dp", 1),
        swap(jnp.concatenate([sent_last[1], last_got[1]], axis=0), "dp", 2),
    ]
    base = width + hw
    up_cut = width * 5 // 12
    up_total, out_total, query_total, key_total, value_total, conv_total = spread(
        "spread_two",
        [
            (0, last_sizes[0], "xz", 0),
            (up_cut, last_sizes[1], "xz", 0),
            (base, last_sizes[2], "xz", 0),
            (2 * up_cut, last_sizes[3], "zx", 1),
            (width, last_sizes[4], "zx", 1),
            (base + cut, last_sizes[5], "zx", 1),
            (base + 3 * hw, last_sizes[6], "xz", 1),
            (base + 3 * hw + half, last_sizes[7], "zx", 1),
        ],
        [width, hw, hw, hw, hw, block],
        [5],
        last,
        [last_got[0], last_far[0], last_got[1], last_far[1]],
    )
    volume = put_half(vol_near, vol_got, chip).astype(F32)
    return (
        volume.reshape(items, seq, -1),
        tokens_grad,
        lines[0],
        lines[1],
        query_total.T,
        lines[VECTORS + 1, :hw],
        key_total.T,
        value_total.T,
        lines[VECTORS + 2, :hw],
        out_total,
        lines[4],
        lines[2],
        lines[3],
        up_total,
        lines[VECTORS],
        down_total,
        lines[5],
        conv_total,
        lines[VECTORS + 3, :CH],
        lines[VECTORS + 3, CH : 2 * CH],
    )


def solution(mesh):
    in_specs = (
        P("dp", None, None),
        P("dp"),
        P(),
        P(),
        P(None, "mp"),
        P("mp"),
        P(None, "mp"),
        P(None, "mp"),
        P("mp"),
        P("mp", None),
        P(),
        P(),
        P(),
        P(None, "mp"),
        P("mp"),
        P("mp", None),
        P(),
        P(None, "mp"),
        P(),
        P(),
        P("dp", None, "mp"),
    )
    out_specs = (
        P("dp", None, "mp"),
        P(("dp", "mp"), None),
        P(),
        P(),
        P(None, "mp"),
        P("mp"),
        P(None, "mp"),
        P(None, "mp"),
        P("mp"),
        P("mp", None),
        P(),
        P(),
        P(),
        P(None, "mp"),
        P("mp"),
        P("mp", None),
        P(),
        P(None, "mp"),
        P(),
        P(),
    )
    return jax.shard_map(shards, mesh=mesh, in_specs=in_specs, out_specs=out_specs, check_vma=False)
```

profile of v0, /device:TPU:0, one launch (start us, length us, event | category | flops | bytes accessed | tf_op | source)
XLA Modules:
  0.0 251.3 jit_solution(1153373885773190853)
XLA Ops:
  3.2 3.0 %collective-permute-start = (bf16[208,768]{1,0:T(8,128)(2,1)}, bf16[208,768]{1,0:T(8,128)(2,1)S(1)}, u32[]{:S(2)}, u32[]{:S(2)}) collective-permute-start(bf16[208,768]{1,0:T(8,128)(2,1)} %pad_maximum_fusion.7), channel_id=1, source_target_pairs={{0,2},{1,3},{2,0},{3,1},{4,6},{5,7},{6,4},{7,5},{8,10},{9,11},{10,... | collective-permute-start | bytes 958472 | tf_op jit(solution)/shard_map/ppermute | solution.py:39
  13.8 10.8 %attend.1 = (bf16[1536,768]{1,0:T(8,128)(2,1)}, bf16[1536,192]{1,0:T(8,128)(2,1)}, bf16[1536,192]{1,0:T(8,128)(2,1)}, bf16[1536,192]{1,0:T(8,128)(2,1)}, f32[3,8...) custom-call(s32[3]{0:T(128)S(1)} %copy-done.4, bf16[1536,768]{1,0:T(8,128)(2,1)} %bitcast.21, ...), custom_call_target="tpu_custom_call" | custom-call | flops 1962934272 | bytes 4718592 | tf_op jit(solution)/shard_map/attend/pallas_call | solution.py:171
  24.5 4.2 %collective-permute-done.1.rest_0_ = bf16[192,768]{1,0:T(8,128)(2,1)} collective-permute-done((bf16[192,768]{1,0:T(8,128)(2,1)}, bf16[192,768]{1,0:T(8,128)(2,1)}, u32[]{:S(2)}, u32[]{:S(2)}) %collective-permute-start.1) | collective-permute-done | bytes 294944 | tf_op jit(solution)/shard_map/ppermute | solution.py:39
  33.7 3.5 %collective-permute-done.5.rest_2_ = bf16[192,768]{1,0:T(8,128)(2,1)S(1)} collective-permute-done((bf16[192,768]{1,0:T(8,128)(2,1)}, bf16[192,768]{1,0:T(8,128)(2,1)S(1)}, u32[]{:S(2)}, u32[]{:S(2)}) %collective-permute-start.5) | collective-permute-done | bytes 294944 | tf_op jit(solution)/shard_map/ppermute | solution.py:39
  38.5 3.0 %collective-permute-done.3.far_ref.refs_1_ = bf16[768,192]{1,0:T(8,128)(2,1)S(1)} collective-permute-done((bf16[768,192]{1,0:T(8,128)(2,1)S(1)}, bf16[768,192]{1,0:T(8,128)(2,1)S(1)}, u32[]{:S(2)}, u32[]{:S(2)}) %collective-permute-start.3) | collective-permute-done | bytes 294944 | tf_op jit(solution)/shard_map/ppermute | solution.py:39
  46.9 3.7 %collective-permute-done.7.rest_3_ = bf16[96,768]{1,0:T(8,128)(2,1)S(1)} collective-permute-done((bf16[96,768]{1,0:T(8,128)(2,1)S(1)}, bf16[96,768]{1,0:T(8,128)(2,1)S(1)}, u32[]{:S(2)}, u32[]{:S(2)}) %collective-permute-start.7) | collective-permute-done | bytes 147488 | tf_op jit(solution)/shard_map/ppermute | solution.py:39
  54.3 7.6 %expand.1 = (f32[768,768]{1,0:T(8,128)S(1)}, bf16[768,768]{1,0:T(8,128)(2,1)S(1)}, bf16[2,768,768]{2,1,0:T(8,128)(2,1)S(1)}, bf16[2,768,768]{2,1,0:T(8,128)(2,1)S(1)}) custom-call(bf16[1536,768]{1,0:T(8,128)(2,1)} %bitcast.22, f32[8,768]{1,0:T(8,128)} %reshape.57.vec_ref.norm_ref, bf16[768,768]{1,0:T(8,128)(2,1)S(1)} %project.1.part_ref, ...), custom_call_target="tpu_custom_call" | custom-call | flops 1811939328 | bytes 8257536 | tf_op jit(solution)/shard_map/expand/pallas_call | solution.py:442
  63.0 3.6 %contract.1.part_ref = bf16[768,768]{1,0:T(8,128)(2,1)S(1)} custom-call(bf16[2,768,768]{2,1,0:T(8,128)(2,1)S(1)} %get-tuple-element.217.act_ref.refs_0_, bf16[768,768]{1,0:T(8,128)(2,1)} %down_ref.3, bf16[256,768]{1,0:T(8,128)(2,1)} %copy-done.11, bf16[256,768]{1,0:T(8,128)(2,1)} %copy-done.14, bf16[256,768]{1,0:T(8,128)(2,1)} %copy-done.13, ...), custom_call_target="tpu_custom_call" | custom-call | flops 1811939328 | bytes 4718592 | tf_op jit(solution)/shard_map/contract/pallas_call | solution.py:472
  66.7 2.8 %collective-permute-done.13.other_ref = bf16[768,768]{1,0:T(8,128)(2,1)S(1)} collective-permute-done((bf16[768,768]{1,0:T(8,128)(2,1)S(1)}, bf16[768,768]{1,0:T(8,128)(2,1)S(1)}, u32[]{:S(2)}, u32[]{:S(2)}) %collective-permute-start.13) | collective-permute-done | bytes 1179680 | tf_op jit(solution)/shard_map/ppermute | solution.py:39
  69.6 4.7 %convolve.1 = (bf16[768,768]{1,0:T(8,128)(2,1)S(1)}, f32[2,768,256]{2,1,0:T(8,128)S(1)}, f32[3,4,128]{2,1,0:T(4,128)S(1)}) custom-call(s32[3]{0:T(128)S(1)} %copy-done.4, f32[8,768]{1,0:T(8,128)} %reshape.57.vec_ref.norm_ref, f32[768,768]{1,0:T(8,128)S(1)} %get-tuple-element.218.mid_ref, bf16[768,768]{1,0:T(8,128)(2,1)S(1)} %contract.1.part_ref, ...), custom_call_target="tpu_custom_call" | custom-call | flops 603979776 | bytes 8257536 | tf_op jit(solution)/shard_map/convolve/pallas_call | solution.py:524
  76.4 2.8 %collective-permute-done.15.got_ref = f32[3,4,128]{2,1,0:T(4,128)S(1)} collective-permute-done((f32[3,4,128]{2,1,0:T(4,128)S(1)}, f32[3,4,128]{2,1,0:T(4,128)S(1)}, u32[]{:S(2)}, u32[]{:S(2)}) %collective-permute-start.15) | collective-permute-done | bytes 6176 | tf_op jit(solution)/shard_map/ppermute | solution.py:39
  79.1 3.9 %norm_back.1 = (bf16[768,256]{1,0:T(8,128)(2,1)S(1)}, bf16[768,256]{1,0:T(8,128)(2,1)S(1)}, bf16[2,768,256]{2,1,0:T(8,128)(2,1)S(1)}, bf16[768,768]{1,0:T(8,128)(2,1)S(1)}, f32[8,768]{1,0:T(8,128)S(1)}) custom-call(s32[3]{0:T(128)S(1)} %copy-done.4, f32[8,768]{1,0:T(8,128)} %reshape.57.vec_ref.norm_ref, f32[3,4,128]{2,1,0:T(4,128)S(1)} %add.76.tot_ref, ...), custom_call_target="tpu_custom_call" | custom-call | flops 603979776 | bytes 3538944 | tf_op jit(solution)/shard_map/norm_back/pallas_call | solution.py:584
  86.3 2.4 down_grad.1
  92.5 6.6 %mlp_back.1 = (bf16[2,768,768]{2,1,0:T(8,128)(2,1)S(1)}, bf16[768,768]{1,0:T(8,128)(2,1)S(1)}, f32[8,768]{1,0:T(8,128)S(1)}, f32[2,8,768]{2,1,0:T(8,128)S(1)}) custom-call(bf16[768,768]{1,0:T(8,128)(2,1)S(1)} %get-tuple-element.228.part_ref, bf16[768,768]{1,0:T(8,128)(2,1)S(1)} %collective-permute-done.16.other_ref, ...), custom_call_target="tpu_custom_call" | custom-call | flops 3623878656 | bytes 11796480 | tf_op jit(solution)/shard_map/mlp_back/pallas_call | solution.py:637
  101.6 2.0 up_grad.1.refs_8_.refs_9_.refs_10_
  107.8 4.5 %mid_back.1 = (bf16[768,192]{1,0:T(8,128)(2,1)S(1)}, bf16[768,192]{1,0:T(8,128)(2,1)S(1)}, bf16[768,768]{1,0:T(8,128)(2,1)S(1)}, f32[384,768]{1,0:T(8,128)S(1)}, f32[8,768]{1,0:T(8,128)S(1)}) custom-call(f32[8,768]{1,0:T(8,128)} %reshape.57.vec_ref.norm_ref, f32[768,768]{1,0:T(8,128)S(1)} %get-tuple-element.218.mid_ref, ...), custom_call_target="tpu_custom_call" | custom-call | flops 452984832 | bytes 7077888 | tf_op jit(solution)/shard_map/mid_back/pallas_call | solution.py:682
  116.8 5.9 %collective-permute-done.22.other_ref = bf16[768,192]{1,0:T(8,128)(2,1)S(1)} collective-permute-done((bf16[768,192]{1,0:T(8,128)(2,1)S(1)}, bf16[768,192]{1,0:T(8,128)(2,1)S(1)}, u32[]{:S(2)}, u32[]{:S(2)}) %collective-permute-start.22) | collective-permute-done | bytes 294944 | tf_op jit(solution)/shard_map/ppermute | solution.py:39
  127.5 11.3 %attend_back.1 = (bf16[1536,192]{1,0:T(8,128)(2,1)}, bf16[1536,192]{1,0:T(8,128)(2,1)}, bf16[1536,192]{1,0:T(8,128)(2,1)}, bf16[576,768]{1,0:T(8,128)(2,1)S(1)}, f32[8,768]{1,0:T(8,128)S(1)}) custom-call(s32[3]{0:T(128)S(1)} %copy-done.4, bf16[1536,768]{1,0:T(8,128)(2,1)} %get-tuple-element.282.normed_ref, bf16[1536,192]{1,0:T(8,128)(2,1)} %get-tuple-element.283.q_ref, ...), custom_call_target="tpu_custom_call" | custom-call | flops 2868903936 | bytes 9437184 | tf_op jit(solution)/shard_map/attend_back/pallas_call | solution.py:251
  140.9 2.9 %turn_three.1 = (bf16[224,768]{1,0:T(8,128)(2,1)S(1)}, bf16[288,768]{1,0:T(8,128)(2,1)}, bf16[320,768]{1,0:T(8,128)(2,1)S(1)}, bf16[32,768]{1,0:T(8,128)(2,1)}, ...) custom-call(bf16[64,768]{1,0:T(8,128)(2,1)} %get-tuple-element.273.r, ...), custom_call_target="tpu_custom_call" | custom-call | tf_op jit(solution)/shard_map/turn_three/pallas_call | solution.py:812
  146.5 2.7 %collective-permute-start.28 = (bf16[96,768]{1,0:T(8,128)(2,1)S(1)}, bf16[96,768]{1,0:T(8,128)(2,1)S(1)}, u32[]{:S(2)}, u32[]{:S(2)}) collective-permute-start(bf16[96,768]{1,0:T(8,128)(2,1)S(1)} %constant_dynamic-slice_fusion), channel_id=1, source_target_pairs={{0,16},{4,20},{8,24},{12,28},{16,0},{20,4},{24,8},{28,12},{1,17},{... | collective-permute-start | bytes 442376 | tf_op jit(solution)/shard_map/ppermute | solution.py:39
  149.9 8.0 %normed_back.1 = (bf16[784,768]{1,0:T(8,128)(2,1)}, f32[384,768]{1,0:T(8,128)}, f32[384,768]{1,0:T(8,128)}, f32[8,768]{1,0:T(8,128)S(1)}) custom-call(s32[3]{0:T(128)S(1)} %copy-done.4, bf16[1536,768]{1,0:T(8,128)(2,1)} %bitcast.23, bf16[1536,192]{1,0:T(8,128)(2,1)} %get-tuple-element.314.dq_ref, bf16[1536,192]{1,0:T(8,128)(2,1)} %get-tuple-element.315.dk_ref, ...), custom_call_target="tpu_custom_call" | custom-call | flops 1358954496 | bytes 9437184 | tf_op jit(solution)/shard_map/normed_back/pallas_call | solution.py:329
  159.2 2.3 collective-permute-start.32
  161.5 2.1 turn_four.1
  176.4 3.5 %collective-permute-start.37 = (bf16[224,768]{1,0:T(8,128)(2,1)S(1)}, bf16[224,768]{1,0:T(8,128)(2,1)S(1)}, u32[]{:S(2)}, u32[]{:S(2)}) collective-permute-start(bf16[224,768]{1,0:T(8,128)(2,1)S(1)} %fusion), channel_id=1, source_target_pairs={{0,16},{4,20},{8,24},{12,28},{16,0},{20,4},{24,8},{28,12},{1,17},{... | collective-permute-start | bytes 1032200 | tf_op jit(solution)/shard_map/ppermute | solution.py:39
  185.1 10.0 %collective-permute-done.37 = bf16[224,768]{1,0:T(8,128)(2,1)S(1)} collective-permute-done((bf16[224,768]{1,0:T(8,128)(2,1)S(1)}, bf16[224,768]{1,0:T(8,128)(2,1)S(1)}, u32[]{:S(2)}, u32[]{:S(2)}) %collective-permute-start.37) | collective-permute-done | bytes 344096 | tf_op jit(solution)/shard_map/ppermute | solution.py:39
  195.3 4.3 %collective-permute-done.42.refs_4_ = bf16[256,768]{1,0:T(8,128)(2,1)S(1)} collective-permute-done((bf16[256,768]{1,0:T(8,128)(2,1)S(1)}, bf16[256,768]{1,0:T(8,128)(2,1)S(1)}, u32[]{:S(2)}, u32[]{:S(2)}) %collective-permute-start.42) | collective-permute-done | bytes 393248 | tf_op jit(solution)/shard_map/ppermute | solution.py:39
  202.8 4.8 %finish.1 = f32[384,768]{1,0:T(8,128)} custom-call(bf16[1536,768]{1,0:T(8,128)(2,1)} %bitcast.24, f32[8,768]{1,0:T(8,128)} %reshape.57.vec_ref.norm_ref, f32[384,768]{1,0:T(8,128)} %get-tuple-element.358.own_ref, bf16[784,768]{1,0:T(8,128)(2,1)S(1)} %collective-permute-done.33.got_ref, bf16[392,768]{1,0:T(8,128)(2,1)S(1)} %collective-permute-done.38.last_ref, ...), custom_call_target="tpu_custom_call" | custom-call | bytes 4128768 | tf_op jit(solution)/shard_map/finish/pallas_call | solution.py:923
  209.5 6.5 %collective-permute-done.44 = bf16[224,768]{1,0:T(8,128)(2,1)S(1)} collective-permute-done((bf16[224,768]{1,0:T(8,128)(2,1)S(1)}, bf16[224,768]{1,0:T(8,128)(2,1)S(1)}, u32[]{:S(2)}, u32[]{:S(2)}) %collective-permute-start.44) | collective-permute-done | bytes 344096 | tf_op jit(solution)/shard_map/ppermute | solution.py:39
  216.8 2.0 collective-permute-start.46
  219.6 7.9 %collective-permute-done.46 = f32[10,768]{1,0:T(8,128)S(1)} collective-permute-done((f32[10,768]{1,0:T(8,128)S(1)}, f32[10,768]{1,0:T(8,128)S(1)}, u32[]{:S(2)}, u32[]{:S(2)}) %collective-permute-start.46) | collective-permute-done | bytes 30752 | tf_op jit(solution)/shard_map/ppermute | solution.py:39
  236.9 10.8 %collective-permute-done.49.refs_2_ = bf16[448,768]{1,0:T(8,128)(2,1)S(1)} collective-permute-done((bf16[448,768]{1,0:T(8,128)(2,1)S(1)}, bf16[448,768]{1,0:T(8,128)(2,1)S(1)}, u32[]{:S(2)}, u32[]{:S(2)}) %collective-permute-start.49) | collective-permute-done | bytes 688160 | tf_op jit(solution)/shard_map/ppermute | solution.py:39
  248.3 3.0 %spread_two.1 = (f32[768,768]{1,0:T(8,128)}, f32[192,768]{1,0:T(8,128)}, f32[192,768]{1,0:T(8,128)}, f32[192,768]{1,0:T(8,128)}, f32[192,768]{1,0:T(8,128)}, /*index=5*/f32[768,256]{1,0:T(8,128)}) custom-call(bf16[448,768]{1,0:T(8,128)(2,1)S(1)} %pad_maximum_fusion.1.refs_0_, bf16[224,768]{1,0:T(8,128)(2,1)S(1)} %collective-permute-done.48.refs_1_, ...), custom_call_target="tpu_custom_call" | custom-call | bytes 11010048 | tf_op jit(solution)/shard_map/spread_two/pallas_call | solution.py:875
  (218 shorter events, 92.7 us)
Async XLA Ops:
  3.2 25.6 %collective-permute-start = (bf16[208,768]{1,0:T(8,128)(2,1)}, bf16[208,768]{1,0:T(8,128)(2,1)S(1)}, u32[]{:S(2)}, u32[]{:S(2)}) collective-permute-start(bf16[208,768]{1,0:T(8,128)(2,1)} %pad_maximum_fusion.7), channel_id=1, source_target_pairs={{0,2},{1,3},{2,0},{3,1},{4,6},{5,7},{6,4},{7,5},{8,10},{9,11},{10,... | collective-permute-start | bytes 958472 | tf_op jit(solution)/shard_map/ppermute | solution.py:39
  7.6 21.1 %collective-permute-start.2 = (bf16[256,768]{1,0:T(8,128)(2,1)S(1)}, bf16[256,768]{1,0:T(8,128)(2,1)S(1)}, u32[]{:S(2)}, u32[]{:S(2)}) collective-permute-start(bf16[256,768]{1,0:T(8,128)(2,1)S(1)} %pad_maximum_fusion.4), channel_id=1, source_target_pairs={{0,2},{1,3},{2,0},{3,1},{4,6},{5,7},{6,4},{7,5},{8,10},{9,11},{10,... | collective-permute-start | bytes 1179656 | tf_op jit(solution)/shard_map/ppermute | solution.py:39
  9.4 19.3 %collective-permute-start.1 = (bf16[192,768]{1,0:T(8,128)(2,1)}, bf16[192,768]{1,0:T(8,128)(2,1)}, u32[]{:S(2)}, u32[]{:S(2)}) collective-permute-start(bf16[192,768]{1,0:T(8,128)(2,1)} %constant_dynamic-slice_fusion.4), channel_id=1, source_target_pairs={{0,2},{1,3},{2,0},{3,1},{4,6},{5,7},{6,4},{7,5},{8,10},{9,11},{10,... | collective-permute-start | bytes 884744 | tf_op jit(solution)/shard_map/ppermute | solution.py:39
  45.4 16.5 %collective-permute-start.9 = (bf16[256,768]{1,0:T(8,128)(2,1)S(1)}, bf16[256,768]{1,0:T(8,128)(2,1)S(1)}, u32[]{:S(2)}, u32[]{:S(2)}) collective-permute-start(bf16[256,768]{1,0:T(8,128)(2,1)S(1)} %pad_maximum_fusion.5), channel_id=1, source_target_pairs={{0,2},{1,3},{2,0},{3,1},{4,6},{5,7},{6,4},{7,5},{8,10},{9,11},{10,... | collective-permute-start | bytes 1179656 | tf_op jit(solution)/shard_map/ppermute | solution.py:39
  50.9 11.1 %collective-permute-start.11 = (bf16[256,768]{1,0:T(8,128)(2,1)S(1)}, bf16[256,768]{1,0:T(8,128)(2,1)S(1)}, u32[]{:S(2)}, u32[]{:S(2)}) collective-permute-start(bf16[256,768]{1,0:T(8,128)(2,1)S(1)} %collective-permute-done.2.rest_0_.rest_5_), channel_id=1, source_target_pairs={{0,8},{4,12},{8,0},{12,4},{16,24},{20,28},{24,16},{28,20},{1,9},{5... | collective-permute-start | bytes 1179656 | tf_op jit(solution)/shard_map/ppermute | solution.py:39
  51.4 10.6 %collective-permute-start.10 = (bf16[256,768]{1,0:T(8,128)(2,1)S(1)}, bf16[256,768]{1,0:T(8,128)(2,1)S(1)}, u32[]{:S(2)}, u32[]{:S(2)}) collective-permute-start(bf16[256,768]{1,0:T(8,128)(2,1)S(1)} %collective-permute-done.2.rest_0_.rest_5_), channel_id=1, source_target_pairs={{0,4},{4,0},{8,12},{12,8},{16,20},{20,16},{24,28},{28,24},{1,5},{5... | collective-permute-start | bytes 1179656 | tf_op jit(solution)/shard_map/ppermute | solution.py:39
  52.8 13.8 %collective-permute-start.12 = (bf16[768,256]{1,0:T(8,128)(2,1)S(1)}, bf16[768,256]{1,0:T(8,128)(2,1)S(1)}, u32[]{:S(2)}, u32[]{:S(2)}) collective-permute-start(bf16[768,256]{1,0:T(8,128)(2,1)S(1)} %constant_dynamic-slice_fusion.1), channel_id=1, source_target_pairs={{0,2},{1,3},{2,0},{3,1},{4,6},{5,7},{6,4},{7,5},{8,10},{9,11},{10,... | collective-permute-start | bytes 1179656 | tf_op jit(solution)/shard_map/ppermute | solution.py:39
  88.7 11.2 %collective-permute-start.17 = (bf16[256,768]{1,0:T(8,128)(2,1)S(1)}, bf16[256,768]{1,0:T(8,128)(2,1)S(1)}, u32[]{:S(2)}, u32[]{:S(2)}) collective-permute-start(bf16[256,768]{1,0:T(8,128)(2,1)S(1)} %get-tuple-element.241), channel_id=1, source_target_pairs={{0,2},{1,3},{2,0},{3,1},{4,6},{5,7},{6,4},{7,5},{8,10},{9,11},{10,... | collective-permute-start | bytes 1179656 | tf_op jit(solution)/shard_map/ppermute | solution.py:39
  89.6 10.9 %collective-permute-start.18 = (bf16[256,768]{1,0:T(8,128)(2,1)S(1)}, bf16[256,768]{1,0:T(8,128)(2,1)S(1)}, u32[]{:S(2)}, u32[]{:S(2)}) collective-permute-start(bf16[256,768]{1,0:T(8,128)(2,1)S(1)} %get-tuple-element.242), channel_id=1, source_target_pairs={{0,4},{4,0},{8,12},{12,8},{16,20},{20,16},{24,28},{28,24},{1,5},{5... | collective-permute-start | bytes 1179656 | tf_op jit(solution)/shard_map/ppermute | solution.py:39
  91.0 10.6 %collective-permute-start.19 = (bf16[256,768]{1,0:T(8,128)(2,1)S(1)}, bf16[256,768]{1,0:T(8,128)(2,1)S(1)}, u32[]{:S(2)}, u32[]{:S(2)}) collective-permute-start(bf16[256,768]{1,0:T(8,128)(2,1)S(1)} %get-tuple-element.243), channel_id=1, source_target_pairs={{0,8},{4,12},{8,0},{12,4},{16,24},{20,28},{24,16},{28,20},{1,9},{5... | collective-permute-start | bytes 1179656 | tf_op jit(solution)/shard_map/ppermute | solution.py:39
  104.9 10.9 %collective-permute-start.23 = (bf16[256,768]{1,0:T(8,128)(2,1)S(1)}, bf16[256,768]{1,0:T(8,128)(2,1)S(1)}, u32[]{:S(2)}, u32[]{:S(2)}) collective-permute-start(bf16[256,768]{1,0:T(8,128)(2,1)S(1)} %get-tuple-element.266), channel_id=1, source_target_pairs={{0,4},{4,0},{8,12},{12,8},{16,20},{20,16},{24,28},{28,24},{1,5},{5... | collective-permute-start | bytes 1179656 | tf_op jit(solution)/shard_map/ppermute | solution.py:39
  106.2 10.6 %collective-permute-start.24 = (bf16[256,768]{1,0:T(8,128)(2,1)S(1)}, bf16[256,768]{1,0:T(8,128)(2,1)S(1)}, u32[]{:S(2)}, u32[]{:S(2)}) collective-permute-start(bf16[256,768]{1,0:T(8,128)(2,1)S(1)} %get-tuple-element.267), channel_id=1, source_target_pairs={{0,8},{4,12},{8,0},{12,4},{16,24},{20,28},{24,16},{28,20},{1,9},{5... | collective-permute-start | bytes 1179656 | tf_op jit(solution)/shard_map/ppermute | solution.py:39
  112.3 10.4 %collective-permute-start.22 = (bf16[768,192]{1,0:T(8,128)(2,1)S(1)}, bf16[768,192]{1,0:T(8,128)(2,1)S(1)}, u32[]{:S(2)}, u32[]{:S(2)}) collective-permute-start(bf16[768,192]{1,0:T(8,128)(2,1)S(1)} %get-tuple-element.263), channel_id=1, source_target_pairs={{0,2},{1,3},{2,0},{3,1},{4,6},{5,7},{6,4},{7,5},{8,10},{9,11},{10,... | collective-permute-start | bytes 884744 | tf_op jit(solution)/shard_map/ppermute | solution.py:39
  124.7 16.0 %collective-permute-start.26 = (bf16[448,768]{1,0:T(8,128)(2,1)}, bf16[448,768]{1,0:T(8,128)(2,1)S(1)}, u32[]{:S(2)}, u32[]{:S(2)}) collective-permute-start(bf16[448,768]{1,0:T(8,128)(2,1)} %get-tuple-element.296), channel_id=1, source_target_pairs={{0,4},{4,0},{8,12},{12,8},{16,20},{20,16},{24,28},{28,24},{1,5},{5... | collective-permute-start | bytes 2064392 | tf_op jit(solution)/shard_map/ppermute | solution.py:39
  125.5 15.4 %collective-permute-start.27 = (bf16[448,768]{1,0:T(8,128)(2,1)S(1)}, bf16[448,768]{1,0:T(8,128)(2,1)S(1)}, u32[]{:S(2)}, u32[]{:S(2)}) collective-permute-start(bf16[448,768]{1,0:T(8,128)(2,1)S(1)} %get-tuple-element.297), channel_id=1, source_target_pairs={{0,8},{4,12},{8,0},{12,4},{16,24},{20,28},{24,16},{28,20},{1,9},{5... | collective-permute-start | bytes 2064392 | tf_op jit(solution)/shard_map/ppermute | solution.py:39
  126.0 13.3 %collective-permute-start.25 = (bf16[384,768]{1,0:T(8,128)(2,1)}, bf16[384,768]{1,0:T(8,128)(2,1)S(1)}, u32[]{:S(2)}, u32[]{:S(2)}) collective-permute-start(bf16[384,768]{1,0:T(8,128)(2,1)} %get-tuple-element.295), channel_id=1, source_target_pairs={{0,2},{1,3},{2,0},{3,1},{4,6},{5,7},{6,4},{7,5},{8,10},{9,11},{10,... | collective-permute-start | bytes 1769480 | tf_op jit(solution)/shard_map/ppermute | solution.py:39
  144.6 13.4 %collective-permute-start.30 = (bf16[288,768]{1,0:T(8,128)(2,1)}, bf16[288,768]{1,0:T(8,128)(2,1)S(1)}, u32[]{:S(2)}, u32[]{:S(2)}) collective-permute-start(bf16[288,768]{1,0:T(8,128)(2,1)} %get-tuple-element.321), channel_id=1, source_target_pairs={{0,4},{4,0},{8,12},{12,8},{16,20},{20,16},{24,28},{28,24},{1,5},{5... | collective-permute-start | bytes 1327112 | tf_op jit(solution)/shard_map/ppermute | solution.py:39
  145.9 13.2 %collective-permute-start.31 = (bf16[320,768]{1,0:T(8,128)(2,1)S(1)}, bf16[320,768]{1,0:T(8,128)(2,1)S(1)}, u32[]{:S(2)}, u32[]{:S(2)}) collective-permute-start(bf16[320,768]{1,0:T(8,128)(2,1)S(1)} %get-tuple-element.322), channel_id=1, source_target_pairs={{0,8},{4,12},{8,0},{12,4},{16,24},{20,28},{24,16},{28,20},{1,9},{5... | collective-permute-start | bytes 1474568 | tf_op jit(solution)/shard_map/ppermute | solution.py:39
  146.5 11.5 %collective-permute-start.28 = (bf16[96,768]{1,0:T(8,128)(2,1)S(1)}, bf16[96,768]{1,0:T(8,128)(2,1)S(1)}, u32[]{:S(2)}, u32[]{:S(2)}) collective-permute-start(bf16[96,768]{1,0:T(8,128)(2,1)S(1)} %constant_dynamic-slice_fusion), channel_id=1, source_target_pairs={{0,16},{4,20},{8,24},{12,28},{16,0},{20,4},{24,8},{28,12},{1,17},{... | collective-permute-start | bytes 442376 | tf_op jit(solution)/shard_map/ppermute | solution.py:39
  159.1 14.5 %collective-permute-start.33 = (bf16[784,768]{1,0:T(8,128)(2,1)}, bf16[784,768]{1,0:T(8,128)(2,1)S(1)}, u32[]{:S(2)}, u32[]{:S(2)}) collective-permute-start(bf16[784,768]{1,0:T(8,128)(2,1)} %get-tuple-element.333), channel_id=1, source_target_pairs={{0,1},{1,0},{2,3},{3,2},{4,5},{5,4},{6,7},{7,6},{8,9},{9,8},{10,11... | collective-permute-start | bytes 3612680 | tf_op jit(solution)/shard_map/ppermute | solution.py:39
  159.2 10.4 %collective-permute-start.32 = (bf16[96,768]{1,0:T(8,128)(2,1)S(1)}, bf16[96,768]{1,0:T(8,128)(2,1)}, u32[]{:S(2)}, u32[]{:S(2)}) collective-permute-start(bf16[96,768]{1,0:T(8,128)(2,1)S(1)} %add_convert_fusion.2), channel_id=1, source_target_pairs={{0,16},{4,20},{8,24},{12,28},{16,0},{20,4},{24,8},{28,12},{1,17},{... | collective-permute-start | bytes 442376 | tf_op jit(solution)/shard_map/ppermute | solution.py:39
  176.4 18.7 %collective-permute-start.37 = (bf16[224,768]{1,0:T(8,128)(2,1)S(1)}, bf16[224,768]{1,0:T(8,128)(2,1)S(1)}, u32[]{:S(2)}, u32[]{:S(2)}) collective-permute-start(bf16[224,768]{1,0:T(8,128)(2,1)S(1)} %fusion), channel_id=1, source_target_pairs={{0,16},{4,20},{8,24},{12,28},{16,0},{20,4},{24,8},{28,12},{1,17},{... | collective-permute-start | bytes 1032200 | tf_op jit(solution)/shard_map/ppermute | solution.py:39
  181.3 18.4 %collective-permute-start.38 = (bf16[392,768]{1,0:T(8,128)(2,1)S(1)}, bf16[392,768]{1,0:T(8,128)(2,1)S(1)}, u32[]{:S(2)}, u32[]{:S(2)}) collective-permute-start(bf16[392,768]{1,0:T(8,128)(2,1)S(1)} %get-tuple-element.346), channel_id=1, source_target_pairs={{0,2},{1,3},{2,0},{3,1},{4,6},{5,7},{6,4},{7,5},{8,10},{9,11},{10,... | collective-permute-start | bytes 1806344 | tf_op jit(solution)/shard_map/ppermute | solution.py:39
  183.7 15.9 %collective-permute-start.42 = (bf16[256,768]{1,0:T(8,128)(2,1)S(1)}, bf16[256,768]{1,0:T(8,128)(2,1)S(1)}, u32[]{:S(2)}, u32[]{:S(2)}) collective-permute-start(bf16[256,768]{1,0:T(8,128)(2,1)S(1)} %pad_maximum_fusion.6), channel_id=1, source_target_pairs={{0,8},{4,12},{8,0},{12,4},{16,24},{20,28},{24,16},{28,20},{1,9},{5... | collective-permute-start | bytes 1179656 | tf_op jit(solution)/shard_map/ppermute | solution.py:39
  183.9 11.5 %collective-permute-start.40 = (bf16[128,768]{1,0:T(8,128)(2,1)S(1)}, bf16[128,768]{1,0:T(8,128)(2,1)S(1)}, u32[]{:S(2)}, u32[]{:S(2)}) collective-permute-start(bf16[128,768]{1,0:T(8,128)(2,1)S(1)} %pad_maximum_fusion.9), channel_id=1, source_target_pairs={{0,4},{4,0},{8,12},{12,8},{16,20},{20,16},{24,28},{28,24},{1,5},{5... | collective-permute-start | bytes 589832 | tf_op jit(solution)/shard_map/ppermute | solution.py:39
  199.7 16.3 %collective-permute-start.44 = (bf16[224,768]{1,0:T(8,128)(2,1)S(1)}, bf16[224,768]{1,0:T(8,128)(2,1)S(1)}, u32[]{:S(2)}, u32[]{:S(2)}) collective-permute-start(bf16[224,768]{1,0:T(8,128)(2,1)S(1)} %add_convert_fusion.1), channel_id=1, source_target_pairs={{0,16},{4,20},{8,24},{12,28},{16,0},{20,4},{24,8},{28,12},{1,17},{... | collective-permute-start | bytes 1032200 | tf_op jit(solution)/shard_map/ppermute | solution.py:39
  201.5 27.5 %collective-permute-start.43 = (bf16[768,256]{1,0:T(8,128)(2,1)S(1)}, bf16[768,256]{1,0:T(8,128)(2,1)}, u32[]{:S(2)}, u32[]{:S(2)}) collective-permute-start(bf16[768,256]{1,0:T(8,128)(2,1)S(1)} %copy-done.6), channel_id=1, source_target_pairs={{0,2},{1,3},{2,0},{3,1},{4,6},{5,7},{6,4},{7,5},{8,10},{9,11},{10,... | collective-permute-start | bytes 1179656 | tf_op jit(solution)/shard_map/ppermute | solution.py:39
  216.8 13.2 %collective-permute-start.48 = (bf16[224,768]{1,0:T(8,128)(2,1)}, bf16[224,768]{1,0:T(8,128)(2,1)S(1)}, u32[]{:S(2)}, u32[]{:S(2)}) collective-permute-start(bf16[224,768]{1,0:T(8,128)(2,1)} %get-tuple-element.382), channel_id=1, source_target_pairs={{0,8},{4,12},{8,0},{12,4},{16,24},{20,28},{24,16},{28,20},{1,9},{5... | collective-permute-start | bytes 1032200 | tf_op jit(solution)/shard_map/ppermute | solution.py:39
  216.8 10.7 %collective-permute-start.46 = (f32[10,768]{1,0:T(8,128)S(1)}, f32[10,768]{1,0:T(8,128)S(1)}, u32[]{:S(2)}, u32[]{:S(2)}) collective-permute-start(f32[10,768]{1,0:T(8,128)S(1)} %fusion.9), channel_id=1, source_target_pairs={{0,8},{4,12},{8,0},{12,4},{16,24},{20,28},{24,16},{28,20},{1,9},{5... | collective-permute-start | bytes 92168 | tf_op jit(solution)/shard_map/ppermute | solution.py:39
  218.8 13.1 %collective-permute-start.50 = (bf16[224,768]{1,0:T(8,128)(2,1)S(1)}, bf16[224,768]{1,0:T(8,128)(2,1)S(1)}, u32[]{:S(2)}, u32[]{:S(2)}) collective-permute-start(bf16[224,768]{1,0:T(8,128)(2,1)S(1)} %get-tuple-element.381), channel_id=1, source_target_pairs={{0,4},{4,0},{8,12},{12,8},{16,20},{20,16},{24,28},{28,24},{1,5},{5... | collective-permute-start | bytes 1032200 | tf_op jit(solution)/shard_map/ppermute | solution.py:39
  231.1 16.6 %collective-permute-start.49 = (bf16[448,768]{1,0:T(8,128)(2,1)S(1)}, bf16[448,768]{1,0:T(8,128)(2,1)S(1)}, u32[]{:S(2)}, u32[]{:S(2)}) collective-permute-start(bf16[448,768]{1,0:T(8,128)(2,1)S(1)} %pad_maximum_fusion.2), channel_id=1, source_target_pairs={{0,4},{4,0},{8,12},{12,8},{16,20},{20,16},{24,28},{28,24},{1,5},{5... | collective-permute-start | bytes 2064392 | tf_op jit(solution)/shard_map/ppermute | solution.py:39
  232.0 16.3 %collective-permute-start.51 = (bf16[448,768]{1,0:T(8,128)(2,1)S(1)}, bf16[448,768]{1,0:T(8,128)(2,1)S(1)}, u32[]{:S(2)}, u32[]{:S(2)}) collective-permute-start(bf16[448,768]{1,0:T(8,128)(2,1)S(1)} %pad_maximum_fusion.3), channel_id=1, source_target_pairs={{0,8},{4,12},{8,0},{12,4},{16,24},{20,28},{24,16},{28,20},{1,9},{5... | collective-permute-start | bytes 2064392 | tf_op jit(solution)/shard_map/ppermute | solution.py:39
  (55 other events, 346.3 us)
where the time goes:
time: 252 us; the launch traced here: 251 us
  Pallas kernels  87 us (35%)
  waiting for transfers between devices  84.6 us (34%)
  starting transfers between devices  58.2 us (23%)
  local copies, waits for them, and re-layouts  12 us (5%)
  other arithmetic  8.17 us (3%)
    ppermute x52, waiting for transfers between devices, swap(): return lax.ppermute(value, axis, [(i, i ^ bit) for i in range(size)])  84.6 us
    ppermute x52, starting transfers between devices, swap(): return lax.ppermute(value, axis, [(i, i ^ bit) for i in range(size)])  58.2 us
    pallas_call x1, Pallas kernels, attend_back(): pl.pallas_call(functools.partial(attend_back_kernel, items, heads, share)...  11.3 us
    pallas_call x1, Pallas kernels, attend(): pl.pallas_call(functools.partial(attend_kernel, items, heads, rows // 2),...  10.8 us
    pallas_call x6, Pallas kernels, emit(): pl.pallas_call(functools.partial(emit_kernel, len(lefts), len(inputs), la...  9.81 us
    pallas_call x1, Pallas kernels, normed_back(): pl.pallas_call(functools.partial(normed_back_kernel, items, share), out_s...  8.03 us
    pallas_call x1, Pallas kernels, expand(): pl.pallas_call(expand_kernel, out_shape=[shape((span, width), F32), shape...  7.63 us
    pallas_call x1, Pallas kernels, mlp_back(): pl.pallas_call(mlp_back_kernel, out_shape=[shape((2, span, width), BF16),...  6.58 us
  transfers between devices with their start and end apart: 52, of which 30 were waited for; matrix products, arithmetic and copies ran while one was open for 6% of the time, Pallas kernels for 26%

commit v1 on v0

--- a/solution.py
+++ b/solution.py
@@ -1052,7 +1052,7 @@
     do_far, em, came["y"] = join(do_far, em, came["y"])
     do_got = swap(do_far, "mp", 2)
     out_raw = products("out_grad", [near, far], em)
-    do_got, out_raw, came["y"], came["x"], came["z"] = join(do_got, out_raw, came["y"], came["x"], came["z"])
+    out_raw, came["y"], came["x"], came["z"] = join(out_raw, came["y"], came["x"], came["z"])
     cut = width * 5 // 12
     fresh = [(up_raw, 0, width, 2, cut), (up_raw, cut, width, 2, cut), (up_raw, 2 * cut, width, 2, width - 2 * cut)]
     fresh.append((out_raw, 0, hw, 2, hw))
@@ -1090,7 +1090,7 @@
     last = jnp.concatenate([last, early], axis=0)
     for bit in late_bits():
         last = finish_reduce(last, bit)
-    edge = sizes[0]
+    edge = sizes[0] + sizes[1]
     sent_near = [first[:edge], first[edge:]]
     near_got = [swap(sent_near[0], "dp", 2), swap(sent_near[1], "dp", 1)]
     second, whole = pass_on(passed, got, own_sums, up_sums)
@@ -1106,10 +1106,11 @@
         last = finish_gather(last, bit)
     whole = (whole + second[share : share + 8].astype(F32))[: VECTORS + 1]
     lines = jnp.concatenate([whole, bias_sums[0:1], bias_sums[2:3], norm_sums[0:1]], axis=0)
-    lines = lines + swap(lines, "dp", 1)
+    for bit in [1, 2] + late_bits():
+        lines = lines + swap(lines, "dp", bit)
     (down_total,) = spread(
         "spread_one",
-        [(0, sizes[0], "xz", 0), (third, sizes[1], "xz", 1), (2 * third, sizes[2], "zx", 1)],
+        [(0, sizes[0], "xz", 0), (third, sizes[1], "xz", 0), (2 * third, sizes[2], "zx", 1)],
         [width],
         [],
         first,
@@ -1119,9 +1120,8 @@
     edge = sum(last_sizes[:3])
     sent_last = [last[:edge], last[edge:]]
     last_got = [swap(sent_last[0], "dp", 2), swap(sent_last[1], "dp", 1)]
-    lines = lines + swap(lines, "dp", 2)
-    for bit in late_bits():
-        lines = lines + swap(lines, "dp", bit)
+    volume = put_half(vol_near, vol_got, chip).astype(F32)
+    volume, *last_got = join(volume, *last_got)
     last_far = [
         swap(jnp.concatenate([sent_last[0], last_got[0]], axis=0), "dp", 1),
         swap(jnp.concatenate([sent_last[1], last_got[1]], axis=0), "dp", 2),
@@ -1145,7 +1145,6 @@
         last,
         [last_got[0], last_far[0], last_got[1], last_far[1]],
     )
-    volume = put_half(vol_near, vol_got, chip).astype(F32)
     return (
         volume.reshape(items, seq, -1),
         tokens_grad,

time: 252 us -> 246 us (0.976)
  waiting for transfers between devices: 84.6 us -> 75.4 us
  starting transfers between devices: 58.2 us -> 61 us
    ppermute x52, waiting for transfers between devices: 84.6 us -> 75.4 us  [swap(): return lax.ppermute(value, axis, [(i, i ^ bit) for i in range(size)])]
    ppermute x52, starting transfers between devices: 58.2 us -> 61 us  [swap(): return lax.ppermute(value, axis, [(i, i ^ bit) for i in range(size)])]
  transfers between devices with their start and end apart: 52 -> 52, of which waited for: 30 -> 31; matrix products, arithmetic and copies ran while one was open for 6% -> 6% of each run, Pallas kernels for 26% -> 28%
where the time goes in v1:
time: 246 us; the launch traced here: 245 us
  Pallas kernels  87.2 us (35%)
  waiting for transfers between devices  75.4 us (31%)
  starting transfers between devices  61 us (25%)
  local copies, waits for them, and re-layouts  12.1 us (5%)
  other arithmetic  7.98 us (3%)
    ppermute x52, waiting for transfers between devices, swap(): return lax.ppermute(value, axis, [(i, i ^ bit) for i in range(size)])  75.4 us
    ppermute x52, starting transfers between devices, swap(): return lax.ppermute(value, axis, [(i, i ^ bit) for i in range(size)])  61 us
    pallas_call x1, Pallas kernels, attend_back(): pl.pallas_call(functools.partial(attend_back_kernel, items, heads, share)...  11.3 us
    pallas_call x1, Pallas kernels, attend(): pl.pallas_call(functools.partial(attend_kernel, items, heads, rows // 2),...  10.8 us
    pallas_call x6, Pallas kernels, emit(): pl.pallas_call(functools.partial(emit_kernel, len(lefts), len(inputs), la...  10.1 us
    pallas_call x1, Pallas kernels, normed_back(): pl.pallas_call(functools.partial(normed_back_kernel, items, share), out_s...  8.03 us
    pallas_call x1, Pallas kernels, expand(): pl.pallas_call(expand_kernel, out_shape=[shape((span, width), F32), shape...  7.63 us
    pallas_call x1, Pallas kernels, mlp_back(): pl.pallas_call(mlp_back_kernel, out_shape=[shape((2, span, width), BF16),...  6.58 us
  transfers between devices with their start and end apart: 52, of which 31 were waited for; matrix products, arithmetic and copies ran while one was open for 6% of the time, Pallas kernels for 28%

profile of v1, /device:TPU:0, one launch (start us, length us, event | category | flops | bytes accessed | tf_op | source)
XLA Modules:
  0.0 245.1 jit_solution(13144521457059300500)
XLA Ops:
  3.2 3.0 %collective-permute-start = (bf16[208,768]{1,0:T(8,128)(2,1)}, bf16[208,768]{1,0:T(8,128)(2,1)S(1)}, u32[]{:S(2)}, u32[]{:S(2)}) collective-permute-start(bf16[208,768]{1,0:T(8,128)(2,1)} %pad_maximum_fusion.6), channel_id=1, source_target_pairs={{0,2},{1,3},{2,0},{3,1},{4,6},{5,7},{6,4},{7,5},{8,10},{9,11},{10,... | collective-permute-start | bytes 958472 | tf_op jit(solution)/shard_map/ppermute | solution.py:39
  13.8 10.8 %attend.1 = (bf16[1536,768]{1,0:T(8,128)(2,1)}, bf16[1536,192]{1,0:T(8,128)(2,1)}, bf16[1536,192]{1,0:T(8,128)(2,1)}, bf16[1536,192]{1,0:T(8,128)(2,1)}, f32[3,8...) custom-call(s32[3]{0:T(128)S(1)} %copy-done.4, bf16[1536,768]{1,0:T(8,128)(2,1)} %bitcast.20, ...), custom_call_target="tpu_custom_call" | custom-call | flops 1962934272 | bytes 4718592 | tf_op jit(solution)/shard_map/attend/pallas_call | solution.py:171
  24.5 4.2 %collective-permute-done.1.rest_0_ = bf16[192,768]{1,0:T(8,128)(2,1)} collective-permute-done((bf16[192,768]{1,0:T(8,128)(2,1)}, bf16[192,768]{1,0:T(8,128)(2,1)}, u32[]{:S(2)}, u32[]{:S(2)}) %collective-permute-start.1) | collective-permute-done | bytes 294944 | tf_op jit(solution)/shard_map/ppermute | solution.py:39
  33.7 3.5 %collective-permute-done.5.rest_2_ = bf16[192,768]{1,0:T(8,128)(2,1)S(1)} collective-permute-done((bf16[192,768]{1,0:T(8,128)(2,1)}, bf16[192,768]{1,0:T(8,128)(2,1)S(1)}, u32[]{:S(2)}, u32[]{:S(2)}) %collective-permute-start.5) | collective-permute-done | bytes 294944 | tf_op jit(solution)/shard_map/ppermute | solution.py:39
  38.5 3.0 %collective-permute-done.3.far_ref.refs_1_ = bf16[768,192]{1,0:T(8,128)(2,1)S(1)} collective-permute-done((bf16[768,192]{1,0:T(8,128)(2,1)S(1)}, bf16[768,192]{1,0:T(8,128)(2,1)S(1)}, u32[]{:S(2)}, u32[]{:S(2)}) %collective-permute-start.3) | collective-permute-done | bytes 294944 | tf_op jit(solution)/shard_map/ppermute | solution.py:39
  46.9 3.7 %collective-permute-done.7.rest_3_ = bf16[96,768]{1,0:T(8,128)(2,1)S(1)} collective-permute-done((bf16[96,768]{1,0:T(8,128)(2,1)S(1)}, bf16[96,768]{1,0:T(8,128)(2,1)S(1)}, u32[]{:S(2)}, u32[]{:S(2)}) %collective-permute-start.7) | collective-permute-done | bytes 147488 | tf_op jit(solution)/shard_map/ppermute | solution.py:39
  54.3 7.6 %expand.1 = (f32[768,768]{1,0:T(8,128)S(1)}, bf16[768,768]{1,0:T(8,128)(2,1)S(1)}, bf16[2,768,768]{2,1,0:T(8,128)(2,1)S(1)}, bf16[2,768,768]{2,1,0:T(8,128)(2,1)S(1)}) custom-call(bf16[1536,768]{1,0:T(8,128)(2,1)} %bitcast.21, f32[8,768]{1,0:T(8,128)} %reshape.57.vec_ref.norm_ref, bf16[768,768]{1,0:T(8,128)(2,1)S(1)} %project.1.part_ref, ...), custom_call_target="tpu_custom_call" | custom-call | flops 1811939328 | bytes 8257536 | tf_op jit(solution)/shard_map/expand/pallas_call | solution.py:442
  63.0 3.6 %contract.1.part_ref = bf16[768,768]{1,0:T(8,128)(2,1)S(1)} custom-call(bf16[2,768,768]{2,1,0:T(8,128)(2,1)S(1)} %get-tuple-element.219.act_ref.refs_0_, bf16[768,768]{1,0:T(8,128)(2,1)} %down_ref.3, bf16[256,768]{1,0:T(8,128)(2,1)} %copy-done.11, bf16[256,768]{1,0:T(8,128)(2,1)} %copy-done.14, bf16[256,768]{1,0:T(8,128)(2,1)} %copy-done.13, ...), custom_call_target="tpu_custom_call" | custom-call | flops 1811939328 | bytes 4718592 | tf_op jit(solution)/shard_map/contract/pallas_call | solution.py:472
  66.7 2.8 %collective-permute-done.13.other_ref = bf16[768,768]{1,0:T(8,128)(2,1)S(1)} collective-permute-done((bf16[768,768]{1,0:T(8,128)(2,1)S(1)}, bf16[768,768]{1,0:T(8,128)(2,1)S(1)}, u32[]{:S(2)}, u32[]{:S(2)}) %collective-permute-start.13) | collective-permute-done | bytes 1179680 | tf_op jit(solution)/shard_map/ppermute | solution.py:39
  69.6 4.7 %convolve.1 = (bf16[768,768]{1,0:T(8,128)(2,1)S(1)}, f32[2,768,256]{2,1,0:T(8,128)S(1)}, f32[3,4,128]{2,1,0:T(4,128)S(1)}) custom-call(s32[3]{0:T(128)S(1)} %copy-done.4, f32[8,768]{1,0:T(8,128)} %reshape.57.vec_ref.norm_ref, f32[768,768]{1,0:T(8,128)S(1)} %get-tuple-element.220.mid_ref, bf16[768,768]{1,0:T(8,128)(2,1)S(1)} %contract.1.part_ref, ...), custom_call_target="tpu_custom_call" | custom-call | flops 603979776 | bytes 8257536 | tf_op jit(solution)/shard_map/convolve/pallas_call | solution.py:524
  76.4 2.8 %collective-permute-done.15.got_ref = f32[3,4,128]{2,1,0:T(4,128)S(1)} collective-permute-done((f32[3,4,128]{2,1,0:T(4,128)S(1)}, f32[3,4,128]{2,1,0:T(4,128)S(1)}, u32[]{:S(2)}, u32[]{:S(2)}) %collective-permute-start.15) | collective-permute-done | bytes 6176 | tf_op jit(solution)/shard_map/ppermute | solution.py:39
  79.1 3.9 %norm_back.1 = (bf16[768,256]{1,0:T(8,128)(2,1)S(1)}, bf16[768,256]{1,0:T(8,128)(2,1)S(1)}, bf16[2,768,256]{2,1,0:T(8,128)(2,1)S(1)}, bf16[768,768]{1,0:T(8,128)(2,1)S(1)}, f32[8,768]{1,0:T(8,128)S(1)}) custom-call(s32[3]{0:T(128)S(1)} %copy-done.4, f32[8,768]{1,0:T(8,128)} %reshape.57.vec_ref.norm_ref, f32[3,4,128]{2,1,0:T(4,128)S(1)} %add.76.tot_ref, ...), custom_call_target="tpu_custom_call" | custom-call | flops 603979776 | bytes 3538944 | tf_op jit(solution)/shard_map/norm_back/pallas_call | solution.py:584
  86.3 2.4 down_grad.1
  92.5 6.6 %mlp_back.1 = (bf16[2,768,768]{2,1,0:T(8,128)(2,1)S(1)}, bf16[768,768]{1,0:T(8,128)(2,1)S(1)}, f32[8,768]{1,0:T(8,128)S(1)}, f32[2,8,768]{2,1,0:T(8,128)S(1)}) custom-call(bf16[768,768]{1,0:T(8,128)(2,1)S(1)} %get-tuple-element.230.part_ref, bf16[768,768]{1,0:T(8,128)(2,1)S(1)} %collective-permute-done.16.other_ref, ...), custom_call_target="tpu_custom_call" | custom-call | flops 3623878656 | bytes 11796480 | tf_op jit(solution)/shard_map/mlp_back/pallas_call | solution.py:637
  107.8 4.5 %mid_back.1 = (bf16[768,192]{1,0:T(8,128)(2,1)S(1)}, bf16[768,192]{1,0:T(8,128)(2,1)S(1)}, bf16[768,768]{1,0:T(8,128)(2,1)S(1)}, f32[384,768]{1,0:T(8,128)S(1)}, f32[8,768]{1,0:T(8,128)S(1)}) custom-call(f32[8,768]{1,0:T(8,128)} %reshape.57.vec_ref.norm_ref, f32[768,768]{1,0:T(8,128)S(1)} %get-tuple-element.220.mid_ref, ...), custom_call_target="tpu_custom_call" | custom-call | flops 452984832 | bytes 7077888 | tf_op jit(solution)/shard_map/mid_back/pallas_call | solution.py:682
  116.8 2.3 turn_two.1
  119.2 3.5 %collective-permute-done.24.other_ref = bf16[768,192]{1,0:T(8,128)(2,1)S(1)} collective-permute-done((bf16[768,192]{1,0:T(8,128)(2,1)S(1)}, bf16[768,192]{1,0:T(8,128)(2,1)S(1)}, u32[]{:S(2)}, u32[]{:S(2)}) %collective-permute-start.24) | collective-permute-done | bytes 294944 | tf_op jit(solution)/shard_map/ppermute | solution.py:39
  125.4 11.3 %attend_back.1 = (bf16[1536,192]{1,0:T(8,128)(2,1)}, bf16[1536,192]{1,0:T(8,128)(2,1)}, bf16[1536,192]{1,0:T(8,128)(2,1)}, bf16[576,768]{1,0:T(8,128)(2,1)S(1)}, f32[8,768]{1,0:T(8,128)S(1)}) custom-call(s32[3]{0:T(128)S(1)} %copy-done.4, bf16[1536,768]{1,0:T(8,128)(2,1)} %get-tuple-element.283.normed_ref, bf16[1536,192]{1,0:T(8,128)(2,1)} %get-tuple-element.284.q_ref, ...), custom_call_target="tpu_custom_call" | custom-call | flops 2868903936 | bytes 9437184 | tf_op jit(solution)/shard_map/attend_back/pallas_call | solution.py:251
  139.1 2.9 %turn_three.1 = (bf16[224,768]{1,0:T(8,128)(2,1)S(1)}, bf16[288,768]{1,0:T(8,128)(2,1)S(1)}, bf16[320,768]{1,0:T(8,128)(2,1)}, bf16[32,768]{1,0:T(8,128)(2,1)}, ...) custom-call(bf16[64,768]{1,0:T(8,128)(2,1)} %get-tuple-element.274.r, ...), custom_call_target="tpu_custom_call" | custom-call | tf_op jit(solution)/shard_map/turn_three/pallas_call | solution.py:812
  144.6 2.7 %collective-permute-start.28 = (bf16[96,768]{1,0:T(8,128)(2,1)S(1)}, bf16[96,768]{1,0:T(8,128)(2,1)S(1)}, u32[]{:S(2)}, u32[]{:S(2)}) collective-permute-start(bf16[96,768]{1,0:T(8,128)(2,1)S(1)} %constant_dynamic-slice_fusion), channel_id=1, source_target_pairs={{0,16},{4,20},{8,24},{12,28},{16,0},{20,4},{24,8},{28,12},{1,17},{... | collective-permute-start | bytes 442376 | tf_op jit(solution)/shard_map/ppermute | solution.py:39
  148.0 8.0 %normed_back.1 = (bf16[784,768]{1,0:T(8,128)(2,1)}, f32[384,768]{1,0:T(8,128)}, f32[384,768]{1,0:T(8,128)}, f32[8,768]{1,0:T(8,128)S(1)}) custom-call(s32[3]{0:T(128)S(1)} %copy-done.4, bf16[1536,768]{1,0:T(8,128)(2,1)} %bitcast.22, bf16[1536,192]{1,0:T(8,128)(2,1)} %get-tuple-element.315.dq_ref, bf16[1536,192]{1,0:T(8,128)(2,1)} %get-tuple-element.316.dk_ref, ...), custom_call_target="tpu_custom_call" | custom-call | flops 1358954496 | bytes 9437184 | tf_op jit(solution)/shard_map/normed_back/pallas_call | solution.py:329
  157.5 2.3 collective-permute-start.32
  174.7 3.4 %collective-permute-start.37 = (bf16[224,768]{1,0:T(8,128)(2,1)S(1)}, bf16[224,768]{1,0:T(8,128)(2,1)S(1)}, u32[]{:S(2)}, u32[]{:S(2)}) collective-permute-start(bf16[224,768]{1,0:T(8,128)(2,1)S(1)} %fusion), channel_id=1, source_target_pairs={{0,16},{4,20},{8,24},{12,28},{16,0},{20,4},{24,8},{28,12},{1,17},{... | collective-permute-start | bytes 1032200 | tf_op jit(solution)/shard_map/ppermute | solution.py:39
  184.2 9.1 %collective-permute-done.37 = bf16[224,768]{1,0:T(8,128)(2,1)S(1)} collective-permute-done((bf16[224,768]{1,0:T(8,128)(2,1)S(1)}, bf16[224,768]{1,0:T(8,128)(2,1)S(1)}, u32[]{:S(2)}, u32[]{:S(2)}) %collective-permute-start.37) | collective-permute-done | bytes 344096 | tf_op jit(solution)/shard_map/ppermute | solution.py:39
  194.3 2.6 %collective-permute-start.44 = (bf16[224,768]{1,0:T(8,128)(2,1)}, bf16[224,768]{1,0:T(8,128)(2,1)}, u32[]{:S(2)}, u32[]{:S(2)}) collective-permute-start(bf16[224,768]{1,0:T(8,128)(2,1)} %add_convert_fusion.1), channel_id=1, source_target_pairs={{0,16},{4,20},{8,24},{12,28},{16,0},{20,4},{24,8},{28,12},{1,17},{... | collective-permute-start | bytes 1032200 | tf_op jit(solution)/shard_map/ppermute | solution.py:39
  198.3 2.8 %collective-permute-done.45 = f32[10,768]{1,0:T(8,128)S(1)} collective-permute-done((f32[10,768]{1,0:T(8,128)S(1)}, f32[10,768]{1,0:T(8,128)S(1)}, u32[]{:S(2)}, u32[]{:S(2)}) %collective-permute-start.45) | collective-permute-done | bytes 30752 | tf_op jit(solution)/shard_map/ppermute | solution.py:39
  201.1 2.5 %collective-permute-start.46 = (f32[10,768]{1,0:T(8,128)S(1)}, f32[10,768]{1,0:T(8,128)S(1)}, u32[]{:S(2)}, u32[]{:S(2)}) collective-permute-start(f32[10,768]{1,0:T(8,128)S(1)} %fusion.9), channel_id=1, source_target_pairs={{0,8},{4,12},{8,0},{12,4},{16,24},{20,28},{24,16},{28,20},{1,9},{5... | collective-permute-start | bytes 92168 | tf_op jit(solution)/shard_map/ppermute | solution.py:39
  203.7 2.3 collective-permute-done.46
  209.5 4.8 %finish.1 = f32[384,768]{1,0:T(8,128)} custom-call(bf16[1536,768]{1,0:T(8,128)(2,1)} %bitcast.23, f32[8,768]{1,0:T(8,128)} %reshape.57.vec_ref.norm_ref, f32[384,768]{1,0:T(8,128)} %get-tuple-element.359.own_ref, bf16[784,768]{1,0:T(8,128)(2,1)S(1)} %collective-permute-done.33.got_ref, bf16[392,768]{1,0:T(8,128)(2,1)S(1)} %collective-permute-done.38.last_ref, ...), custom_call_target="tpu_custom_call" | custom-call | bytes 4128768 | tf_op jit(solution)/shard_map/finish/pallas_call | solution.py:923
  219.5 5.8 %collective-permute-done.49.refs_3_ = bf16[224,768]{1,0:T(8,128)(2,1)S(1)} collective-permute-done((bf16[224,768]{1,0:T(8,128)(2,1)S(1)}, bf16[224,768]{1,0:T(8,128)(2,1)S(1)}, u32[]{:S(2)}, u32[]{:S(2)}) %collective-permute-start.49) | collective-permute-done | bytes 344096 | tf_op jit(solution)/shard_map/ppermute | solution.py:39
  229.5 11.1 %collective-permute-done.51.refs_4_ = bf16[448,768]{1,0:T(8,128)(2,1)S(1)} collective-permute-done((bf16[448,768]{1,0:T(8,128)(2,1)S(1)}, bf16[448,768]{1,0:T(8,128)(2,1)S(1)}, u32[]{:S(2)}, u32[]{:S(2)}) %collective-permute-start.51) | collective-permute-done | bytes 688160 | tf_op jit(solution)/shard_map/ppermute | solution.py:39
  242.1 3.0 %spread_two.1 = (f32[768,768]{1,0:T(8,128)}, f32[192,768]{1,0:T(8,128)}, f32[192,768]{1,0:T(8,128)}, f32[192,768]{1,0:T(8,128)}, f32[192,768]{1,0:T(8,128)}, /*index=5*/f32[768,256]{1,0:T(8,128)}) custom-call(bf16[448,768]{1,0:T(8,128)(2,1)S(1)} %pad_maximum_fusion.refs_0_, bf16[224,768]{1,0:T(8,128)(2,1)S(1)} %collective-permute-done.48.refs_1_, ...), custom_call_target="tpu_custom_call" | custom-call | bytes 11010048 | tf_op jit(solution)/shard_map/spread_two/pallas_call | solution.py:875
  (217 shorter events, 96.1 us)
Async XLA Ops:
  3.2 25.6 %collective-permute-start = (bf16[208,768]{1,0:T(8,128)(2,1)}, bf16[208,768]{1,0:T(8,128)(2,1)S(1)}, u32[]{:S(2)}, u32[]{:S(2)}) collective-permute-start(bf16[208,768]{1,0:T(8,128)(2,1)} %pad_maximum_fusion.6), channel_id=1, source_target_pairs={{0,2},{1,3},{2,0},{3,1},{4,6},{5,7},{6,4},{7,5},{8,10},{9,11},{10,... | collective-permute-start | bytes 958472 | tf_op jit(solution)/shard_map/ppermute | solution.py:39
  7.6 21.1 %collective-permute-start.2 = (bf16[256,768]{1,0:T(8,128)(2,1)S(1)}, bf16[256,768]{1,0:T(8,128)(2,1)S(1)}, u32[]{:S(2)}, u32[]{:S(2)}) collective-permute-start(bf16[256,768]{1,0:T(8,128)(2,1)S(1)} %pad_maximum_fusion.3), channel_id=1, source_target_pairs={{0,2},{1,3},{2,0},{3,1},{4,6},{5,7},{6,4},{7,5},{8,10},{9,11},{10,... | collective-permute-start | bytes 1179656 | tf_op jit(solution)/shard_map/ppermute | solution.py:39
  9.4 19.3 %collective-permute-start.1 = (bf16[192,768]{1,0:T(8,128)(2,1)}, bf16[192,768]{1,0:T(8,128)(2,1)}, u32[]{:S(2)}, u32[]{:S(2)}) collective-permute-start(bf16[192,768]{1,0:T(8,128)(2,1)} %constant_dynamic-slice_fusion.4), channel_id=1, source_target_pairs={{0,2},{1,3},{2,0},{3,1},{4,6},{5,7},{6,4},{7,5},{8,10},{9,11},{10,... | collective-permute-start | bytes 884744 | tf_op jit(solution)/shard_map/ppermute | solution.py:39
  32.1 9.4 %collective-permute-start.3 = (bf16[768,192]{1,0:T(8,128)(2,1)S(1)}, bf16[768,192]{1,0:T(8,128)(2,1)S(1)}, u32[]{:S(2)}, u32[]{:S(2)}) collective-permute-start(bf16[768,192]{1,0:T(8,128)(2,1)S(1)} %get-tuple-element.200), channel_id=1, source_target_pairs={{0,2},{1,3},{2,0},{3,1},{4,6},{5,7},{6,4},{7,5},{8,10},{9,11},{10,... | collective-permute-start | bytes 884744 | tf_op jit(solution)/shard_map/ppermute | solution.py:39
  45.4 16.5 %collective-permute-start.9 = (bf16[256,768]{1,0:T(8,128)(2,1)S(1)}, bf16[256,768]{1,0:T(8,128)(2,1)S(1)}, u32[]{:S(2)}, u32[]{:S(2)}) collective-permute-start(bf16[256,768]{1,0:T(8,128)(2,1)S(1)} %pad_maximum_fusion.4), channel_id=1, source_target_pairs={{0,2},{1,3},{2,0},{3,1},{4,6},{5,7},{6,4},{7,5},{8,10},{9,11},{10,... | collective-permute-start | bytes 1179656 | tf_op jit(solution)/shard_map/ppermute | solution.py:39
  50.9 11.1 %collective-permute-start.11 = (bf16[256,768]{1,0:T(8,128)(2,1)S(1)}, bf16[256,768]{1,0:T(8,128)(2,1)S(1)}, u32[]{:S(2)}, u32[]{:S(2)}) collective-permute-start(bf16[256,768]{1,0:T(8,128)(2,1)S(1)} %collective-permute-done.2.rest_0_.rest_5_), channel_id=1, source_target_pairs={{0,8},{4,12},{8,0},{12,4},{16,24},{20,28},{24,16},{28,20},{1,9},{5... | collective-permute-start | bytes 1179656 | tf_op jit(solution)/shard_map/ppermute | solution.py:39
  51.4 10.6 %collective-permute-start.10 = (bf16[256,768]{1,0:T(8,128)(2,1)S(1)}, bf16[256,768]{1,0:T(8,128)(2,1)S(1)}, u32[]{:S(2)}, u32[]{:S(2)}) collective-permute-start(bf16[256,768]{1,0:T(8,128)(2,1)S(1)} %collective-permute-done.2.rest_0_.rest_5_), channel_id=1, source_target_pairs={{0,4},{4,0},{8,12},{12,8},{16,20},{20,16},{24,28},{28,24},{1,5},{5... | collective-permute-start | bytes 1179656 | tf_op jit(solution)/shard_map/ppermute | solution.py:39
  52.8 13.8 %collective-permute-start.12 = (bf16[768,256]{1,0:T(8,128)(2,1)S(1)}, bf16[768,256]{1,0:T(8,128)(2,1)S(1)}, u32[]{:S(2)}, u32[]{:S(2)}) collective-permute-start(bf16[768,256]{1,0:T(8,128)(2,1)S(1)} %constant_dynamic-slice_fusion.1), channel_id=1, source_target_pairs={{0,2},{1,3},{2,0},{3,1},{4,6},{5,7},{6,4},{7,5},{8,10},{9,11},{10,... | collective-permute-start | bytes 1179656 | tf_op jit(solution)/shard_map/ppermute | solution.py:39
  88.7 11.2 %collective-permute-start.17 = (bf16[256,768]{1,0:T(8,128)(2,1)S(1)}, bf16[256,768]{1,0:T(8,128)(2,1)S(1)}, u32[]{:S(2)}, u32[]{:S(2)}) collective-permute-start(bf16[256,768]{1,0:T(8,128)(2,1)S(1)} %get-tuple-element.243), channel_id=1, source_target_pairs={{0,2},{1,3},{2,0},{3,1},{4,6},{5,7},{6,4},{7,5},{8,10},{9,11},{10,... | collective-permute-start | bytes 1179656 | tf_op jit(solution)/shard_map/ppermute | solution.py:39
  89.6 10.9 %collective-permute-start.18 = (bf16[256,768]{1,0:T(8,128)(2,1)S(1)}, bf16[256,768]{1,0:T(8,128)(2,1)S(1)}, u32[]{:S(2)}, u32[]{:S(2)}) collective-permute-start(bf16[256,768]{1,0:T(8,128)(2,1)S(1)} %get-tuple-element.244), channel_id=1, source_target_pairs={{0,4},{4,0},{8,12},{12,8},{16,20},{20,16},{24,28},{28,24},{1,5},{5... | collective-permute-start | bytes 1179656 | tf_op jit(solution)/shard_map/ppermute | solution.py:39
  91.0 10.6 %collective-permute-start.19 = (bf16[256,768]{1,0:T(8,128)(2,1)S(1)}, bf16[256,768]{1,0:T(8,128)(2,1)S(1)}, u32[]{:S(2)}, u32[]{:S(2)}) collective-permute-start(bf16[256,768]{1,0:T(8,128)(2,1)S(1)} %get-tuple-element.245), channel_id=1, source_target_pairs={{0,8},{4,12},{8,0},{12,4},{16,24},{20,28},{24,16},{28,20},{1,9},{5... | collective-permute-start | bytes 1179656 | tf_op jit(solution)/shard_map/ppermute | solution.py:39
  104.9 10.9 %collective-permute-start.22 = (bf16[256,768]{1,0:T(8,128)(2,1)S(1)}, bf16[256,768]{1,0:T(8,128)(2,1)S(1)}, u32[]{:S(2)}, u32[]{:S(2)}) collective-permute-start(bf16[256,768]{1,0:T(8,128)(2,1)S(1)} %get-tuple-element.267), channel_id=1, source_target_pairs={{0,4},{4,0},{8,12},{12,8},{16,20},{20,16},{24,28},{28,24},{1,5},{5... | collective-permute-start | bytes 1179656 | tf_op jit(solution)/shard_map/ppermute | solution.py:39
  106.2 10.6 %collective-permute-start.23 = (bf16[256,768]{1,0:T(8,128)(2,1)S(1)}, bf16[256,768]{1,0:T(8,128)(2,1)S(1)}, u32[]{:S(2)}, u32[]{:S(2)}) collective-permute-start(bf16[256,768]{1,0:T(8,128)(2,1)S(1)} %get-tuple-element.268), channel_id=1, source_target_pairs={{0,8},{4,12},{8,0},{12,4},{16,24},{20,28},{24,16},{28,20},{1,9},{5... | collective-permute-start | bytes 1179656 | tf_op jit(solution)/shard_map/ppermute | solution.py:39
  112.3 10.4 %collective-permute-start.24 = (bf16[768,192]{1,0:T(8,128)(2,1)S(1)}, bf16[768,192]{1,0:T(8,128)(2,1)S(1)}, u32[]{:S(2)}, u32[]{:S(2)}) collective-permute-start(bf16[768,192]{1,0:T(8,128)(2,1)S(1)} %get-tuple-element.289), channel_id=1, source_target_pairs={{0,2},{1,3},{2,0},{3,1},{4,6},{5,7},{6,4},{7,5},{8,10},{9,11},{10,... | collective-permute-start | bytes 884744 | tf_op jit(solution)/shard_map/ppermute | solution.py:39
  122.7 15.9 %collective-permute-start.26 = (bf16[448,768]{1,0:T(8,128)(2,1)}, bf16[448,768]{1,0:T(8,128)(2,1)S(1)}, u32[]{:S(2)}, u32[]{:S(2)}) collective-permute-start(bf16[448,768]{1,0:T(8,128)(2,1)} %get-tuple-element.297), channel_id=1, source_target_pairs={{0,4},{4,0},{8,12},{12,8},{16,20},{20,16},{24,28},{28,24},{1,5},{5... | collective-permute-start | bytes 2064392 | tf_op jit(solution)/shard_map/ppermute | solution.py:39
  123.4 15.6 %collective-permute-start.27 = (bf16[448,768]{1,0:T(8,128)(2,1)}, bf16[448,768]{1,0:T(8,128)(2,1)S(1)}, u32[]{:S(2)}, u32[]{:S(2)}) collective-permute-start(bf16[448,768]{1,0:T(8,128)(2,1)} %get-tuple-element.298), channel_id=1, source_target_pairs={{0,8},{4,12},{8,0},{12,4},{16,24},{20,28},{24,16},{28,20},{1,9},{5... | collective-permute-start | bytes 2064392 | tf_op jit(solution)/shard_map/ppermute | solution.py:39
  123.9 13.3 %collective-permute-start.25 = (bf16[384,768]{1,0:T(8,128)(2,1)}, bf16[384,768]{1,0:T(8,128)(2,1)S(1)}, u32[]{:S(2)}, u32[]{:S(2)}) collective-permute-start(bf16[384,768]{1,0:T(8,128)(2,1)} %get-tuple-element.296), channel_id=1, source_target_pairs={{0,2},{1,3},{2,0},{3,1},{4,6},{5,7},{6,4},{7,5},{8,10},{9,11},{10,... | collective-permute-start | bytes 1769480 | tf_op jit(solution)/shard_map/ppermute | solution.py:39
  142.7 13.4 %collective-permute-start.30 = (bf16[288,768]{1,0:T(8,128)(2,1)S(1)}, bf16[288,768]{1,0:T(8,128)(2,1)S(1)}, u32[]{:S(2)}, u32[]{:S(2)}) collective-permute-start(bf16[288,768]{1,0:T(8,128)(2,1)S(1)} %get-tuple-element.322), channel_id=1, source_target_pairs={{0,4},{4,0},{8,12},{12,8},{16,20},{20,16},{24,28},{28,24},{1,5},{5... | collective-permute-start | bytes 1327112 | tf_op jit(solution)/shard_map/ppermute | solution.py:39
  144.0 13.4 %collective-permute-start.31 = (bf16[320,768]{1,0:T(8,128)(2,1)}, bf16[320,768]{1,0:T(8,128)(2,1)S(1)}, u32[]{:S(2)}, u32[]{:S(2)}) collective-permute-start(bf16[320,768]{1,0:T(8,128)(2,1)} %get-tuple-element.323), channel_id=1, source_target_pairs={{0,8},{4,12},{8,0},{12,4},{16,24},{20,28},{24,16},{28,20},{1,9},{5... | collective-permute-start | bytes 1474568 | tf_op jit(solution)/shard_map/ppermute | solution.py:39
  144.6 11.4 %collective-permute-start.28 = (bf16[96,768]{1,0:T(8,128)(2,1)S(1)}, bf16[96,768]{1,0:T(8,128)(2,1)S(1)}, u32[]{:S(2)}, u32[]{:S(2)}) collective-permute-start(bf16[96,768]{1,0:T(8,128)(2,1)S(1)} %constant_dynamic-slice_fusion), channel_id=1, source_target_pairs={{0,16},{4,20},{8,24},{12,28},{16,0},{20,4},{24,8},{28,12},{1,17},{... | collective-permute-start | bytes 442376 | tf_op jit(solution)/shard_map/ppermute | solution.py:39
  157.4 14.4 %collective-permute-start.33 = (bf16[784,768]{1,0:T(8,128)(2,1)}, bf16[784,768]{1,0:T(8,128)(2,1)S(1)}, u32[]{:S(2)}, u32[]{:S(2)}) collective-permute-start(bf16[784,768]{1,0:T(8,128)(2,1)} %get-tuple-element.334), channel_id=1, source_target_pairs={{0,1},{1,0},{2,3},{3,2},{4,5},{5,4},{6,7},{7,6},{8,9},{9,8},{10,11... | collective-permute-start | bytes 3612680 | tf_op jit(solution)/shard_map/ppermute | solution.py:39
  157.5 10.3 %collective-permute-start.32 = (bf16[96,768]{1,0:T(8,128)(2,1)S(1)}, bf16[96,768]{1,0:T(8,128)(2,1)}, u32[]{:S(2)}, u32[]{:S(2)}) collective-permute-start(bf16[96,768]{1,0:T(8,128)(2,1)S(1)} %add_convert_fusion.2), channel_id=1, source_target_pairs={{0,16},{4,20},{8,24},{12,28},{16,0},{20,4},{24,8},{28,12},{1,17},{... | collective-permute-start | bytes 442376 | tf_op jit(solution)/shard_map/ppermute | solution.py:39
  173.0 10.6 %collective-permute-start.41 = (bf16[64,768]{1,0:T(8,128)(2,1)S(1)}, bf16[64,768]{1,0:T(8,128)(2,1)S(1)}, u32[]{:S(2)}, u32[]{:S(2)}) collective-permute-start(bf16[64,768]{1,0:T(8,128)(2,1)S(1)} %slice.69), channel_id=1, source_target_pairs={{0,4},{4,0},{8,12},{12,8},{16,20},{20,16},{24,28},{28,24},{1,5},{5... | collective-permute-start | bytes 294920 | tf_op jit(solution)/shard_map/ppermute | solution.py:39
  174.7 18.6 %collective-permute-start.37 = (bf16[224,768]{1,0:T(8,128)(2,1)S(1)}, bf16[224,768]{1,0:T(8,128)(2,1)S(1)}, u32[]{:S(2)}, u32[]{:S(2)}) collective-permute-start(bf16[224,768]{1,0:T(8,128)(2,1)S(1)} %fusion), channel_id=1, source_target_pairs={{0,16},{4,20},{8,24},{12,28},{16,0},{20,4},{24,8},{28,12},{1,17},{... | collective-permute-start | bytes 1032200 | tf_op jit(solution)/shard_map/ppermute | solution.py:39
  179.5 14.8 %collective-permute-start.38 = (bf16[392,768]{1,0:T(8,128)(2,1)S(1)}, bf16[392,768]{1,0:T(8,128)(2,1)S(1)}, u32[]{:S(2)}, u32[]{:S(2)}) collective-permute-start(bf16[392,768]{1,0:T(8,128)(2,1)S(1)} %get-tuple-element.347), channel_id=1, source_target_pairs={{0,2},{1,3},{2,0},{3,1},{4,6},{5,7},{6,4},{7,5},{8,10},{9,11},{10,... | collective-permute-start | bytes 1806344 | tf_op jit(solution)/shard_map/ppermute | solution.py:39
  182.0 12.3 %collective-permute-start.40 = (bf16[256,768]{1,0:T(8,128)(2,1)S(1)}, bf16[256,768]{1,0:T(8,128)(2,1)S(1)}, u32[]{:S(2)}, u32[]{:S(2)}) collective-permute-start(bf16[256,768]{1,0:T(8,128)(2,1)S(1)} %pad_maximum_fusion.5), channel_id=1, source_target_pairs={{0,4},{4,0},{8,12},{12,8},{16,20},{20,16},{24,28},{28,24},{1,5},{5... | collective-permute-start | bytes 1179656 | tf_op jit(solution)/shard_map/ppermute | solution.py:39
  183.6 10.7 %collective-permute-start.42 = (bf16[128,768]{1,0:T(8,128)(2,1)S(1)}, bf16[128,768]{1,0:T(8,128)(2,1)S(1)}, u32[]{:S(2)}, u32[]{:S(2)}) collective-permute-start(bf16[128,768]{1,0:T(8,128)(2,1)S(1)} %pad_maximum_fusion.8), channel_id=1, source_target_pairs={{0,8},{4,12},{8,0},{12,4},{16,24},{20,28},{24,16},{28,20},{1,9},{5... | collective-permute-start | bytes 589832 | tf_op jit(solution)/shard_map/ppermute | solution.py:39
  194.3 21.7 %collective-permute-start.44 = (bf16[224,768]{1,0:T(8,128)(2,1)}, bf16[224,768]{1,0:T(8,128)(2,1)}, u32[]{:S(2)}, u32[]{:S(2)}) collective-permute-start(bf16[224,768]{1,0:T(8,128)(2,1)} %add_convert_fusion.1), channel_id=1, source_target_pairs={{0,16},{4,20},{8,24},{12,28},{16,0},{20,4},{24,8},{28,12},{1,17},{... | collective-permute-start | bytes 1032200 | tf_op jit(solution)/shard_map/ppermute | solution.py:39
  206.0 10.1 %collective-permute-start.47 = (f32[10,768]{1,0:T(8,128)S(1)}, f32[10,768]{1,0:T(8,128)S(1)}, u32[]{:S(2)}, u32[]{:S(2)}) collective-permute-start(f32[10,768]{1,0:T(8,128)S(1)} %add.87), channel_id=1, source_target_pairs={{0,16},{4,20},{8,24},{12,28},{16,0},{20,4},{24,8},{28,12},{1,17},{... | collective-permute-start | bytes 92168 | tf_op jit(solution)/shard_map/ppermute | solution.py:39
  208.0 10.1 %collective-permute-start.43 = (bf16[768,256]{1,0:T(8,128)(2,1)}, bf16[768,256]{1,0:T(8,128)(2,1)S(1)}, u32[]{:S(2)}, u32[]{:S(2)}) collective-permute-start(bf16[768,256]{1,0:T(8,128)(2,1)} %copy-done.6), channel_id=1, source_target_pairs={{0,2},{1,3},{2,0},{3,1},{4,6},{5,7},{6,4},{7,5},{8,10},{9,11},{10,... | collective-permute-start | bytes 1179656 | tf_op jit(solution)/shard_map/ppermute | solution.py:39
  225.8 14.8 %collective-permute-start.51 = (bf16[448,768]{1,0:T(8,128)(2,1)S(1)}, bf16[448,768]{1,0:T(8,128)(2,1)S(1)}, u32[]{:S(2)}, u32[]{:S(2)}) collective-permute-start(bf16[448,768]{1,0:T(8,128)(2,1)S(1)} %pad_maximum_fusion.2), channel_id=1, source_target_pairs={{0,8},{4,12},{8,0},{12,4},{16,24},{20,28},{24,16},{28,20},{1,9},{5... | collective-permute-start | bytes 2064392 | tf_op jit(solution)/shard_map/ppermute | solution.py:39
  227.1 15.0 %collective-permute-start.50 = (bf16[448,768]{1,0:T(8,128)(2,1)S(1)}, bf16[448,768]{1,0:T(8,128)(2,1)S(1)}, u32[]{:S(2)}, u32[]{:S(2)}) collective-permute-start(bf16[448,768]{1,0:T(8,128)(2,1)S(1)} %pad_maximum_fusion.1), channel_id=1, source_target_pairs={{0,4},{4,0},{8,12},{12,8},{16,20},{20,16},{24,28},{28,24},{1,5},{5... | collective-permute-start | bytes 2064392 | tf_op jit(solution)/shard_map/ppermute | solution.py:39
  (55 other events, 311.1 us)

commit v2 on v1

--- a/solution.py
+++ b/solution.py
@@ -692,7 +692,7 @@
         out_specs=[vmem()] * 5,
         scratch_shapes=[pltpu.VMEM((span, width), F32)],
         **params("mid_back", 4 * span * width * hw, 12 * width * width),
-    )(*in_hbm(vecs), mid, part, other, grad, got, *in_hbm(out_w, pack))
+    )(vecs, mid, part, other, grad, got, out_w, pack)
 
 
 LINKS = {"y": ("mp", 2), "x": ("dp", 1), "z": ("dp", 2)}
@@ -1007,11 +1007,14 @@
     cot_rows = cotangent.reshape(rows, -1)
     cot_sent = lax.dynamic_slice_in_dim(cot_rows, (1 - chip) * span, span, 0)
     low_sent = low_quarter(mine ^ 3)
-    far, low_part, low_sent, cot_sent, *up_parts = join(far, low_part, low_sent, cot_sent, *up_parts)
+    last_half = quarter // 2
+    turned = [up_parts[2][:last_half], up_parts[1][last_half:]]
+    far, low_part, low_sent, cot_sent, turned[0], turned[1], *up_parts = join(
+        far, low_part, low_sent, cot_sent, *turned, *up_parts
+    )
     low_last = swap(low_sent, "mp", 2)
-    last_half = quarter // 2
-    up_parts.append(swap(up_parts[2][:last_half], "dp", 1))
-    up_parts.append(swap(up_parts[1][last_half:], "dp", 2))
+    up_parts.append(swap(turned[0], "dp", 1))
+    up_parts.append(swap(turned[1], "dp", 2))
 
     part = project(near, far, out_w, out_far)
     part_got = swap(part, "mp", 1)

time: 246 us -> 244 us (level)
  transfers between devices with their start and end apart: 52 -> 52, of which waited for: 31 -> 32; matrix products, arithmetic and copies ran while one was open for 6% -> 6% of each run, Pallas kernels for 28% -> 28%
where the time goes in v2:
time: 244 us; the launch traced here: 243 us
  Pallas kernels  86.5 us (35%)
  waiting for transfers between devices  74.4 us (30%)
  starting transfers between devices  60.9 us (25%)
  local copies, waits for them, and re-layouts  12.2 us (5%)
  other arithmetic  7.98 us (3%)
    ppermute x52, waiting for transfers between devices, swap(): return lax.ppermute(value, axis, [(i, i ^ bit) for i in range(size)])  74.4 us
    ppermute x52, starting transfers between devices, swap(): return lax.ppermute(value, axis, [(i, i ^ bit) for i in range(size)])  60.9 us
    pallas_call x1, Pallas kernels, attend_back(): pl.pallas_call(functools.partial(attend_back_kernel, items, heads, share)...  11.3 us
    pallas_call x1, Pallas kernels, attend(): pl.pallas_call(functools.partial(attend_kernel, items, heads, rows // 2),...  10.8 us
    pallas_call x6, Pallas kernels, emit(): pl.pallas_call(functools.partial(emit_kernel, len(lefts), len(inputs), la...  10.4 us
    pallas_call x1, Pallas kernels, normed_back(): pl.pallas_call(functools.partial(normed_back_kernel, items, share), out_s...  8.03 us
    pallas_call x1, Pallas kernels, expand(): pl.pallas_call(expand_kernel, out_shape=[shape((span, width), F32), shape...  7.63 us
    pallas_call x1, Pallas kernels, mlp_back(): pl.pallas_call(mlp_back_kernel, out_shape=[shape((2, span, width), BF16),...  6.58 us
  transfers between devices with their start and end apart: 52, of which 32 were waited for; matrix products, arithmetic and copies ran while one was open for 6% of the time, Pallas kernels for 28%

profile of v2, /device:TPU:0, one launch (start us, length us, event | category | flops | bytes accessed | tf_op | source)
XLA Modules:
  0.0 243.2 jit_solution(14211726927486783054)
XLA Ops:
  3.2 3.0 %collective-permute-start = (bf16[208,768]{1,0:T(8,128)(2,1)}, bf16[208,768]{1,0:T(8,128)(2,1)S(1)}, u32[]{:S(2)}, u32[]{:S(2)}) collective-permute-start(bf16[208,768]{1,0:T(8,128)(2,1)} %pad_maximum_fusion.6), channel_id=1, source_target_pairs={{0,2},{1,3},{2,0},{3,1},{4,6},{5,7},{6,4},{7,5},{8,10},{9,11},{10,... | collective-permute-start | bytes 958472 | tf_op jit(solution)/shard_map/ppermute | solution.py:39
  13.8 10.8 %attend.1 = (bf16[1536,768]{1,0:T(8,128)(2,1)}, bf16[1536,192]{1,0:T(8,128)(2,1)}, bf16[1536,192]{1,0:T(8,128)(2,1)}, bf16[1536,192]{1,0:T(8,128)(2,1)}, f32[3,8...) custom-call(s32[3]{0:T(128)S(1)} %copy-done.7, bf16[1536,768]{1,0:T(8,128)(2,1)} %bitcast.20, ...), custom_call_target="tpu_custom_call" | custom-call | flops 1962934272 | bytes 4718592 | tf_op jit(solution)/shard_map/attend/pallas_call | solution.py:171
  24.5 4.2 %collective-permute-done.1.rest_0_ = bf16[192,768]{1,0:T(8,128)(2,1)} collective-permute-done((bf16[192,768]{1,0:T(8,128)(2,1)}, bf16[192,768]{1,0:T(8,128)(2,1)}, u32[]{:S(2)}, u32[]{:S(2)}) %collective-permute-start.1) | collective-permute-done | bytes 294944 | tf_op jit(solution)/shard_map/ppermute | solution.py:39
  33.7 3.5 %collective-permute-done.5.rest_1_ = bf16[192,768]{1,0:T(8,128)(2,1)S(1)} collective-permute-done((bf16[192,768]{1,0:T(8,128)(2,1)}, bf16[192,768]{1,0:T(8,128)(2,1)S(1)}, u32[]{:S(2)}, u32[]{:S(2)}) %collective-permute-start.5) | collective-permute-done | bytes 294944 | tf_op jit(solution)/shard_map/ppermute | solution.py:39
  45.9 3.7 %collective-permute-done.7.rest_3_ = bf16[96,768]{1,0:T(8,128)(2,1)S(1)} collective-permute-done((bf16[96,768]{1,0:T(8,128)(2,1)S(1)}, bf16[96,768]{1,0:T(8,128)(2,1)S(1)}, u32[]{:S(2)}, u32[]{:S(2)}) %collective-permute-start.7) | collective-permute-done | bytes 147488 | tf_op jit(solution)/shard_map/ppermute | solution.py:39
  53.4 7.6 %expand.1 = (f32[768,768]{1,0:T(8,128)S(1)}, bf16[768,768]{1,0:T(8,128)(2,1)S(1)}, bf16[2,768,768]{2,1,0:T(8,128)(2,1)S(1)}, bf16[2,768,768]{2,1,0:T(8,128)(2,1)S(1)}) custom-call(bf16[1536,768]{1,0:T(8,128)(2,1)} %bitcast.21, f32[8,768]{1,0:T(8,128)} %reshape.57.vec_ref.norm_ref, bf16[768,768]{1,0:T(8,128)(2,1)S(1)} %project.1.part_ref, ...), custom_call_target="tpu_custom_call" | custom-call | flops 1811939328 | bytes 8257536 | tf_op jit(solution)/shard_map/expand/pallas_call | solution.py:442
  62.0 3.6 %contract.1.part_ref = bf16[768,768]{1,0:T(8,128)(2,1)S(1)} custom-call(bf16[2,768,768]{2,1,0:T(8,128)(2,1)S(1)} %get-tuple-element.223.act_ref.refs_0_, bf16[768,768]{1,0:T(8,128)(2,1)} %down_ref.3, bf16[256,768]{1,0:T(8,128)(2,1)} %copy-done.13, bf16[256,768]{1,0:T(8,128)(2,1)} %copy-done.16, bf16[256,768]{1,0:T(8,128)(2,1)} %copy-done.15, ...), custom_call_target="tpu_custom_call" | custom-call | flops 1811939328 | bytes 4718592 | tf_op jit(solution)/shard_map/contract/pallas_call | solution.py:472
  65.7 2.8 %collective-permute-done.13.other_ref = bf16[768,768]{1,0:T(8,128)(2,1)S(1)} collective-permute-done((bf16[768,768]{1,0:T(8,128)(2,1)S(1)}, bf16[768,768]{1,0:T(8,128)(2,1)S(1)}, u32[]{:S(2)}, u32[]{:S(2)}) %collective-permute-start.13) | collective-permute-done | bytes 1179680 | tf_op jit(solution)/shard_map/ppermute | solution.py:39
  68.6 4.7 %convolve.1 = (bf16[768,768]{1,0:T(8,128)(2,1)S(1)}, f32[2,768,256]{2,1,0:T(8,128)S(1)}, f32[3,4,128]{2,1,0:T(4,128)S(1)}) custom-call(s32[3]{0:T(128)S(1)} %copy-done.7, f32[8,768]{1,0:T(8,128)} %reshape.57.vec_ref.norm_ref, f32[768,768]{1,0:T(8,128)S(1)} %get-tuple-element.224.mid_ref, bf16[768,768]{1,0:T(8,128)(2,1)S(1)} %contract.1.part_ref, ...), custom_call_target="tpu_custom_call" | custom-call | flops 603979776 | bytes 8257536 | tf_op jit(solution)/shard_map/convolve/pallas_call | solution.py:524
  75.3 2.8 %collective-permute-done.15.got_ref = f32[3,4,128]{2,1,0:T(4,128)S(1)} collective-permute-done((f32[3,4,128]{2,1,0:T(4,128)S(1)}, f32[3,4,128]{2,1,0:T(4,128)S(1)}, u32[]{:S(2)}, u32[]{:S(2)}) %collective-permute-start.15) | collective-permute-done | bytes 6176 | tf_op jit(solution)/shard_map/ppermute | solution.py:39
  78.1 3.9 %norm_back.1 = (bf16[768,256]{1,0:T(8,128)(2,1)S(1)}, bf16[768,256]{1,0:T(8,128)(2,1)S(1)}, bf16[2,768,256]{2,1,0:T(8,128)(2,1)S(1)}, bf16[768,768]{1,0:T(8,128)(2,1)S(1)}, f32[8,768]{1,0:T(8,128)S(1)}) custom-call(s32[3]{0:T(128)S(1)} %copy-done.7, f32[8,768]{1,0:T(8,128)} %reshape.57.vec_ref.norm_ref, f32[3,4,128]{2,1,0:T(4,128)S(1)} %add.76.tot_ref, ...), custom_call_target="tpu_custom_call" | custom-call | flops 603979776 | bytes 3538944 | tf_op jit(solution)/shard_map/norm_back/pallas_call | solution.py:584
  85.3 2.4 down_grad.1
  91.5 6.6 %mlp_back.1 = (bf16[2,768,768]{2,1,0:T(8,128)(2,1)S(1)}, bf16[768,768]{1,0:T(8,128)(2,1)S(1)}, f32[8,768]{1,0:T(8,128)S(1)}, f32[2,8,768]{2,1,0:T(8,128)S(1)}) custom-call(bf16[768,768]{1,0:T(8,128)(2,1)S(1)} %get-tuple-element.234.part_ref, bf16[768,768]{1,0:T(8,128)(2,1)S(1)} %collective-permute-done.16.other_ref, ...), custom_call_target="tpu_custom_call" | custom-call | flops 3623878656 | bytes 11796480 | tf_op jit(solution)/shard_map/mlp_back/pallas_call | solution.py:637
  106.8 3.4 %mid_back.1 = (bf16[768,192]{1,0:T(8,128)(2,1)S(1)}, bf16[768,192]{1,0:T(8,128)(2,1)S(1)}, bf16[768,768]{1,0:T(8,128)(2,1)S(1)}, f32[384,768]{1,0:T(8,128)S(1)}, f32[8,768]{1,0:T(8,128)S(1)}) custom-call(f32[8,768]{1,0:T(8,128)S(1)} %copy-done.4, f32[768,768]{1,0:T(8,128)S(1)} %get-tuple-element.224.mid_ref, ...), custom_call_target="tpu_custom_call" | custom-call | flops 452984832 | bytes 7077888 | tf_op jit(solution)/shard_map/mid_back/pallas_call | solution.py:682
  111.8 2.9 %collective-permute-done.22.refs_6_ = bf16[256,768]{1,0:T(8,128)(2,1)S(1)} collective-permute-done((bf16[256,768]{1,0:T(8,128)(2,1)S(1)}, bf16[256,768]{1,0:T(8,128)(2,1)S(1)}, u32[]{:S(2)}, u32[]{:S(2)}) %collective-permute-start.22) | collective-permute-done | bytes 393248 | tf_op jit(solution)/shard_map/ppermute | solution.py:39
  118.2 2.5 %collective-permute-done.24.other_ref = bf16[768,192]{1,0:T(8,128)(2,1)S(1)} collective-permute-done((bf16[768,192]{1,0:T(8,128)(2,1)S(1)}, bf16[768,192]{1,0:T(8,128)(2,1)S(1)}, u32[]{:S(2)}, u32[]{:S(2)}) %collective-permute-start.24) | collective-permute-done | bytes 294944 | tf_op jit(solution)/shard_map/ppermute | solution.py:39
  124.1 11.3 %attend_back.1 = (bf16[1536,192]{1,0:T(8,128)(2,1)}, bf16[1536,192]{1,0:T(8,128)(2,1)}, bf16[1536,192]{1,0:T(8,128)(2,1)}, bf16[576,768]{1,0:T(8,128)(2,1)S(1)}, f32[8,768]{1,0:T(8,128)S(1)}) custom-call(s32[3]{0:T(128)S(1)} %copy-done.7, bf16[1536,768]{1,0:T(8,128)(2,1)} %get-tuple-element.287.normed_ref, bf16[1536,192]{1,0:T(8,128)(2,1)} %get-tuple-element.288.q_ref, ...), custom_call_target="tpu_custom_call" | custom-call | flops 2868903936 | bytes 9437184 | tf_op jit(solution)/shard_map/attend_back/pallas_call | solution.py:251
  137.4 3.2 %turn_three.1 = (bf16[224,768]{1,0:T(8,128)(2,1)S(1)}, bf16[288,768]{1,0:T(8,128)(2,1)}, bf16[320,768]{1,0:T(8,128)(2,1)}, bf16[32,768]{1,0:T(8,128)(2,1)}, bf16...) custom-call(bf16[64,768]{1,0:T(8,128)(2,1)} %get-tuple-element.278.r, ...), custom_call_target="tpu_custom_call" | custom-call | tf_op jit(solution)/shard_map/turn_three/pallas_call | solution.py:812
  143.2 2.6 %collective-permute-start.28 = (bf16[96,768]{1,0:T(8,128)(2,1)S(1)}, bf16[96,768]{1,0:T(8,128)(2,1)S(1)}, u32[]{:S(2)}, u32[]{:S(2)}) collective-permute-start(bf16[96,768]{1,0:T(8,128)(2,1)S(1)} %constant_dynamic-slice_fusion), channel_id=1, source_target_pairs={{0,16},{4,20},{8,24},{12,28},{16,0},{20,4},{24,8},{28,12},{1,17},{... | collective-permute-start | bytes 442376 | tf_op jit(solution)/shard_map/ppermute | solution.py:39
  146.8 8.0 %normed_back.1 = (bf16[784,768]{1,0:T(8,128)(2,1)}, f32[384,768]{1,0:T(8,128)}, f32[384,768]{1,0:T(8,128)}, f32[8,768]{1,0:T(8,128)S(1)}) custom-call(s32[3]{0:T(128)S(1)} %copy-done.7, bf16[1536,768]{1,0:T(8,128)(2,1)} %bitcast.22, bf16[1536,192]{1,0:T(8,128)(2,1)} %get-tuple-element.319.dq_ref, bf16[1536,192]{1,0:T(8,128)(2,1)} %get-tuple-element.320.dk_ref, ...), custom_call_target="tpu_custom_call" | custom-call | flops 1358954496 | bytes 9437184 | tf_op jit(solution)/shard_map/normed_back/pallas_call | solution.py:329
  155.7 2.7 %collective-permute-start.32 = (bf16[96,768]{1,0:T(8,128)(2,1)S(1)}, bf16[96,768]{1,0:T(8,128)(2,1)}, u32[]{:S(2)}, u32[]{:S(2)}) collective-permute-start(bf16[96,768]{1,0:T(8,128)(2,1)S(1)} %add_convert_fusion.2), channel_id=1, source_target_pairs={{0,16},{4,20},{8,24},{12,28},{16,0},{20,4},{24,8},{28,12},{1,17},{... | collective-permute-start | bytes 442376 | tf_op jit(solution)/shard_map/ppermute | solution.py:39
  163.6 2.7 %collective-permute-done.32 = bf16[96,768]{1,0:T(8,128)(2,1)} collective-permute-done((bf16[96,768]{1,0:T(8,128)(2,1)S(1)}, bf16[96,768]{1,0:T(8,128)(2,1)}, u32[]{:S(2)}, u32[]{:S(2)}) %collective-permute-start.32) | collective-permute-done | bytes 147488 | tf_op jit(solution)/shard_map/ppermute | solution.py:39
  167.3 2.6 %collective-permute-done.36.refs_8_ = bf16[144,768]{1,0:T(8,128)(2,1)S(1)} collective-permute-done((bf16[144,768]{1,0:T(8,128)(2,1)S(1)}, bf16[144,768]{1,0:T(8,128)(2,1)S(1)}, u32[]{:S(2)}, u32[]{:S(2)}) %collective-permute-start.36) | collective-permute-done | bytes 221216 | tf_op jit(solution)/shard_map/ppermute | solution.py:39
  173.1 3.5 %collective-permute-start.37 = (bf16[224,768]{1,0:T(8,128)(2,1)S(1)}, bf16[224,768]{1,0:T(8,128)(2,1)S(1)}, u32[]{:S(2)}, u32[]{:S(2)}) collective-permute-start(bf16[224,768]{1,0:T(8,128)(2,1)S(1)} %fusion), channel_id=1, source_target_pairs={{0,16},{4,20},{8,24},{12,28},{16,0},{20,4},{24,8},{28,12},{1,17},{... | collective-permute-start | bytes 1032200 | tf_op jit(solution)/shard_map/ppermute | solution.py:39
  182.0 9.7 %collective-permute-done.37 = bf16[224,768]{1,0:T(8,128)(2,1)S(1)} collective-permute-done((bf16[224,768]{1,0:T(8,128)(2,1)S(1)}, bf16[224,768]{1,0:T(8,128)(2,1)S(1)}, u32[]{:S(2)}, u32[]{:S(2)}) %collective-permute-start.37) | collective-permute-done | bytes 344096 | tf_op jit(solution)/shard_map/ppermute | solution.py:39
  192.7 2.4 %collective-permute-start.44 = (bf16[224,768]{1,0:T(8,128)(2,1)}, bf16[224,768]{1,0:T(8,128)(2,1)}, u32[]{:S(2)}, u32[]{:S(2)}) collective-permute-start(bf16[224,768]{1,0:T(8,128)(2,1)} %add_convert_fusion.1), channel_id=1, source_target_pairs={{0,16},{4,20},{8,24},{12,28},{16,0},{20,4},{24,8},{28,12},{1,17},{... | collective-permute-start | bytes 1032200 | tf_op jit(solution)/shard_map/ppermute | solution.py:39
  196.4 2.9 %collective-permute-done.45 = f32[10,768]{1,0:T(8,128)S(1)} collective-permute-done((f32[10,768]{1,0:T(8,128)S(1)}, f32[10,768]{1,0:T(8,128)S(1)}, u32[]{:S(2)}, u32[]{:S(2)}) %collective-permute-start.45) | collective-permute-done | bytes 30752 | tf_op jit(solution)/shard_map/ppermute | solution.py:39
  199.3 2.5 %collective-permute-start.46 = (f32[10,768]{1,0:T(8,128)S(1)}, f32[10,768]{1,0:T(8,128)S(1)}, u32[]{:S(2)}, u32[]{:S(2)}) collective-permute-start(f32[10,768]{1,0:T(8,128)S(1)} %fusion.9), channel_id=1, source_target_pairs={{0,8},{4,12},{8,0},{12,4},{16,24},{20,28},{24,16},{28,20},{1,9},{5... | collective-permute-start | bytes 92168 | tf_op jit(solution)/shard_map/ppermute | solution.py:39
  207.3 4.8 %finish.1 = f32[384,768]{1,0:T(8,128)} custom-call(bf16[1536,768]{1,0:T(8,128)(2,1)} %bitcast.23, f32[8,768]{1,0:T(8,128)} %reshape.57.vec_ref.norm_ref, f32[384,768]{1,0:T(8,128)} %get-tuple-element.363.own_ref, bf16[784,768]{1,0:T(8,128)(2,1)S(1)} %collective-permute-done.33.got_ref, bf16[392,768]{1,0:T(8,128)(2,1)S(1)} %collective-permute-done.38.last_ref, ...), custom_call_target="tpu_custom_call" | custom-call | bytes 4128768 | tf_op jit(solution)/shard_map/finish/pallas_call | solution.py:923
  217.4 5.7 %collective-permute-done.49.refs_3_ = bf16[224,768]{1,0:T(8,128)(2,1)S(1)} collective-permute-done((bf16[224,768]{1,0:T(8,128)(2,1)S(1)}, bf16[224,768]{1,0:T(8,128)(2,1)S(1)}, u32[]{:S(2)}, u32[]{:S(2)}) %collective-permute-start.49) | collective-permute-done | bytes 344096 | tf_op jit(solution)/shard_map/ppermute | solution.py:39
  227.7 11.1 %collective-permute-done.51.refs_4_ = bf16[448,768]{1,0:T(8,128)(2,1)S(1)} collective-permute-done((bf16[448,768]{1,0:T(8,128)(2,1)S(1)}, bf16[448,768]{1,0:T(8,128)(2,1)S(1)}, u32[]{:S(2)}, u32[]{:S(2)}) %collective-permute-start.51) | collective-permute-done | bytes 688160 | tf_op jit(solution)/shard_map/ppermute | solution.py:39
  240.2 3.0 %spread_two.1 = (f32[768,768]{1,0:T(8,128)}, f32[192,768]{1,0:T(8,128)}, f32[192,768]{1,0:T(8,128)}, f32[192,768]{1,0:T(8,128)}, f32[192,768]{1,0:T(8,128)}, /*index=5*/f32[768,256]{1,0:T(8,128)}) custom-call(bf16[448,768]{1,0:T(8,128)(2,1)S(1)} %pad_maximum_fusion.refs_0_, bf16[224,768]{1,0:T(8,128)(2,1)S(1)} %collective-permute-done.48.refs_1_, ...), custom_call_target="tpu_custom_call" | custom-call | bytes 11010048 | tf_op jit(solution)/shard_map/spread_two/pallas_call | solution.py:875
  (221 shorter events, 94.5 us)
Async XLA Ops:
  3.2 25.6 %collective-permute-start = (bf16[208,768]{1,0:T(8,128)(2,1)}, bf16[208,768]{1,0:T(8,128)(2,1)S(1)}, u32[]{:S(2)}, u32[]{:S(2)}) collective-permute-start(bf16[208,768]{1,0:T(8,128)(2,1)} %pad_maximum_fusion.6), channel_id=1, source_target_pairs={{0,2},{1,3},{2,0},{3,1},{4,6},{5,7},{6,4},{7,5},{8,10},{9,11},{10,... | collective-permute-start | bytes 958472 | tf_op jit(solution)/shard_map/ppermute | solution.py:39
  7.6 21.1 %collective-permute-start.2 = (bf16[256,768]{1,0:T(8,128)(2,1)S(1)}, bf16[256,768]{1,0:T(8,128)(2,1)S(1)}, u32[]{:S(2)}, u32[]{:S(2)}) collective-permute-start(bf16[256,768]{1,0:T(8,128)(2,1)S(1)} %pad_maximum_fusion.3), channel_id=1, source_target_pairs={{0,2},{1,3},{2,0},{3,1},{4,6},{5,7},{6,4},{7,5},{8,10},{9,11},{10,... | collective-permute-start | bytes 1179656 | tf_op jit(solution)/shard_map/ppermute | solution.py:39
  9.4 19.3 %collective-permute-start.1 = (bf16[192,768]{1,0:T(8,128)(2,1)}, bf16[192,768]{1,0:T(8,128)(2,1)}, u32[]{:S(2)}, u32[]{:S(2)}) collective-permute-start(bf16[192,768]{1,0:T(8,128)(2,1)} %constant_dynamic-slice_fusion.4), channel_id=1, source_target_pairs={{0,2},{1,3},{2,0},{3,1},{4,6},{5,7},{6,4},{7,5},{8,10},{9,11},{10,... | collective-permute-start | bytes 884744 | tf_op jit(solution)/shard_map/ppermute | solution.py:39
  32.1 9.4 %collective-permute-start.3 = (bf16[768,192]{1,0:T(8,128)(2,1)S(1)}, bf16[768,192]{1,0:T(8,128)(2,1)S(1)}, u32[]{:S(2)}, u32[]{:S(2)}) collective-permute-start(bf16[768,192]{1,0:T(8,128)(2,1)S(1)} %get-tuple-element.202), channel_id=1, source_target_pairs={{0,2},{1,3},{2,0},{3,1},{4,6},{5,7},{6,4},{7,5},{8,10},{9,11},{10,... | collective-permute-start | bytes 884744 | tf_op jit(solution)/shard_map/ppermute | solution.py:39
  44.5 16.5 %collective-permute-start.9 = (bf16[256,768]{1,0:T(8,128)(2,1)S(1)}, bf16[256,768]{1,0:T(8,128)(2,1)S(1)}, u32[]{:S(2)}, u32[]{:S(2)}) collective-permute-start(bf16[256,768]{1,0:T(8,128)(2,1)S(1)} %pad_maximum_fusion.4), channel_id=1, source_target_pairs={{0,2},{1,3},{2,0},{3,1},{4,6},{5,7},{6,4},{7,5},{8,10},{9,11},{10,... | collective-permute-start | bytes 1179656 | tf_op jit(solution)/shard_map/ppermute | solution.py:39
  49.9 11.1 %collective-permute-start.11 = (bf16[256,768]{1,0:T(8,128)(2,1)S(1)}, bf16[256,768]{1,0:T(8,128)(2,1)S(1)}, u32[]{:S(2)}, u32[]{:S(2)}) collective-permute-start(bf16[256,768]{1,0:T(8,128)(2,1)S(1)} %collective-permute-done.2.rest_0_.rest_5_), channel_id=1, source_target_pairs={{0,8},{4,12},{8,0},{12,4},{16,24},{20,28},{24,16},{28,20},{1,9},{5... | collective-permute-start | bytes 1179656 | tf_op jit(solution)/shard_map/ppermute | solution.py:39
  50.4 10.6 %collective-permute-start.10 = (bf16[256,768]{1,0:T(8,128)(2,1)S(1)}, bf16[256,768]{1,0:T(8,128)(2,1)S(1)}, u32[]{:S(2)}, u32[]{:S(2)}) collective-permute-start(bf16[256,768]{1,0:T(8,128)(2,1)S(1)} %collective-permute-done.2.rest_0_.rest_5_), channel_id=1, source_target_pairs={{0,4},{4,0},{8,12},{12,8},{16,20},{20,16},{24,28},{28,24},{1,5},{5... | collective-permute-start | bytes 1179656 | tf_op jit(solution)/shard_map/ppermute | solution.py:39
  51.8 13.8 %collective-permute-start.12 = (bf16[768,256]{1,0:T(8,128)(2,1)S(1)}, bf16[768,256]{1,0:T(8,128)(2,1)S(1)}, u32[]{:S(2)}, u32[]{:S(2)}) collective-permute-start(bf16[768,256]{1,0:T(8,128)(2,1)S(1)} %constant_dynamic-slice_fusion.1), channel_id=1, source_target_pairs={{0,2},{1,3},{2,0},{3,1},{4,6},{5,7},{6,4},{7,5},{8,10},{9,11},{10,... | collective-permute-start | bytes 1179656 | tf_op jit(solution)/shard_map/ppermute | solution.py:39
  87.7 11.2 %collective-permute-start.17 = (bf16[256,768]{1,0:T(8,128)(2,1)S(1)}, bf16[256,768]{1,0:T(8,128)(2,1)S(1)}, u32[]{:S(2)}, u32[]{:S(2)}) collective-permute-start(bf16[256,768]{1,0:T(8,128)(2,1)S(1)} %get-tuple-element.247), channel_id=1, source_target_pairs={{0,2},{1,3},{2,0},{3,1},{4,6},{5,7},{6,4},{7,5},{8,10},{9,11},{10,... | collective-permute-start | bytes 1179656 | tf_op jit(solution)/shard_map/ppermute | solution.py:39
  88.6 10.9 %collective-permute-start.18 = (bf16[256,768]{1,0:T(8,128)(2,1)S(1)}, bf16[256,768]{1,0:T(8,128)(2,1)S(1)}, u32[]{:S(2)}, u32[]{:S(2)}) collective-permute-start(bf16[256,768]{1,0:T(8,128)(2,1)S(1)} %get-tuple-element.248), channel_id=1, source_target_pairs={{0,4},{4,0},{8,12},{12,8},{16,20},{20,16},{24,28},{28,24},{1,5},{5... | collective-permute-start | bytes 1179656 | tf_op jit(solution)/shard_map/ppermute | solution.py:39
  89.9 10.6 %collective-permute-start.19 = (bf16[256,768]{1,0:T(8,128)(2,1)S(1)}, bf16[256,768]{1,0:T(8,128)(2,1)S(1)}, u32[]{:S(2)}, u32[]{:S(2)}) collective-permute-start(bf16[256,768]{1,0:T(8,128)(2,1)S(1)} %get-tuple-element.249), channel_id=1, source_target_pairs={{0,8},{4,12},{8,0},{12,4},{16,24},{20,28},{24,16},{28,20},{1,9},{5... | collective-permute-start | bytes 1179656 | tf_op jit(solution)/shard_map/ppermute | solution.py:39
  103.9 10.9 %collective-permute-start.22 = (bf16[256,768]{1,0:T(8,128)(2,1)S(1)}, bf16[256,768]{1,0:T(8,128)(2,1)S(1)}, u32[]{:S(2)}, u32[]{:S(2)}) collective-permute-start(bf16[256,768]{1,0:T(8,128)(2,1)S(1)} %get-tuple-element.271), channel_id=1, source_target_pairs={{0,4},{4,0},{8,12},{12,8},{16,20},{20,16},{24,28},{28,24},{1,5},{5... | collective-permute-start | bytes 1179656 | tf_op jit(solution)/shard_map/ppermute | solution.py:39
  105.2 10.6 %collective-permute-start.23 = (bf16[256,768]{1,0:T(8,128)(2,1)S(1)}, bf16[256,768]{1,0:T(8,128)(2,1)S(1)}, u32[]{:S(2)}, u32[]{:S(2)}) collective-permute-start(bf16[256,768]{1,0:T(8,128)(2,1)S(1)} %get-tuple-element.272), channel_id=1, source_target_pairs={{0,8},{4,12},{8,0},{12,4},{16,24},{20,28},{24,16},{28,20},{1,9},{5... | collective-permute-start | bytes 1179656 | tf_op jit(solution)/shard_map/ppermute | solution.py:39
  110.3 10.4 %collective-permute-start.24 = (bf16[768,192]{1,0:T(8,128)(2,1)S(1)}, bf16[768,192]{1,0:T(8,128)(2,1)S(1)}, u32[]{:S(2)}, u32[]{:S(2)}) collective-permute-start(bf16[768,192]{1,0:T(8,128)(2,1)S(1)} %get-tuple-element.293), channel_id=1, source_target_pairs={{0,2},{1,3},{2,0},{3,1},{4,6},{5,7},{6,4},{7,5},{8,10},{9,11},{10,... | collective-permute-start | bytes 884744 | tf_op jit(solution)/shard_map/ppermute | solution.py:39
  120.7 15.9 %collective-permute-start.26 = (bf16[448,768]{1,0:T(8,128)(2,1)}, bf16[448,768]{1,0:T(8,128)(2,1)S(1)}, u32[]{:S(2)}, u32[]{:S(2)}) collective-permute-start(bf16[448,768]{1,0:T(8,128)(2,1)} %get-tuple-element.301), channel_id=1, source_target_pairs={{0,4},{4,0},{8,12},{12,8},{16,20},{20,16},{24,28},{28,24},{1,5},{5... | collective-permute-start | bytes 2064392 | tf_op jit(solution)/shard_map/ppermute | solution.py:39
  121.4 15.9 %collective-permute-start.27 = (bf16[448,768]{1,0:T(8,128)(2,1)}, bf16[448,768]{1,0:T(8,128)(2,1)S(1)}, u32[]{:S(2)}, u32[]{:S(2)}) collective-permute-start(bf16[448,768]{1,0:T(8,128)(2,1)} %get-tuple-element.302), channel_id=1, source_target_pairs={{0,8},{4,12},{8,0},{12,4},{16,24},{20,28},{24,16},{28,20},{1,9},{5... | collective-permute-start | bytes 2064392 | tf_op jit(solution)/shard_map/ppermute | solution.py:39
  123.0 13.6 %collective-permute-start.25 = (bf16[384,768]{1,0:T(8,128)(2,1)}, bf16[384,768]{1,0:T(8,128)(2,1)S(1)}, u32[]{:S(2)}, u32[]{:S(2)}) collective-permute-start(bf16[384,768]{1,0:T(8,128)(2,1)} %get-tuple-element.300), channel_id=1, source_target_pairs={{0,2},{1,3},{2,0},{3,1},{4,6},{5,7},{6,4},{7,5},{8,10},{9,11},{10,... | collective-permute-start | bytes 1769480 | tf_op jit(solution)/shard_map/ppermute | solution.py:39
  140.6 14.3 %collective-permute-start.30 = (bf16[288,768]{1,0:T(8,128)(2,1)}, bf16[288,768]{1,0:T(8,128)(2,1)S(1)}, u32[]{:S(2)}, u32[]{:S(2)}) collective-permute-start(bf16[288,768]{1,0:T(8,128)(2,1)} %get-tuple-element.326), channel_id=1, source_target_pairs={{0,4},{4,0},{8,12},{12,8},{16,20},{20,16},{24,28},{28,24},{1,5},{5... | collective-permute-start | bytes 1327112 | tf_op jit(solution)/shard_map/ppermute | solution.py:39
  141.6 13.4 %collective-permute-start.31 = (bf16[320,768]{1,0:T(8,128)(2,1)}, bf16[320,768]{1,0:T(8,128)(2,1)S(1)}, u32[]{:S(2)}, u32[]{:S(2)}) collective-permute-start(bf16[320,768]{1,0:T(8,128)(2,1)} %get-tuple-element.327), channel_id=1, source_target_pairs={{0,8},{4,12},{8,0},{12,4},{16,24},{20,28},{24,16},{28,20},{1,9},{5... | collective-permute-start | bytes 1474568 | tf_op jit(solution)/shard_map/ppermute | solution.py:39
  143.2 11.6 %collective-permute-start.28 = (bf16[96,768]{1,0:T(8,128)(2,1)S(1)}, bf16[96,768]{1,0:T(8,128)(2,1)S(1)}, u32[]{:S(2)}, u32[]{:S(2)}) collective-permute-start(bf16[96,768]{1,0:T(8,128)(2,1)S(1)} %constant_dynamic-slice_fusion), channel_id=1, source_target_pairs={{0,16},{4,20},{8,24},{12,28},{16,0},{20,4},{24,8},{28,12},{1,17},{... | collective-permute-start | bytes 442376 | tf_op jit(solution)/shard_map/ppermute | solution.py:39
  155.7 14.4 %collective-permute-start.33 = (bf16[784,768]{1,0:T(8,128)(2,1)}, bf16[784,768]{1,0:T(8,128)(2,1)S(1)}, u32[]{:S(2)}, u32[]{:S(2)}) collective-permute-start(bf16[784,768]{1,0:T(8,128)(2,1)} %get-tuple-element.338), channel_id=1, source_target_pairs={{0,1},{1,0},{2,3},{3,2},{4,5},{5,4},{6,7},{7,6},{8,9},{9,8},{10,11... | collective-permute-start | bytes 3612680 | tf_op jit(solution)/shard_map/ppermute | solution.py:39
  155.7 10.6 %collective-permute-start.32 = (bf16[96,768]{1,0:T(8,128)(2,1)S(1)}, bf16[96,768]{1,0:T(8,128)(2,1)}, u32[]{:S(2)}, u32[]{:S(2)}) collective-permute-start(bf16[96,768]{1,0:T(8,128)(2,1)S(1)} %add_convert_fusion.2), channel_id=1, source_target_pairs={{0,16},{4,20},{8,24},{12,28},{16,0},{20,4},{24,8},{28,12},{1,17},{... | collective-permute-start | bytes 442376 | tf_op jit(solution)/shard_map/ppermute | solution.py:39
  172.0 9.9 %collective-permute-start.41 = (bf16[64,768]{1,0:T(8,128)(2,1)S(1)}, bf16[64,768]{1,0:T(8,128)(2,1)S(1)}, u32[]{:S(2)}, u32[]{:S(2)}) collective-permute-start(bf16[64,768]{1,0:T(8,128)(2,1)S(1)} %slice.69), channel_id=1, source_target_pairs={{0,4},{4,0},{8,12},{12,8},{16,20},{20,16},{24,28},{28,24},{1,5},{5... | collective-permute-start | bytes 294920 | tf_op jit(solution)/shard_map/ppermute | solution.py:39
  173.1 18.6 %collective-permute-start.37 = (bf16[224,768]{1,0:T(8,128)(2,1)S(1)}, bf16[224,768]{1,0:T(8,128)(2,1)S(1)}, u32[]{:S(2)}, u32[]{:S(2)}) collective-permute-start(bf16[224,768]{1,0:T(8,128)(2,1)S(1)} %fusion), channel_id=1, source_target_pairs={{0,16},{4,20},{8,24},{12,28},{16,0},{20,4},{24,8},{28,12},{1,17},{... | collective-permute-start | bytes 1032200 | tf_op jit(solution)/shard_map/ppermute | solution.py:39
  178.1 14.6 %collective-permute-start.38 = (bf16[392,768]{1,0:T(8,128)(2,1)S(1)}, bf16[392,768]{1,0:T(8,128)(2,1)S(1)}, u32[]{:S(2)}, u32[]{:S(2)}) collective-permute-start(bf16[392,768]{1,0:T(8,128)(2,1)S(1)} %get-tuple-element.351), channel_id=1, source_target_pairs={{0,2},{1,3},{2,0},{3,1},{4,6},{5,7},{6,4},{7,5},{8,10},{9,11},{10,... | collective-permute-start | bytes 1806344 | tf_op jit(solution)/shard_map/ppermute | solution.py:39
  179.8 12.8 %collective-permute-start.40 = (bf16[256,768]{1,0:T(8,128)(2,1)S(1)}, bf16[256,768]{1,0:T(8,128)(2,1)S(1)}, u32[]{:S(2)}, u32[]{:S(2)}) collective-permute-start(bf16[256,768]{1,0:T(8,128)(2,1)S(1)} %pad_maximum_fusion.5), channel_id=1, source_target_pairs={{0,4},{4,0},{8,12},{12,8},{16,20},{20,16},{24,28},{28,24},{1,5},{5... | collective-permute-start | bytes 1179656 | tf_op jit(solution)/shard_map/ppermute | solution.py:39
  181.9 10.8 %collective-permute-start.42 = (bf16[128,768]{1,0:T(8,128)(2,1)S(1)}, bf16[128,768]{1,0:T(8,128)(2,1)S(1)}, u32[]{:S(2)}, u32[]{:S(2)}) collective-permute-start(bf16[128,768]{1,0:T(8,128)(2,1)S(1)} %pad_maximum_fusion.8), channel_id=1, source_target_pairs={{0,8},{4,12},{8,0},{12,4},{16,24},{20,28},{24,16},{28,20},{1,9},{5... | collective-permute-start | bytes 589832 | tf_op jit(solution)/shard_map/ppermute | solution.py:39
  192.7 21.2 %collective-permute-start.44 = (bf16[224,768]{1,0:T(8,128)(2,1)}, bf16[224,768]{1,0:T(8,128)(2,1)}, u32[]{:S(2)}, u32[]{:S(2)}) collective-permute-start(bf16[224,768]{1,0:T(8,128)(2,1)} %add_convert_fusion.1), channel_id=1, source_target_pairs={{0,16},{4,20},{8,24},{12,28},{16,0},{20,4},{24,8},{28,12},{1,17},{... | collective-permute-start | bytes 1032200 | tf_op jit(solution)/shard_map/ppermute | solution.py:39
  204.1 9.7 %collective-permute-start.47 = (f32[10,768]{1,0:T(8,128)S(1)}, f32[10,768]{1,0:T(8,128)S(1)}, u32[]{:S(2)}, u32[]{:S(2)}) collective-permute-start(f32[10,768]{1,0:T(8,128)S(1)} %add.87), channel_id=1, source_target_pairs={{0,16},{4,20},{8,24},{12,28},{16,0},{20,4},{24,8},{28,12},{1,17},{... | collective-permute-start | bytes 92168 | tf_op jit(solution)/shard_map/ppermute | solution.py:39
  206.1 9.9 %collective-permute-start.43 = (bf16[768,256]{1,0:T(8,128)(2,1)}, bf16[768,256]{1,0:T(8,128)(2,1)S(1)}, u32[]{:S(2)}, u32[]{:S(2)}) collective-permute-start(bf16[768,256]{1,0:T(8,128)(2,1)} %copy-done.9), channel_id=1, source_target_pairs={{0,2},{1,3},{2,0},{3,1},{4,6},{5,7},{6,4},{7,5},{8,10},{9,11},{10,... | collective-permute-start | bytes 1179656 | tf_op jit(solution)/shard_map/ppermute | solution.py:39
  223.6 15.1 %collective-permute-start.51 = (bf16[448,768]{1,0:T(8,128)(2,1)S(1)}, bf16[448,768]{1,0:T(8,128)(2,1)S(1)}, u32[]{:S(2)}, u32[]{:S(2)}) collective-permute-start(bf16[448,768]{1,0:T(8,128)(2,1)S(1)} %pad_maximum_fusion.2), channel_id=1, source_target_pairs={{0,8},{4,12},{8,0},{12,4},{16,24},{20,28},{24,16},{28,20},{1,9},{5... | collective-permute-start | bytes 2064392 | tf_op jit(solution)/shard_map/ppermute | solution.py:39
  225.1 15.1 %collective-permute-start.50 = (bf16[448,768]{1,0:T(8,128)(2,1)S(1)}, bf16[448,768]{1,0:T(8,128)(2,1)S(1)}, u32[]{:S(2)}, u32[]{:S(2)}) collective-permute-start(bf16[448,768]{1,0:T(8,128)(2,1)S(1)} %pad_maximum_fusion.1), channel_id=1, source_target_pairs={{0,4},{4,0},{8,12},{12,8},{16,20},{20,16},{24,28},{28,24},{1,5},{5... | collective-permute-start | bytes 2064392 | tf_op jit(solution)/shard_map/ppermute | solution.py:39
  (57 other events, 319.7 us)

commit v3 on v2

--- a/solution.py
+++ b/solution.py
@@ -1001,17 +1001,16 @@
     low_part = swap(low_quarter(mine), "mp", 2)
 
     normed, q, k, v, lse, near, other = attend(lengths, rows2d, vecs, *weights, items, seq)
-    out_far, near, other, up_part, low_part = join(out_far, near, other, up_part, low_part)
+    out_far, near, other, up_part = join(out_far, near, other, up_part)
     far = swap(other, "mp", 2)
-    up_parts = [up_part, swap(up_part, "dp", 1), swap(up_part, "dp", 2)]
     cot_rows = cotangent.reshape(rows, -1)
     cot_sent = lax.dynamic_slice_in_dim(cot_rows, (1 - chip) * span, span, 0)
     low_sent = low_quarter(mine ^ 3)
+    up_part, low_sent = join(up_part, low_sent)
+    up_parts = [up_part, swap(up_part, "dp", 1), swap(up_part, "dp", 2)]
     last_half = quarter // 2
     turned = [up_parts[2][:last_half], up_parts[1][last_half:]]
-    far, low_part, low_sent, cot_sent, turned[0], turned[1], *up_parts = join(
-        far, low_part, low_sent, cot_sent, *turned, *up_parts
-    )
+    far, low_sent, cot_sent, turned[0], turned[1], *up_parts = join(far, low_sent, cot_sent, *turned, *up_parts)
     low_last = swap(low_sent, "mp", 2)
     up_parts.append(swap(turned[0], "dp", 1))
     up_parts.append(swap(turned[1], "dp", 2))
@@ -1086,15 +1085,17 @@
     came = {link: in_hbm(value)[0] for link, value in came.items()}
     sends, kept, early = turn("turn_four", kept, came, [None, None] + list("zyxxzx"), width)
     came = send_all(sends)
-    first, got, vol_far, came["y"], came["x"], came["z"] = join(first, got, vol_far, came["y"], came["x"], came["z"])
+    edge = sizes[0] + sizes[1]
+    sent_near = [first[:edge], first[edge:]]
+    sent_near[0], sent_near[1], first, got, vol_far, came["y"], came["x"], came["z"] = join(
+        *sent_near, first, got, vol_far, came["y"], came["x"], came["z"]
+    )
     kept = [kept[i] for i in (0, 1, 4, 2, 3, 5)]
     unused, unused, last = turn("turn_five", kept, came, [None] * 6, width)
     last_sizes = [k.blocks * k.rows for k in kept] + conv_sizes
     last = jnp.concatenate([last, early], axis=0)
     for bit in late_bits():
         last = finish_reduce(last, bit)
-    edge = sizes[0] + sizes[1]
-    sent_near = [first[:edge], first[edge:]]
     near_got = [swap(sent_near[0], "dp", 2), swap(sent_near[1], "dp", 1)]
     second, whole = pass_on(passed, got, own_sums, up_sums)
     second = swap(second, "mp", 2)

time: 244 us -> 243 us (level)
  waiting for transfers between devices: 74.4 us -> 87.6 us
  starting transfers between devices: 60.9 us -> 48.3 us
  local copies, waits for them, and re-layouts: 12.2 us -> 8.58 us
    ppermute x52, waiting for transfers between devices: 74.4 us -> 87.6 us  [swap(): return lax.ppermute(value, axis, [(i, i ^ bit) for i in range(size)])]
    ppermute x52, starting transfers between devices: 60.9 us -> 48.3 us  [swap(): return lax.ppermute(value, axis, [(i, i ^ bit) for i in range(size)])]
  transfers between devices with their start and end apart: 52 -> 52, of which waited for: 32 -> 35; matrix products, arithmetic and copies ran while one was open for 6% -> 6% of each run, Pallas kernels for 28% -> 28%
where the time goes in v3:
time: 243 us; the launch traced here: 241 us
  waiting for transfers between devices  87.6 us (36%)
  Pallas kernels  86.5 us (36%)
  starting transfers between devices  48.3 us (20%)
  other arithmetic  8.74 us (4%)
  local copies, waits for them, and re-layouts  8.58 us (4%)
    ppermute x52, waiting for transfers between devices, swap(): return lax.ppermute(value, axis, [(i, i ^ bit) for i in range(size)])  87.6 us
    ppermute x52, starting transfers between devices, swap(): return lax.ppermute(value, axis, [(i, i ^ bit) for i in range(size)])  48.3 us
    pallas_call x1, Pallas kernels, attend_back(): pl.pallas_call(functools.partial(attend_back_kernel, items, heads, share)...  11.2 us
    pallas_call x1, Pallas kernels, attend(): pl.pallas_call(functools.partial(attend_kernel, items, heads, rows // 2),...  10.8 us
    pallas_call x6, Pallas kernels, emit(): pl.pallas_call(functools.partial(emit_kernel, len(lefts), len(inputs), la...  10.3 us
    pallas_call x1, Pallas kernels, normed_back(): pl.pallas_call(functools.partial(normed_back_kernel, items, share), out_s...  8.03 us
    pallas_call x1, Pallas kernels, expand(): pl.pallas_call(expand_kernel, out_shape=[shape((span, width), F32), shape...  7.63 us
    pallas_call x1, Pallas kernels, mlp_back(): pl.pallas_call(mlp_back_kernel, out_shape=[shape((2, span, width), BF16),...  6.58 us
  transfers between devices with their start and end apart: 52, of which 35 were waited for; matrix products, arithmetic and copies ran while one was open for 6% of the time, Pallas kernels for 28%

profile of v3, /device:TPU:0, one launch (start us, length us, event | category | flops | bytes accessed | tf_op | source)
XLA Modules:
  0.0 241.1 jit_solution(9581195941613563830)
XLA Ops:
  1.8 3.0 %collective-permute-start.1 = (bf16[192,768]{1,0:T(8,128)(2,1)S(1)}, bf16[192,768]{1,0:T(8,128)(2,1)}, u32[]{:S(2)}, u32[]{:S(2)}) collective-permute-start(bf16[192,768]{1,0:T(8,128)(2,1)S(1)} %constant_dynamic-slice_fusion.4), channel_id=1, source_target_pairs={{0,2},{1,3},{2,0},{3,1},{4,6},{5,7},{6,4},{7,5},{8,10},{9,11},{10,... | collective-permute-start | bytes 884744 | tf_op jit(solution)/shard_map/ppermute | solution.py:39
  10.3 10.8 %attend.1 = (bf16[1536,768]{1,0:T(8,128)(2,1)}, bf16[1536,192]{1,0:T(8,128)(2,1)}, bf16[1536,192]{1,0:T(8,128)(2,1)}, bf16[1536,192]{1,0:T(8,128)(2,1)}, f32[3,8...) custom-call(s32[3]{0:T(128)S(1)} %copy-done.7, bf16[1536,768]{1,0:T(8,128)(2,1)} %bitcast.20, ...), custom_call_target="tpu_custom_call" | custom-call | flops 1962934272 | bytes 4718592 | tf_op jit(solution)/shard_map/attend/pallas_call | solution.py:171
  21.1 2.8 %collective-permute-start.4 = (bf16[192,768]{1,0:T(8,128)(2,1)}, bf16[192,768]{1,0:T(8,128)(2,1)S(1)}, u32[]{:S(2)}, u32[]{:S(2)}) collective-permute-start(bf16[192,768]{1,0:T(8,128)(2,1)} %collective-permute-done.1.rest_0_), channel_id=1, source_target_pairs={{0,4},{4,0},{8,12},{12,8},{16,20},{20,16},{24,28},{28,24},{1,5},{5... | collective-permute-start | bytes 884744 | tf_op jit(solution)/shard_map/ppermute | solution.py:39
  27.1 3.5 %collective-permute-done.4.rest_1_ = bf16[192,768]{1,0:T(8,128)(2,1)S(1)} collective-permute-done((bf16[192,768]{1,0:T(8,128)(2,1)}, bf16[192,768]{1,0:T(8,128)(2,1)S(1)}, u32[]{:S(2)}, u32[]{:S(2)}) %collective-permute-start.4) | collective-permute-done | bytes 294944 | tf_op jit(solution)/shard_map/ppermute | solution.py:39
  32.1 3.2 %collective-permute-done.2.far_ref.refs_1_ = bf16[768,192]{1,0:T(8,128)(2,1)S(1)} collective-permute-done((bf16[768,192]{1,0:T(8,128)(2,1)S(1)}, bf16[768,192]{1,0:T(8,128)(2,1)S(1)}, u32[]{:S(2)}, u32[]{:S(2)}) %collective-permute-start.2) | collective-permute-done | bytes 294944 | tf_op jit(solution)/shard_map/ppermute | solution.py:39
  40.0 9.1 %collective-permute-done.6.rest_0_.rest_5_ = bf16[256,768]{1,0:T(8,128)(2,1)S(1)} collective-permute-done((bf16[256,768]{1,0:T(8,128)(2,1)S(1)}, bf16[256,768]{1,0:T(8,128)(2,1)S(1)}, u32[]{:S(2)}, u32[]{:S(2)}) %collective-permute-start.6) | collective-permute-done | bytes 393248 | tf_op jit(solution)/shard_map/ppermute | solution.py:39
  51.5 7.6 %expand.1 = (f32[768,768]{1,0:T(8,128)S(1)}, bf16[768,768]{1,0:T(8,128)(2,1)S(1)}, bf16[2,768,768]{2,1,0:T(8,128)(2,1)S(1)}, bf16[2,768,768]{2,1,0:T(8,128)(2,1)S(1)}) custom-call(bf16[1536,768]{1,0:T(8,128)(2,1)} %bitcast.21, f32[8,768]{1,0:T(8,128)} %reshape.57.vec_ref.norm_ref, bf16[768,768]{1,0:T(8,128)(2,1)S(1)} %project.1.part_ref, ...), custom_call_target="tpu_custom_call" | custom-call | flops 1811939328 | bytes 8257536 | tf_op jit(solution)/shard_map/expand/pallas_call | solution.py:442
  60.4 3.6 %contract.1.part_ref = bf16[768,768]{1,0:T(8,128)(2,1)S(1)} custom-call(bf16[2,768,768]{2,1,0:T(8,128)(2,1)S(1)} %get-tuple-element.225.act_ref.refs_0_, bf16[768,768]{1,0:T(8,128)(2,1)} %down_ref.3, bf16[256,768]{1,0:T(8,128)(2,1)} %copy-done.13, bf16[256,768]{1,0:T(8,128)(2,1)} %copy-done.16, bf16[256,768]{1,0:T(8,128)(2,1)} %copy-done.15, ...), custom_call_target="tpu_custom_call" | custom-call | flops 1811939328 | bytes 4718592 | tf_op jit(solution)/shard_map/contract/pallas_call | solution.py:472
  65.6 2.8 %collective-permute-done.13.other_ref = bf16[768,768]{1,0:T(8,128)(2,1)S(1)} collective-permute-done((bf16[768,768]{1,0:T(8,128)(2,1)S(1)}, bf16[768,768]{1,0:T(8,128)(2,1)S(1)}, u32[]{:S(2)}, u32[]{:S(2)}) %collective-permute-start.13) | collective-permute-done | bytes 1179680 | tf_op jit(solution)/shard_map/ppermute | solution.py:39
  68.4 4.7 %convolve.1 = (bf16[768,768]{1,0:T(8,128)(2,1)S(1)}, f32[2,768,256]{2,1,0:T(8,128)S(1)}, f32[3,4,128]{2,1,0:T(4,128)S(1)}) custom-call(s32[3]{0:T(128)S(1)} %copy-done.7, f32[8,768]{1,0:T(8,128)} %reshape.57.vec_ref.norm_ref, f32[768,768]{1,0:T(8,128)S(1)} %get-tuple-element.226.mid_ref, bf16[768,768]{1,0:T(8,128)(2,1)S(1)} %contract.1.part_ref, ...), custom_call_target="tpu_custom_call" | custom-call | flops 603979776 | bytes 8257536 | tf_op jit(solution)/shard_map/convolve/pallas_call | solution.py:524
  78.0 3.9 %norm_back.1 = (bf16[768,256]{1,0:T(8,128)(2,1)S(1)}, bf16[768,256]{1,0:T(8,128)(2,1)S(1)}, bf16[2,768,256]{2,1,0:T(8,128)(2,1)S(1)}, bf16[768,768]{1,0:T(8,128)(2,1)S(1)}, f32[8,768]{1,0:T(8,128)S(1)}) custom-call(s32[3]{0:T(128)S(1)} %copy-done.7, f32[8,768]{1,0:T(8,128)} %reshape.57.vec_ref.norm_ref, f32[3,4,128]{2,1,0:T(4,128)S(1)} %add.76.tot_ref, ...), custom_call_target="tpu_custom_call" | custom-call | flops 603979776 | bytes 3538944 | tf_op jit(solution)/shard_map/norm_back/pallas_call | solution.py:584
  85.2 2.4 down_grad.1
  89.9 6.6 %mlp_back.1 = (bf16[2,768,768]{2,1,0:T(8,128)(2,1)S(1)}, bf16[768,768]{1,0:T(8,128)(2,1)S(1)}, f32[8,768]{1,0:T(8,128)S(1)}, f32[2,8,768]{2,1,0:T(8,128)S(1)}) custom-call(bf16[768,768]{1,0:T(8,128)(2,1)S(1)} %get-tuple-element.236.part_ref, bf16[768,768]{1,0:T(8,128)(2,1)S(1)} %collective-permute-done.16.other_ref, ...), custom_call_target="tpu_custom_call" | custom-call | flops 3623878656 | bytes 11796480 | tf_op jit(solution)/shard_map/mlp_back/pallas_call | solution.py:637
  96.5 2.2 collective-permute-done.17.refs_3_
  105.5 3.4 %mid_back.1 = (bf16[768,192]{1,0:T(8,128)(2,1)S(1)}, bf16[768,192]{1,0:T(8,128)(2,1)S(1)}, bf16[768,768]{1,0:T(8,128)(2,1)S(1)}, f32[384,768]{1,0:T(8,128)S(1)}, f32[8,768]{1,0:T(8,128)S(1)}) custom-call(f32[8,768]{1,0:T(8,128)S(1)} %copy-done.4, f32[768,768]{1,0:T(8,128)S(1)} %get-tuple-element.226.mid_ref, ...), custom_call_target="tpu_custom_call" | custom-call | flops 452984832 | bytes 7077888 | tf_op jit(solution)/shard_map/mid_back/pallas_call | solution.py:682
  111.3 3.1 %collective-permute-done.22.refs_6_ = bf16[256,768]{1,0:T(8,128)(2,1)S(1)} collective-permute-done((bf16[256,768]{1,0:T(8,128)(2,1)S(1)}, bf16[256,768]{1,0:T(8,128)(2,1)S(1)}, u32[]{:S(2)}, u32[]{:S(2)}) %collective-permute-start.22) | collective-permute-done | bytes 393248 | tf_op jit(solution)/shard_map/ppermute | solution.py:39
  115.7 2.3 turn_two.1
  118.0 2.2 collective-permute-done.24.other_ref
  123.2 11.2 %attend_back.1 = (bf16[1536,192]{1,0:T(8,128)(2,1)}, bf16[1536,192]{1,0:T(8,128)(2,1)}, bf16[1536,192]{1,0:T(8,128)(2,1)}, bf16[576,768]{1,0:T(8,128)(2,1)S(1)}, f32[8,768]{1,0:T(8,128)S(1)}) custom-call(s32[3]{0:T(128)S(1)} %copy-done.7, bf16[1536,768]{1,0:T(8,128)(2,1)} %get-tuple-element.289.normed_ref, bf16[1536,192]{1,0:T(8,128)(2,1)} %get-tuple-element.290.q_ref, ...), custom_call_target="tpu_custom_call" | custom-call | flops 2868903936 | bytes 9437184 | tf_op jit(solution)/shard_map/attend_back/pallas_call | solution.py:251
  137.6 3.2 %turn_three.1 = (bf16[224,768]{1,0:T(8,128)(2,1)S(1)}, bf16[288,768]{1,0:T(8,128)(2,1)}, bf16[320,768]{1,0:T(8,128)(2,1)}, bf16[32,768]{1,0:T(8,128)(2,1)}, bf16...) custom-call(bf16[64,768]{1,0:T(8,128)(2,1)} %get-tuple-element.280.r, ...), custom_call_target="tpu_custom_call" | custom-call | tf_op jit(solution)/shard_map/turn_three/pallas_call | solution.py:812
  144.5 8.0 %normed_back.1 = (bf16[784,768]{1,0:T(8,128)(2,1)}, f32[384,768]{1,0:T(8,128)}, f32[384,768]{1,0:T(8,128)}, f32[8,768]{1,0:T(8,128)S(1)}) custom-call(s32[3]{0:T(128)S(1)} %copy-done.7, bf16[1536,768]{1,0:T(8,128)(2,1)} %bitcast.22, bf16[1536,192]{1,0:T(8,128)(2,1)} %get-tuple-element.321.dq_ref, bf16[1536,192]{1,0:T(8,128)(2,1)} %get-tuple-element.322.dk_ref, ...), custom_call_target="tpu_custom_call" | custom-call | flops 1358954496 | bytes 9437184 | tf_op jit(solution)/shard_map/normed_back/pallas_call | solution.py:329
  155.6 2.2 collective-permute-start.32
  162.1 4.0 %collective-permute-done.32 = bf16[96,768]{1,0:T(8,128)(2,1)} collective-permute-done((bf16[96,768]{1,0:T(8,128)(2,1)S(1)}, bf16[96,768]{1,0:T(8,128)(2,1)}, u32[]{:S(2)}, u32[]{:S(2)}) %collective-permute-start.32) | collective-permute-done | bytes 147488 | tf_op jit(solution)/shard_map/ppermute | solution.py:39
  175.4 2.3 collective-permute-done.39.refs_1_
  181.7 7.8 %collective-permute-done.37 = bf16[224,768]{1,0:T(8,128)(2,1)S(1)} collective-permute-done((bf16[224,768]{1,0:T(8,128)(2,1)S(1)}, bf16[224,768]{1,0:T(8,128)(2,1)S(1)}, u32[]{:S(2)}, u32[]{:S(2)}) %collective-permute-start.37) | collective-permute-done | bytes 344096 | tf_op jit(solution)/shard_map/ppermute | solution.py:39
  192.8 3.9 %collective-permute-done.45 = f32[10,768]{1,0:T(8,128)S(1)} collective-permute-done((f32[10,768]{1,0:T(8,128)S(1)}, f32[10,768]{1,0:T(8,128)S(1)}, u32[]{:S(2)}, u32[]{:S(2)}) %collective-permute-start.45) | collective-permute-done | bytes 30752 | tf_op jit(solution)/shard_map/ppermute | solution.py:39
  197.7 3.2 %collective-permute-done.46 = f32[10,768]{1,0:T(8,128)S(1)} collective-permute-done((f32[10,768]{1,0:T(8,128)S(1)}, f32[10,768]{1,0:T(8,128)S(1)}, u32[]{:S(2)}, u32[]{:S(2)}) %collective-permute-start.46) | collective-permute-done | bytes 30752 | tf_op jit(solution)/shard_map/ppermute | solution.py:39
  200.9 3.0 %collective-permute-start.47 = (f32[10,768]{1,0:T(8,128)S(1)}, f32[10,768]{1,0:T(8,128)S(1)}, u32[]{:S(2)}, u32[]{:S(2)}) collective-permute-start(f32[10,768]{1,0:T(8,128)S(1)} %add.87), channel_id=1, source_target_pairs={{0,16},{4,20},{8,24},{12,28},{16,0},{20,4},{24,8},{28,12},{1,17},{... | collective-permute-start | bytes 92168 | tf_op jit(solution)/shard_map/ppermute | solution.py:39
  205.1 4.8 %finish.1 = f32[384,768]{1,0:T(8,128)} custom-call(bf16[1536,768]{1,0:T(8,128)(2,1)} %bitcast.23, f32[8,768]{1,0:T(8,128)} %reshape.57.vec_ref.norm_ref, f32[384,768]{1,0:T(8,128)} %get-tuple-element.367.own_ref, bf16[784,768]{1,0:T(8,128)(2,1)S(1)} %collective-permute-done.33.got_ref, bf16[392,768]{1,0:T(8,128)(2,1)S(1)} %collective-permute-done.38.last_ref, ...), custom_call_target="tpu_custom_call" | custom-call | bytes 4128768 | tf_op jit(solution)/shard_map/finish/pallas_call | solution.py:923
  216.1 6.1 %collective-permute-done.49.refs_3_ = bf16[224,768]{1,0:T(8,128)(2,1)S(1)} collective-permute-done((bf16[224,768]{1,0:T(8,128)(2,1)S(1)}, bf16[224,768]{1,0:T(8,128)(2,1)S(1)}, u32[]{:S(2)}, u32[]{:S(2)}) %collective-permute-start.49) | collective-permute-done | bytes 344096 | tf_op jit(solution)/shard_map/ppermute | solution.py:39
  226.2 11.9 %collective-permute-done.51.refs_4_ = bf16[448,768]{1,0:T(8,128)(2,1)S(1)} collective-permute-done((bf16[448,768]{1,0:T(8,128)(2,1)S(1)}, bf16[448,768]{1,0:T(8,128)(2,1)S(1)}, u32[]{:S(2)}, u32[]{:S(2)}) %collective-permute-start.51) | collective-permute-done | bytes 688160 | tf_op jit(solution)/shard_map/ppermute | solution.py:39
  238.1 3.0 %spread_two.1 = (f32[768,768]{1,0:T(8,128)}, f32[192,768]{1,0:T(8,128)}, f32[192,768]{1,0:T(8,128)}, f32[192,768]{1,0:T(8,128)}, f32[192,768]{1,0:T(8,128)}, /*index=5*/f32[768,256]{1,0:T(8,128)}) custom-call(bf16[448,768]{1,0:T(8,128)(2,1)S(1)} %pad_maximum_fusion.refs_0_, bf16[224,768]{1,0:T(8,128)(2,1)S(1)} %collective-permute-done.48.refs_1_, ...), custom_call_target="tpu_custom_call" | custom-call | bytes 11010048 | tf_op jit(solution)/shard_map/spread_two/pallas_call | solution.py:875
  (229 shorter events, 87.8 us)
Async XLA Ops:
  1.8 19.3 %collective-permute-start.1 = (bf16[192,768]{1,0:T(8,128)(2,1)S(1)}, bf16[192,768]{1,0:T(8,128)(2,1)}, u32[]{:S(2)}, u32[]{:S(2)}) collective-permute-start(bf16[192,768]{1,0:T(8,128)(2,1)S(1)} %constant_dynamic-slice_fusion.4), channel_id=1, source_target_pairs={{0,2},{1,3},{2,0},{3,1},{4,6},{5,7},{6,4},{7,5},{8,10},{9,11},{10,... | collective-permute-start | bytes 884744 | tf_op jit(solution)/shard_map/ppermute | solution.py:39
  6.7 14.4 %collective-permute-start = (bf16[208,768]{1,0:T(8,128)(2,1)S(1)}, bf16[208,768]{1,0:T(8,128)(2,1)S(1)}, u32[]{:S(2)}, u32[]{:S(2)}) collective-permute-start(bf16[208,768]{1,0:T(8,128)(2,1)S(1)} %pad_maximum_fusion.7), channel_id=1, source_target_pairs={{0,2},{1,3},{2,0},{3,1},{4,6},{5,7},{6,4},{7,5},{8,10},{9,11},{10,... | collective-permute-start | bytes 958472 | tf_op jit(solution)/shard_map/ppermute | solution.py:39
  37.0 12.1 %collective-permute-start.5 = (bf16[768,768]{1,0:T(8,128)(2,1)S(1)}, bf16[768,768]{1,0:T(8,128)(2,1)S(1)}, u32[]{:S(2)}, u32[]{:S(2)}) collective-permute-start(bf16[768,768]{1,0:T(8,128)(2,1)S(1)} %project.1.part_ref), channel_id=1, source_target_pairs={{0,1},{1,0},{2,3},{3,2},{4,5},{5,4},{6,7},{7,6},{8,9},{9,8},{10,11... | collective-permute-start | bytes 3538952 | tf_op jit(solution)/shard_map/ppermute | solution.py:39
  37.1 12.0 %collective-permute-start.6 = (bf16[256,768]{1,0:T(8,128)(2,1)S(1)}, bf16[256,768]{1,0:T(8,128)(2,1)S(1)}, u32[]{:S(2)}, u32[]{:S(2)}) collective-permute-start(bf16[256,768]{1,0:T(8,128)(2,1)S(1)} %pad_maximum_fusion.4), channel_id=1, source_target_pairs={{0,2},{1,3},{2,0},{3,1},{4,6},{5,7},{6,4},{7,5},{8,10},{9,11},{10,... | collective-permute-start | bytes 1179656 | tf_op jit(solution)/shard_map/ppermute | solution.py:39
  38.7 10.4 %collective-permute-start.7 = (bf16[96,768]{1,0:T(8,128)(2,1)S(1)}, bf16[96,768]{1,0:T(8,128)(2,1)S(1)}, u32[]{:S(2)}, u32[]{:S(2)}) collective-permute-start(bf16[96,768]{1,0:T(8,128)(2,1)S(1)} %slice.88), channel_id=1, source_target_pairs={{0,4},{4,0},{8,12},{12,8},{16,20},{20,16},{24,28},{28,24},{1,5},{5... | collective-permute-start | bytes 442376 | tf_op jit(solution)/shard_map/ppermute | solution.py:39
  39.5 19.7 %collective-permute-start.9 = (bf16[256,768]{1,0:T(8,128)(2,1)S(1)}, bf16[256,768]{1,0:T(8,128)(2,1)S(1)}, u32[]{:S(2)}, u32[]{:S(2)}) collective-permute-start(bf16[256,768]{1,0:T(8,128)(2,1)S(1)} %copy-done.23), channel_id=1, source_target_pairs={{0,2},{1,3},{2,0},{3,1},{4,6},{5,7},{6,4},{7,5},{8,10},{9,11},{10,... | collective-permute-start | bytes 1179656 | tf_op jit(solution)/shard_map/ppermute | solution.py:39
  49.1 10.4 %collective-permute-start.11 = (bf16[256,768]{1,0:T(8,128)(2,1)S(1)}, bf16[256,768]{1,0:T(8,128)(2,1)S(1)}, u32[]{:S(2)}, u32[]{:S(2)}) collective-permute-start(bf16[256,768]{1,0:T(8,128)(2,1)S(1)} %collective-permute-done.6.rest_0_.rest_5_), channel_id=1, source_target_pairs={{0,8},{4,12},{8,0},{12,4},{16,24},{20,28},{24,16},{28,20},{1,9},{5... | collective-permute-start | bytes 1179656 | tf_op jit(solution)/shard_map/ppermute | solution.py:39
  50.0 15.6 %collective-permute-start.12 = (bf16[768,256]{1,0:T(8,128)(2,1)S(1)}, bf16[768,256]{1,0:T(8,128)(2,1)S(1)}, u32[]{:S(2)}, u32[]{:S(2)}) collective-permute-start(bf16[768,256]{1,0:T(8,128)(2,1)S(1)} %constant_dynamic-slice_fusion.2), channel_id=1, source_target_pairs={{0,2},{1,3},{2,0},{3,1},{4,6},{5,7},{6,4},{7,5},{8,10},{9,11},{10,... | collective-permute-start | bytes 1179656 | tf_op jit(solution)/shard_map/ppermute | solution.py:39
  87.5 11.2 %collective-permute-start.17 = (bf16[256,768]{1,0:T(8,128)(2,1)S(1)}, bf16[256,768]{1,0:T(8,128)(2,1)S(1)}, u32[]{:S(2)}, u32[]{:S(2)}) collective-permute-start(bf16[256,768]{1,0:T(8,128)(2,1)S(1)} %get-tuple-element.249), channel_id=1, source_target_pairs={{0,2},{1,3},{2,0},{3,1},{4,6},{5,7},{6,4},{7,5},{8,10},{9,11},{10,... | collective-permute-start | bytes 1179656 | tf_op jit(solution)/shard_map/ppermute | solution.py:39
  89.1 10.9 %collective-permute-start.18 = (bf16[256,768]{1,0:T(8,128)(2,1)S(1)}, bf16[256,768]{1,0:T(8,128)(2,1)S(1)}, u32[]{:S(2)}, u32[]{:S(2)}) collective-permute-start(bf16[256,768]{1,0:T(8,128)(2,1)S(1)} %get-tuple-element.250), channel_id=1, source_target_pairs={{0,4},{4,0},{8,12},{12,8},{16,20},{20,16},{24,28},{28,24},{1,5},{5... | collective-permute-start | bytes 1179656 | tf_op jit(solution)/shard_map/ppermute | solution.py:39
  89.5 10.6 %collective-permute-start.19 = (bf16[256,768]{1,0:T(8,128)(2,1)S(1)}, bf16[256,768]{1,0:T(8,128)(2,1)S(1)}, u32[]{:S(2)}, u32[]{:S(2)}) collective-permute-start(bf16[256,768]{1,0:T(8,128)(2,1)S(1)} %get-tuple-element.251), channel_id=1, source_target_pairs={{0,8},{4,12},{8,0},{12,4},{16,24},{20,28},{24,16},{28,20},{1,9},{5... | collective-permute-start | bytes 1179656 | tf_op jit(solution)/shard_map/ppermute | solution.py:39
  103.4 10.9 %collective-permute-start.22 = (bf16[256,768]{1,0:T(8,128)(2,1)S(1)}, bf16[256,768]{1,0:T(8,128)(2,1)S(1)}, u32[]{:S(2)}, u32[]{:S(2)}) collective-permute-start(bf16[256,768]{1,0:T(8,128)(2,1)S(1)} %get-tuple-element.273), channel_id=1, source_target_pairs={{0,4},{4,0},{8,12},{12,8},{16,20},{20,16},{24,28},{28,24},{1,5},{5... | collective-permute-start | bytes 1179656 | tf_op jit(solution)/shard_map/ppermute | solution.py:39
  105.1 10.6 %collective-permute-start.23 = (bf16[256,768]{1,0:T(8,128)(2,1)S(1)}, bf16[256,768]{1,0:T(8,128)(2,1)S(1)}, u32[]{:S(2)}, u32[]{:S(2)}) collective-permute-start(bf16[256,768]{1,0:T(8,128)(2,1)S(1)} %get-tuple-element.274), channel_id=1, source_target_pairs={{0,8},{4,12},{8,0},{12,4},{16,24},{20,28},{24,16},{28,20},{1,9},{5... | collective-permute-start | bytes 1179656 | tf_op jit(solution)/shard_map/ppermute | solution.py:39
  109.9 10.3 %collective-permute-start.24 = (bf16[768,192]{1,0:T(8,128)(2,1)S(1)}, bf16[768,192]{1,0:T(8,128)(2,1)S(1)}, u32[]{:S(2)}, u32[]{:S(2)}) collective-permute-start(bf16[768,192]{1,0:T(8,128)(2,1)S(1)} %get-tuple-element.295), channel_id=1, source_target_pairs={{0,2},{1,3},{2,0},{3,1},{4,6},{5,7},{6,4},{7,5},{8,10},{9,11},{10,... | collective-permute-start | bytes 884744 | tf_op jit(solution)/shard_map/ppermute | solution.py:39
  120.2 16.0 %collective-permute-start.26 = (bf16[448,768]{1,0:T(8,128)(2,1)}, bf16[448,768]{1,0:T(8,128)(2,1)S(1)}, u32[]{:S(2)}, u32[]{:S(2)}) collective-permute-start(bf16[448,768]{1,0:T(8,128)(2,1)} %get-tuple-element.303), channel_id=1, source_target_pairs={{0,4},{4,0},{8,12},{12,8},{16,20},{20,16},{24,28},{28,24},{1,5},{5... | collective-permute-start | bytes 2064392 | tf_op jit(solution)/shard_map/ppermute | solution.py:39
  121.9 15.7 %collective-permute-start.27 = (bf16[448,768]{1,0:T(8,128)(2,1)}, bf16[448,768]{1,0:T(8,128)(2,1)S(1)}, u32[]{:S(2)}, u32[]{:S(2)}) collective-permute-start(bf16[448,768]{1,0:T(8,128)(2,1)} %get-tuple-element.304), channel_id=1, source_target_pairs={{0,8},{4,12},{8,0},{12,4},{16,24},{20,28},{24,16},{28,20},{1,9},{5... | collective-permute-start | bytes 2064392 | tf_op jit(solution)/shard_map/ppermute | solution.py:39
  122.3 13.3 %collective-permute-start.25 = (bf16[384,768]{1,0:T(8,128)(2,1)}, bf16[384,768]{1,0:T(8,128)(2,1)S(1)}, u32[]{:S(2)}, u32[]{:S(2)}) collective-permute-start(bf16[384,768]{1,0:T(8,128)(2,1)} %get-tuple-element.302), channel_id=1, source_target_pairs={{0,2},{1,3},{2,0},{3,1},{4,6},{5,7},{6,4},{7,5},{8,10},{9,11},{10,... | collective-permute-start | bytes 1769480 | tf_op jit(solution)/shard_map/ppermute | solution.py:39
  140.7 12.8 %collective-permute-start.30 = (bf16[288,768]{1,0:T(8,128)(2,1)}, bf16[288,768]{1,0:T(8,128)(2,1)S(1)}, u32[]{:S(2)}, u32[]{:S(2)}) collective-permute-start(bf16[288,768]{1,0:T(8,128)(2,1)} %get-tuple-element.328), channel_id=1, source_target_pairs={{0,4},{4,0},{8,12},{12,8},{16,20},{20,16},{24,28},{28,24},{1,5},{5... | collective-permute-start | bytes 1327112 | tf_op jit(solution)/shard_map/ppermute | solution.py:39
  141.8 13.7 %collective-permute-start.31 = (bf16[320,768]{1,0:T(8,128)(2,1)}, bf16[320,768]{1,0:T(8,128)(2,1)S(1)}, u32[]{:S(2)}, u32[]{:S(2)}) collective-permute-start(bf16[320,768]{1,0:T(8,128)(2,1)} %get-tuple-element.329), channel_id=1, source_target_pairs={{0,8},{4,12},{8,0},{12,4},{16,24},{20,28},{24,16},{28,20},{1,9},{5... | collective-permute-start | bytes 1474568 | tf_op jit(solution)/shard_map/ppermute | solution.py:39
  142.3 11.2 %collective-permute-start.28 = (bf16[96,768]{1,0:T(8,128)(2,1)S(1)}, bf16[96,768]{1,0:T(8,128)(2,1)S(1)}, u32[]{:S(2)}, u32[]{:S(2)}) collective-permute-start(bf16[96,768]{1,0:T(8,128)(2,1)S(1)} %constant_dynamic-slice_fusion), channel_id=1, source_target_pairs={{0,16},{4,20},{8,24},{12,28},{16,0},{20,4},{24,8},{28,12},{1,17},{... | collective-permute-start | bytes 442376 | tf_op jit(solution)/shard_map/ppermute | solution.py:39
  155.5 14.3 %collective-permute-start.33 = (bf16[784,768]{1,0:T(8,128)(2,1)}, bf16[784,768]{1,0:T(8,128)(2,1)S(1)}, u32[]{:S(2)}, u32[]{:S(2)}) collective-permute-start(bf16[784,768]{1,0:T(8,128)(2,1)} %get-tuple-element.340), channel_id=1, source_target_pairs={{0,1},{1,0},{2,3},{3,2},{4,5},{5,4},{6,7},{7,6},{8,9},{9,8},{10,11... | collective-permute-start | bytes 3612680 | tf_op jit(solution)/shard_map/ppermute | solution.py:39
  155.6 10.5 %collective-permute-start.32 = (bf16[96,768]{1,0:T(8,128)(2,1)S(1)}, bf16[96,768]{1,0:T(8,128)(2,1)}, u32[]{:S(2)}, u32[]{:S(2)}) collective-permute-start(bf16[96,768]{1,0:T(8,128)(2,1)S(1)} %add_convert_fusion.2), channel_id=1, source_target_pairs={{0,16},{4,20},{8,24},{12,28},{16,0},{20,4},{24,8},{28,12},{1,17},{... | collective-permute-start | bytes 442376 | tf_op jit(solution)/shard_map/ppermute | solution.py:39
  170.4 11.1 %collective-permute-start.41 = (bf16[64,768]{1,0:T(8,128)(2,1)}, bf16[64,768]{1,0:T(8,128)(2,1)S(1)}, u32[]{:S(2)}, u32[]{:S(2)}) collective-permute-start(bf16[64,768]{1,0:T(8,128)(2,1)} %slice.92), channel_id=1, source_target_pairs={{0,4},{4,0},{8,12},{12,8},{16,20},{20,16},{24,28},{28,24},{1,5},{5... | collective-permute-start | bytes 294920 | tf_op jit(solution)/shard_map/ppermute | solution.py:39
  172.0 17.4 %collective-permute-start.37 = (bf16[224,768]{1,0:T(8,128)(2,1)S(1)}, bf16[224,768]{1,0:T(8,128)(2,1)S(1)}, u32[]{:S(2)}, u32[]{:S(2)}) collective-permute-start(bf16[224,768]{1,0:T(8,128)(2,1)S(1)} %fusion), channel_id=1, source_target_pairs={{0,16},{4,20},{8,24},{12,28},{16,0},{20,4},{24,8},{28,12},{1,17},{... | collective-permute-start | bytes 1032200 | tf_op jit(solution)/shard_map/ppermute | solution.py:39
  174.5 18.0 %collective-permute-start.38 = (bf16[392,768]{1,0:T(8,128)(2,1)S(1)}, bf16[392,768]{1,0:T(8,128)(2,1)S(1)}, u32[]{:S(2)}, u32[]{:S(2)}) collective-permute-start(bf16[392,768]{1,0:T(8,128)(2,1)S(1)} %get-tuple-element.353), channel_id=1, source_target_pairs={{0,2},{1,3},{2,0},{3,1},{4,6},{5,7},{6,4},{7,5},{8,10},{9,11},{10,... | collective-permute-start | bytes 1806344 | tf_op jit(solution)/shard_map/ppermute | solution.py:39
  178.6 13.8 %collective-permute-start.40 = (bf16[256,768]{1,0:T(8,128)(2,1)S(1)}, bf16[256,768]{1,0:T(8,128)(2,1)S(1)}, u32[]{:S(2)}, u32[]{:S(2)}) collective-permute-start(bf16[256,768]{1,0:T(8,128)(2,1)S(1)} %pad_maximum_fusion.5), channel_id=1, source_target_pairs={{0,4},{4,0},{8,12},{12,8},{16,20},{20,16},{24,28},{28,24},{1,5},{5... | collective-permute-start | bytes 1179656 | tf_op jit(solution)/shard_map/ppermute | solution.py:39
  181.5 11.0 %collective-permute-start.42 = (bf16[128,768]{1,0:T(8,128)(2,1)S(1)}, bf16[128,768]{1,0:T(8,128)(2,1)S(1)}, u32[]{:S(2)}, u32[]{:S(2)}) collective-permute-start(bf16[128,768]{1,0:T(8,128)(2,1)S(1)} %pad_maximum_fusion.8), channel_id=1, source_target_pairs={{0,8},{4,12},{8,0},{12,4},{16,24},{20,28},{24,16},{28,20},{1,9},{5... | collective-permute-start | bytes 589832 | tf_op jit(solution)/shard_map/ppermute | solution.py:39
  192.5 19.3 %collective-permute-start.44 = (bf16[224,768]{1,0:T(8,128)(2,1)}, bf16[224,768]{1,0:T(8,128)(2,1)}, u32[]{:S(2)}, u32[]{:S(2)}) collective-permute-start(bf16[224,768]{1,0:T(8,128)(2,1)} %add_convert_fusion.1), channel_id=1, source_target_pairs={{0,16},{4,20},{8,24},{12,28},{16,0},{20,4},{24,8},{28,12},{1,17},{... | collective-permute-start | bytes 1032200 | tf_op jit(solution)/shard_map/ppermute | solution.py:39
  200.9 10.8 %collective-permute-start.47 = (f32[10,768]{1,0:T(8,128)S(1)}, f32[10,768]{1,0:T(8,128)S(1)}, u32[]{:S(2)}, u32[]{:S(2)}) collective-permute-start(f32[10,768]{1,0:T(8,128)S(1)} %add.87), channel_id=1, source_target_pairs={{0,16},{4,20},{8,24},{12,28},{16,0},{20,4},{24,8},{28,12},{1,17},{... | collective-permute-start | bytes 92168 | tf_op jit(solution)/shard_map/ppermute | solution.py:39
  203.9 10.9 %collective-permute-start.43 = (bf16[768,256]{1,0:T(8,128)(2,1)}, bf16[768,256]{1,0:T(8,128)(2,1)S(1)}, u32[]{:S(2)}, u32[]{:S(2)}) collective-permute-start(bf16[768,256]{1,0:T(8,128)(2,1)} %copy-done.9), channel_id=1, source_target_pairs={{0,2},{1,3},{2,0},{3,1},{4,6},{5,7},{6,4},{7,5},{8,10},{9,11},{10,... | collective-permute-start | bytes 1179656 | tf_op jit(solution)/shard_map/ppermute | solution.py:39
  222.4 15.6 %collective-permute-start.51 = (bf16[448,768]{1,0:T(8,128)(2,1)S(1)}, bf16[448,768]{1,0:T(8,128)(2,1)S(1)}, u32[]{:S(2)}, u32[]{:S(2)}) collective-permute-start(bf16[448,768]{1,0:T(8,128)(2,1)S(1)} %pad_maximum_fusion.2), channel_id=1, source_target_pairs={{0,8},{4,12},{8,0},{12,4},{16,24},{20,28},{24,16},{28,20},{1,9},{5... | collective-permute-start | bytes 2064392 | tf_op jit(solution)/shard_map/ppermute | solution.py:39
  222.8 15.4 %collective-permute-start.50 = (bf16[448,768]{1,0:T(8,128)(2,1)S(1)}, bf16[448,768]{1,0:T(8,128)(2,1)S(1)}, u32[]{:S(2)}, u32[]{:S(2)}) collective-permute-start(bf16[448,768]{1,0:T(8,128)(2,1)S(1)} %pad_maximum_fusion.1), channel_id=1, source_target_pairs={{0,4},{4,0},{8,12},{12,8},{16,20},{20,16},{24,28},{28,24},{1,5},{5... | collective-permute-start | bytes 2064392 | tf_op jit(solution)/shard_map/ppermute | solution.py:39
  (61 other events, 330.4 us)
